TPU v7x, 256 devices: a whole 4x4x8 slice. The times are simulated.
256 devices in a mesh: occi: 8 (over x_lo, y), occj: 32 (over z, x_hi, core).
Axes of the slice: x: 4 (x_hi: 2, x_lo: 2; x = x_hi * 2 + x_lo), y: 4, z: 8, core: 2. Of those that a mesh axis runs over, the one named last changes fastest.
Arguments:
- amplitudes: bfloat16 [64, 64, 256, 256], P('occi', 'occj'), may hold values from -6 to 6
- exchange: bfloat16 [64, 64, 256, 256], P('occi', 'occj'), may hold values from -6 to 6
- fock_virt: bfloat16 [256, 256], replicated, may hold values from -0.375 to 0.375
- intersection: bfloat16 [256, 256], replicated, may hold values from -0.1875 to 0.1875
- transform: bfloat16 [256, 256], replicated, may hold values from -0.375 to 0.375
- virt_energy: float32 [256], replicated, may hold values from 0.5 to 4
- occ_energy: float32 [64], replicated, may hold values from -1.5 to -0.3
- partners: int32 [64, 2], replicated, may hold values from 0 to 63, as said below
- coupling: float32 [64, 2], replicated, may hold values from -0.6 to 0.6
- domain: int32 [64, 8], replicated, may hold values 0 or 1
Outputs:
- residual: float32 [64, 64, 256, 256], P('occi', 'occj')
- new_amplitudes: bfloat16 [64, 64, 256, 256], P('occi', 'occj')
Inputs may be any that keep to these rules, and one draw needn't show every extreme that they name: The 2 partners of orbital i are distinct, differ from i, and lie within 2 of i; the first lies exactly 2 away.
All inputs are finite; a program needn't handle non-finite values.
Results may differ from a plain program's by a relative error of at most 0.0085.
Values may be sent and summed in bfloat16 or wider, within the bound.
No kernel may reach another device: no remote copies, remote signals or barrier semaphores. Data moves between devices by JAX's collectives and lax.ppermute only.
A program may use at most 128 MiB of HBM per device.

v0:
```python
import jax
import jax.numpy as jnp
from jax import lax
from jax.sharding import PartitionSpec as P

REACH = 2


def extended_2(block, sides, width):
    for axis, dim in sides:
        count = lax.axis_size(axis)
        forward = [(i, i + 1) for i in range(count - 1)]
        backward = [(target, source) for source, target in forward]
        low = lax.ppermute(
            lax.slice_in_dim(block, block.shape[dim] - width, None, axis=dim), axis, forward
        )
        high = lax.ppermute(lax.slice_in_dim(block, 0, width, axis=dim), axis, backward)
        block = jnp.concatenate([low, block, high], axis=dim)
    return block


def flip_blocks(block):
    rows_i = block.shape[0]
    cols_j = block.shape[1]
    width = block.shape[2]
    count_i = lax.axis_size("occi")
    count_j = lax.axis_size("occj")
    group = count_j // count_i
    slab = width // count_j
    moved = lax.all_to_all(
        block.reshape(1, rows_i, cols_j, width, width),
        "occj",
        split_axis=3,
        concat_axis=0,
        tiled=True,
    )
    moved = lax.all_to_all(
        moved.reshape(count_j, 1, rows_i, cols_j, slab, width),
        "occi",
        split_axis=0,
        concat_axis=1,
        tiled=True,
    )
    moved = moved.reshape(group, count_j, cols_j, cols_j, 1, slab, width)
    moved = lax.all_to_all(moved, "occj", split_axis=1, concat_axis=4, tiled=True)
    moved = moved.reshape(group, cols_j, cols_j, width, width)
    return jnp.transpose(moved, (0, 2, 1, 4, 3)).reshape(rows_i, cols_j, width, width)


def mix_rows(extended, lists, weights, start):
    local = lists - start + REACH
    total = jnp.zeros((lists.shape[0],) + extended.shape[1:], jnp.float32)
    for slot in range(lists.shape[1]):
        picked = jnp.take(extended, local[:, slot], axis=0).astype(jnp.float32)
        total = total + weights[:, slot, None, None, None] * picked
    return total


def mix_columns(extended, lists, weights, start):
    local = lists - start + REACH
    shape = (extended.shape[0], lists.shape[0]) + extended.shape[2:]
    total = jnp.zeros(shape, jnp.float32)
    for slot in range(lists.shape[1]):
        picked = jnp.take(extended, local[:, slot], axis=1).astype(jnp.float32)
        total = total + weights[None, :, slot, None, None] * picked
    return total


def per_device(
    amplitudes,
    exchange,
    fock_virt,
    intersection,
    transform,
    virt_energy,
    occ_energy,
    partners,
    coupling,
    domain,
):
    rows_i = amplitudes.shape[0]
    cols_j = amplitudes.shape[1]
    width = amplitudes.shape[2]
    tiles = domain.shape[1]
    start_i = lax.axis_index("occi") * rows_i
    start_j = lax.axis_index("occj") * cols_j
    intersection_full = (
        jnp.eye(width, dtype=jnp.float32) + intersection.astype(jnp.float32)
    ).astype(jnp.bfloat16)
    a1 = jnp.einsum(
        "ab,rsbc->rsac", fock_virt, amplitudes, preferred_element_type=jnp.float32
    ).astype(jnp.bfloat16)
    first = jnp.einsum("rsab,bc->rsac", a1, intersection_full, preferred_element_type=jnp.float32)
    a2 = jnp.einsum(
        "ab,rsbc->rsac", intersection_full, amplitudes, preferred_element_type=jnp.float32
    ).astype(jnp.bfloat16)
    second = jnp.einsum("rsab,bc->rsac", a2, fock_virt, preferred_element_type=jnp.float32)
    mirror = flip_blocks(amplitudes)
    sym = (0.5 * (amplitudes.astype(jnp.float32) + mirror.astype(jnp.float32))).astype(jnp.bfloat16)
    lists_i = lax.dynamic_slice_in_dim(partners, start_i, rows_i, 0)
    weights_i = lax.dynamic_slice_in_dim(coupling, start_i, rows_i, 0)
    extended_i = extended_2(sym, (("occi", 0),), REACH)
    c_row = mix_rows(extended_i, lists_i, weights_i, start_i).astype(jnp.bfloat16)
    lists_j = lax.dynamic_slice_in_dim(partners, start_j, cols_j, 0)
    weights_j = lax.dynamic_slice_in_dim(coupling, start_j, cols_j, 0)
    extended_j = extended_2(sym, (("occj", 1),), REACH)
    c_col = mix_columns(extended_j, lists_j, weights_j, start_j).astype(jnp.bfloat16)
    coup = c_row.astype(jnp.float32) + c_col.astype(jnp.float32)
    masks = jnp.repeat(domain.astype(jnp.float32), width // tiles, axis=1)
    mask_i = lax.dynamic_slice_in_dim(masks, start_i, rows_i, 0)
    mask_j = lax.dynamic_slice_in_dim(masks, start_j, cols_j, 0)
    mpair = jnp.maximum(mask_i[:, None, :], mask_j[None, :, :])
    two = mpair[:, :, :, None] * mpair[:, :, None, :]
    cmask = (coup * two).astype(jnp.bfloat16)
    b1 = jnp.einsum(
        "ab,rsbc->rsac", intersection_full, cmask, preferred_element_type=jnp.float32
    ).astype(jnp.bfloat16)
    third = jnp.einsum("rsab,bc->rsac", b1, intersection_full, preferred_element_type=jnp.float32)
    residual = two * (exchange.astype(jnp.float32) + first + second - third)
    resid_b = residual.astype(jnp.bfloat16)
    q1 = jnp.einsum("ba,rsbc->rsac", transform, resid_b, preferred_element_type=jnp.float32).astype(
        jnp.bfloat16
    )
    q2 = jnp.einsum("rsab,bc->rsac", q1, transform, preferred_element_type=jnp.float32)
    occ_i = lax.dynamic_slice_in_dim(occ_energy, start_i, rows_i, 0)
    occ_j = lax.dynamic_slice_in_dim(occ_energy, start_j, cols_j, 0)
    pair_shift = occ_i[:, None] + occ_j[None, :]
    denom = (
        virt_energy[None, None, :, None]
        + virt_energy[None, None, None, :]
        - pair_shift[:, :, None, None]
    )
    zeta = (q2 / denom).astype(jnp.bfloat16)
    u1 = jnp.einsum("ab,rsbc->rsac", transform, zeta, preferred_element_type=jnp.float32).astype(
        jnp.bfloat16
    )
    u2 = jnp.einsum("rsab,cb->rsac", u1, transform, preferred_element_type=jnp.float32)
    fresh = (amplitudes.astype(jnp.float32) - u2).astype(jnp.bfloat16)
    return (residual, fresh)


def solution(mesh):
    return jax.shard_map(
        per_device,
        mesh=mesh,
        in_specs=(
            P("occi", "occj", None, None),
            P("occi", "occj", None, None),
            P(),
            P(),
            P(),
            P(),
            P(),
            P(),
            P(),
            P(),
        ),
        out_specs=(P("occi", "occj", None, None), P("occi", "occj", None, None)),
        check_vma=False,
    )
```

profile of v0, /device:TPU:3, one launch (start us, length us, event | category | flops | bytes accessed | tf_op | source)
XLA Modules:
  0.0 281.1 jit_solution(13498421750724093916)
XLA Ops:
  0.6 0.0 copy-start
  0.6 3.8 %copy.94 = bf16[8,2,256,256]{3,1,0,2:T(2,128)(2,1)S(1)} copy(bf16[8,2,256,256]{3,2,1,0:T(8,128)(2,1)} %param.14) | data formatting | bytes 4194304 | tf_op args[0]
  4.4 61.2 %all_to_all.42 = bf16[1,8,2,256,256]{4,2,1,0,3:T(2,128)(2,1)S(1)} all-to-all(bf16[1,8,2,256,256]{4,2,1,0,3:T(2,128)(2,1)S(1)} %bitcast.98), channel_id=1, replica_groups=mesh['occi'=8,'occj'=32] {'occj'}, dimensions={3} | all-to-all | bytes 4194304 | tf_op jit(solution)/shard_map/all_to_all | solution.py:30
  65.6 0.7 copy.93
  66.3 0.2 copy.56
  66.6 29.6 %all_to_all.43 = bf16[32,1,8,2,8,256]{5,4,3,2,1,0:T(8,128)(2,1)S(1)} all-to-all(bf16[32,1,8,2,8,256]{5,4,3,2,1,0:T(8,128)(2,1)S(1)} %copy.56), channel_id=1, replica_groups=mesh['occi'=8,'occj'=32] {'occi'}, dimensions={0} | all-to-all | bytes 4194304 | tf_op jit(solution)/shard_map/all_to_all | solution.py:37
  96.3 0.2 copy.57
  96.5 1.5 copy.58
  98.0 0.0 copy-start.10
  98.0 0.0 copy-start.7
  98.0 0.0 copy-start.9
  98.0 7.9 %all-to-all-start.2 = ((bf16[4,32,2,2,1,8,256]{6,5,3,2,0,4,1:T(8,128)(2,1)}), bf16[4,32,2,2,1,8,256]{6,5,3,2,0,4,1:T(8,128)(2,1)S(1)}, u32[]{:S(2)}, u32[]{:S(2)}) async-start(bf16[4,32,2,2,1,8,256]{6,5,3,2,0,4,1:T(8,128)(2,1)} %copy.58), calls=%async_computation.2 | async-start | bytes 4194304 | tf_op jit(solution)/shard_map/all_to_all | solution.py:45
  105.9 0.0 copy-done.8
  106.0 0.1 constant_dynamic-slice_fusion.5
  106.1 0.1 copy.50
  106.2 0.0 copy-done.10
  106.2 0.1 dynamic_slice.30
  106.2 0.1 dynamic_slice.31
  106.3 0.1 constant_dynamic-slice_fusion.4
  106.4 0.1 copy.51
  106.5 0.0 copy-done.7
  106.5 0.1 fusion.69
  106.6 0.1 fusion.71
  106.6 0.0 copy-done.9
  106.7 0.1 constant_dynamic-slice_fusion.3
  106.7 0.1 constant_dynamic-slice_fusion.1
  106.8 0.1 broadcast_add_fusion.1
  106.9 49.1 %all-to-all-done.2 = bf16[4,32,2,2,1,8,256]{6,5,3,2,0,4,1:T(8,128)(2,1)S(1)} async-done(((bf16[4,32,2,2,1,8,256]{6,5,3,2,0,4,1:T(8,128)(2,1)}), bf16[4,32,2,2,1,8,256]{6,5,3,2,0,4,1:T(8,128)(2,1)S(1)}, u32[]{:S(2)}, u32[]{:S(2)}) %all-to-all-start.2) | async-done | bytes 2097184 | tf_op jit(solution)/shard_map/all_to_all | solution.py:45
  156.0 2.4 convert_bitcast_fusion
  158.4 0.0 copy-start.2
  158.4 5.4 %copy.60 = f32[4,2,2,256,256]{4,3,2,1,0:T(8,128)} copy(f32[4,2,2,256,256]{3,4,1,2,0:T(8,128)} %convert_bitcast_fusion) | data formatting | bytes 8388608 | tf_op jit(solution)/shard_map/convert_element_type | solution.py:99
  163.8 0.0 copy-done.2
  163.8 0.0 copy-start.6
  163.8 0.0 copy-start.3
  163.8 4.2 %fusion.1 = bf16[8,2,256,256]{3,2,1,0:T(8,128)(2,1)} fusion(bf16[8,2,256,256]{3,2,1,0:T(8,128)(2,1)S(1)} %copy-done.2, f32[4,2,2,256,256]{4,3,2,1,0:T(8,128)} %copy.60), kind=kLoop, calls=%fused_computation.10 | loop fusion | flops 4194304 | bytes 8388608 | tf_op jit(solution)/shard_map/convert_element_type | solution.py:99
  168.0 5.1 %collective-permute-start.2 = (bf16[8,2,256,256]{3,2,1,0:T(8,128)(2,1)}, bf16[8,2,256,256]{3,2,1,0:T(8,128)(2,1)}, u32[]{:S(2)}, u32[]{:S(2)}) collective-permute-start(bf16[8,2,256,256]{3,2,1,0:T(8,128)(2,1)} %fusion.1), channel_id=1, source_target_pairs={{0,1},{1,2},{2,3},{3,4},{4,5},{5,6},{6,7},{7,8},{8,9},{9,10},{10,1... | collective-permute-start | bytes 6291464 | tf_op jit(solution)/shard_map/ppermute | solution.py:14
  173.1 1.9 collective-permute-start.3
  175.1 0.0 copy-done.6
  175.1 0.8 broadcast_add_fusion
  175.9 0.0 copy-done
  175.9 0.0 copy-done.3
  175.9 4.1 %fusion.10 = f32[8,2,256,256]{3,2,1,0:T(8,128)} fusion(bf16[8,2,256,256]{3,2,1,0:T(8,128)(2,1)S(1)} %copy-done.2, bf16[256,256]{1,0:T(8,128)(2,1)S(1)} %copy-done, bf16[256,256]{1,0:T(8,128)(2,1)S(1)} %copy-done.3), kind=kOutput, calls=%fused_computation.24 | convolution fusion | flops 1075118080 | bytes 6553600 | tf_op jit(solution)/shard_map/rsab,bc->rsac/dot_general | solution.py:93
  180.0 2.3 fusion.74
  182.2 2.2 collective-permute-start
  184.4 5.4 %collective-permute-start.1 = (bf16[2,2,256,256]{3,2,1,0:T(8,128)(2,1)}, bf16[2,2,256,256]{3,2,1,0:T(8,128)(2,1)S(1)}, u32[]{:S(2)}, u32[]{:S(2)}) collective-permute-start(bf16[2,2,256,256]{3,2,1,0:T(8,128)(2,1)} %get-tuple-element.13), channel_id=1, source_target_pairs={{32,0},{64,32},{96,64},{128,96},{160,128},{192,160},{224,192},{33,... | collective-permute-start | bytes 1572872 | tf_op jit(solution)/shard_map/ppermute | solution.py:17
  189.8 3.3 %fusion.8 = f32[8,2,256,256]{3,2,1,0:T(8,128)} fusion(bf16[8,2,256,256]{3,2,1,0:T(8,128)(2,1)S(1)} %copy-done.2, bf16[256,256]{1,0:T(8,128)(2,1)S(1)} %copy-done, bf16[256,256]{1,0:T(8,128)(2,1)S(1)} %copy-done.3), kind=kOutput, calls=%fused_computation.22 | convolution fusion | flops 1075118080 | bytes 6553600 | tf_op jit(solution)/shard_map/rsab,bc->rsac/dot_general | solution.py:97
  193.1 39.3 %collective-permute-done = bf16[2,2,256,256]{3,2,1,0:T(8,128)(2,1)S(1)} collective-permute-done((bf16[2,2,256,256]{3,2,1,0:T(8,128)(2,1)}, bf16[2,2,256,256]{3,2,1,0:T(8,128)(2,1)S(1)}, u32[]{:S(2)}, u32[]{:S(2)}) %collective-permute-start) | collective-permute-done | bytes 524320 | tf_op jit(solution)/shard_map/ppermute | solution.py:14
  232.4 0.0 collective-permute-done.1
  232.4 3.0 %pad_maximum_fusion.1 = bf16[12,2,256,256]{3,2,1,0:T(8,128)(2,1)} fusion(bf16[2,2,256,256]{3,2,1,0:T(8,128)(2,1)S(1)} %collective-permute-done.1, bf16[8,2,256,256]{3,2,1,0:T(8,128)(2,1)} %fusion.1, bf16[2,2,256,256]{3,2,1,0:T(8,128)(2,1)S(1)} %collective-permute-done), kind=kLoop, calls=%fused_computation.17 | loop fusion | flops 3145728 | bytes 6291456 | tf_op jit(solution)/shard_map/concatenate | solution.py:18
  235.5 3.9 %gather_fusion = bf16[8,2,256,256]{3,2,1,0:T(8,128)(2,1)} fusion(bf16[12,2,256,256]{3,2,1,0:T(8,128)(2,1)} %pad_maximum_fusion.1, s32[1024]{0:T(1024)S(1)} %get-tuple-element.25), kind=kCustom, calls=%fused_computation.clone | custom fusion | bytes 4194336 | tf_op jit(solution)/shard_map/jit(_take)/gather | solution.py:54
  239.4 3.9 %gather_fusion.1 = bf16[8,2,256,256]{3,2,1,0:T(8,128)(2,1)} fusion(bf16[12,2,256,256]{3,2,1,0:T(8,128)(2,1)} %pad_maximum_fusion.1, s32[1024]{0:T(1024)S(1)} %get-tuple-element.24), kind=kCustom, calls=%fused_computation.2.clone | custom fusion | bytes 4194336 | tf_op jit(solution)/shard_map/jit(_take)/gather | solution.py:54
  243.3 0.0 collective-permute-done.2
  243.3 0.0 collective-permute-done.3
  243.3 6.4 %pad_maximum_fusion = bf16[8,6,256,256]{3,2,1,0:T(8,128)(2,1)} fusion(bf16[8,2,256,256]{3,2,1,0:T(8,128)(2,1)} %collective-permute-done.3, bf16[8,2,256,256]{3,2,1,0:T(8,128)(2,1)} %fusion.1, bf16[8,2,256,256]{3,2,1,0:T(8,128)(2,1)} %collective-permute-done.2), kind=kLoop, calls=%fused_computation.4 | loop fusion | flops 6291456 | bytes 12582912 | tf_op jit(solution)/shard_map/concatenate | solution.py:18
  249.7 4.8 %gather_fusion.2 = bf16[2,8,256,256]{3,2,1,0:T(8,128)(2,1)} fusion(bf16[8,6,256,256]{3,2,1,0:T(8,128)(2,1)} %pad_maximum_fusion, s32[1024]{0:T(1024)S(1)} %get-tuple-element.23), kind=kCustom, calls=%fused_computation.1.clone | custom fusion | bytes 4194312 | tf_op jit(solution)/shard_map/jit(_take)/gather | solution.py:64
  254.5 4.8 %gather_fusion.3 = bf16[2,8,256,256]{3,2,1,0:T(8,128)(2,1)} fusion(bf16[8,6,256,256]{3,2,1,0:T(8,128)(2,1)} %pad_maximum_fusion, s32[1024]{0:T(1024)S(1)} %get-tuple-element.22), kind=kCustom, calls=%fused_computation.3.clone | custom fusion | bytes 4194312 | tf_op jit(solution)/shard_map/jit(_take)/gather | solution.py:64
  259.3 0.0 copy-start.4
  259.3 10.0 %multiply_multiply_fusion = f32[8,2,256,256]{3,2,1,0:T(8,128)} fusion(f32[8,2,256,256]{3,2,1,0:T(8,128)} %fusion.8, f32[8,2,256,256]{3,2,1,0:T(8,128)} %fusion.10, bf16[8,2,256,256]{3,2,1,0:T(8,128)(2,1)} %param.15, bf16[2,8,256,256]{3,2,1,0:T(8,128)(2,1)} %gather_fusion.3, bf16[2,8,256,256]{3,2,1,0:T(8,128)(2,1)} %gather_fusion.2, ...), kind=kOutput, calls=%fused_computation.5 | convolution fusion | flops 1104805888 | bytes 23216228 | tf_op jit(solution)/shard_map/rsab,bc->rsac/dot_general | solution.py:118
  269.3 0.0 copy-done.4
  269.3 6.3 %fusion.5 = f32[8,2,256,256]{3,2,1,0:T(8,128)} fusion(f32[8,2,256,256]{3,2,1,0:T(8,128)} %multiply_multiply_fusion, bf16[256,256]{1,0:T(8,128)(2,1)S(1)} %copy-done.4), kind=kOutput, calls=%fused_computation.19 | convolution fusion | flops 1075838976 | bytes 8519680 | tf_op jit(solution)/shard_map/rsab,bc->rsac/dot_general | solution.py:124
  275.6 0.0 copy-done.5
  275.6 0.0 copy-start.1
  275.6 5.5 %fusion.2 = bf16[8,2,256,256]{3,2,1,0:T(8,128)(2,1)} fusion(bf16[8,2,256,256]{3,2,1,0:T(8,128)(2,1)S(1)} %copy-done.2, f32[8,2,256,256]{3,2,1,0:T(8,128)} %fusion.5, f32[8,2]{1,0:T(8,128)S(1)} %broadcast_add_fusion.1, f32[256,256]{1,0:T(8,128)S(1)} %copy-done.5, bf16[256,256]{1,0:T(8,128)(2,1)S(1)} %copy-done.4), kind=kOutput, calls=%fused_computation.11 | convolution fusion | flops 1081081856 | bytes 8781888 | tf_op jit(solution)/shard_map/rsab,cb->rsac/dot_general | solution.py:137
  281.1 0.0 copy-done.1
  (11 shorter events, 0.1 us)
Async XLA Ops:
  0.6 175.3 %copy-start = (bf16[256,256]{1,0:T(8,128)(2,1)S(1)}, bf16[256,256]{1,0:T(8,128)(2,1)}, u32[]{:S(2)}) copy-start(bf16[256,256]{1,0:T(8,128)(2,1)} %param.16) | copy-start | bytes 393220
  98.0 8.0 %copy-start.8 = (s32[64,8]{0,1:T(8,128)S(1)}, s32[64,8]{0,1:T(8,128)}, u32[]{:S(2)}) copy-start(s32[64,8]{0,1:T(8,128)} %param.23) | copy-start | bytes 6148
  98.0 8.2 %copy-start.10 = (f32[64]{0:T(128)S(1)}, f32[64]{0:T(128)}, u32[]{:S(2)}) copy-start(f32[64]{0:T(128)} %param.20) | copy-start | bytes 772
  98.0 8.5 %copy-start.7 = (s32[64,2]{0,1:T(2,128)S(1)}, s32[64,2]{0,1:T(2,128)}, u32[]{:S(2)}) copy-start(s32[64,2]{0,1:T(2,128)} %param.21) | copy-start | bytes 1540
  98.0 8.7 %copy-start.9 = (f32[64,2]{0,1:T(2,128)S(1)}, f32[64,2]{0,1:T(2,128)}, u32[]{:S(2)}) copy-start(f32[64,2]{0,1:T(2,128)} %param.22) | copy-start | bytes 1540
  98.0 58.0 %all-to-all-start.2 = ((bf16[4,32,2,2,1,8,256]{6,5,3,2,0,4,1:T(8,128)(2,1)}), bf16[4,32,2,2,1,8,256]{6,5,3,2,0,4,1:T(8,128)(2,1)S(1)}, u32[]{:S(2)}, u32[]{:S(2)}) async-start(bf16[4,32,2,2,1,8,256]{6,5,3,2,0,4,1:T(8,128)(2,1)} %copy.58), calls=%async_computation.2 | async-start | bytes 4194304 | tf_op jit(solution)/shard_map/all_to_all | solution.py:45
  158.4 5.4 %copy-start.2 = (bf16[8,2,256,256]{3,2,1,0:T(8,128)(2,1)S(1)}, bf16[8,2,256,256]{3,2,1,0:T(8,128)(2,1)}, u32[]{:S(2)}) copy-start(bf16[8,2,256,256]{3,2,1,0:T(8,128)(2,1)} %param.14) | copy-start | bytes 6291460
  163.8 11.3 %copy-start.6 = (f32[256]{0:T(256)S(1)}, f32[256]{0:T(256)}, u32[]{:S(2)}) copy-start(f32[256]{0:T(256)} %param.19) | copy-start | bytes 3076
  163.8 12.1 %copy-start.3 = (bf16[256,256]{1,0:T(8,128)(2,1)S(1)}, bf16[256,256]{1,0:T(8,128)(2,1)}, u32[]{:S(2)}) copy-start(bf16[256,256]{1,0:T(8,128)(2,1)} %param.17) | copy-start | bytes 393220
  168.0 75.3 %collective-permute-start.2 = (bf16[8,2,256,256]{3,2,1,0:T(8,128)(2,1)}, bf16[8,2,256,256]{3,2,1,0:T(8,128)(2,1)}, u32[]{:S(2)}, u32[]{:S(2)}) collective-permute-start(bf16[8,2,256,256]{3,2,1,0:T(8,128)(2,1)} %fusion.1), channel_id=1, source_target_pairs={{0,1},{1,2},{2,3},{3,4},{4,5},{5,6},{6,7},{7,8},{8,9},{9,10},{10,1... | collective-permute-start | bytes 6291464 | tf_op jit(solution)/shard_map/ppermute | solution.py:14
  173.1 70.2 %collective-permute-start.3 = (bf16[8,2,256,256]{3,2,1,0:T(8,128)(2,1)}, bf16[8,2,256,256]{3,2,1,0:T(8,128)(2,1)}, u32[]{:S(2)}, u32[]{:S(2)}) collective-permute-start(bf16[8,2,256,256]{3,2,1,0:T(8,128)(2,1)} %fusion.1), channel_id=1, source_target_pairs={{1,0},{2,1},{3,2},{4,3},{5,4},{6,5},{7,6},{8,7},{9,8},{10,9},{11,1... | collective-permute-start | bytes 6291464 | tf_op jit(solution)/shard_map/ppermute | solution.py:17
  182.2 50.2 %collective-permute-start = (bf16[2,2,256,256]{3,2,1,0:T(8,128)(2,1)}, bf16[2,2,256,256]{3,2,1,0:T(8,128)(2,1)S(1)}, u32[]{:S(2)}, u32[]{:S(2)}) collective-permute-start(bf16[2,2,256,256]{3,2,1,0:T(8,128)(2,1)} %get-tuple-element.12), channel_id=1, source_target_pairs={{0,32},{32,64},{64,96},{96,128},{128,160},{160,192},{192,224},{1,3... | collective-permute-start | bytes 1572872 | tf_op jit(solution)/shard_map/ppermute | solution.py:14
  184.4 48.0 %collective-permute-start.1 = (bf16[2,2,256,256]{3,2,1,0:T(8,128)(2,1)}, bf16[2,2,256,256]{3,2,1,0:T(8,128)(2,1)S(1)}, u32[]{:S(2)}, u32[]{:S(2)}) collective-permute-start(bf16[2,2,256,256]{3,2,1,0:T(8,128)(2,1)} %get-tuple-element.13), channel_id=1, source_target_pairs={{32,0},{64,32},{96,64},{128,96},{160,128},{192,160},{224,192},{33,... | collective-permute-start | bytes 1572872 | tf_op jit(solution)/shard_map/ppermute | solution.py:17
  259.3 10.0 %copy-start.4 = (bf16[256,256]{1,0:T(8,128)(2,1)S(1)}, bf16[256,256]{1,0:T(8,128)(2,1)}, u32[]{:S(2)}) copy-start(bf16[256,256]{1,0:T(8,128)(2,1)} %param.18) | copy-start | bytes 393220
  269.3 6.3 %copy-start.5 = (f32[256,256]{1,0:T(8,128)S(1)}, f32[256,256]{1,0:T(8,128)}, u32[]{:S(2)}) copy-start(f32[256,256]{1,0:T(8,128)} %broadcast_add_fusion) | copy-start | bytes 786436
  275.6 5.5 %copy-start.1 = (bf16[256,256]{1,0:T(8,128)(2,1)S(1)}, bf16[256,256]{1,0:T(8,128)(2,1)}, u32[]{:S(2)}) copy-start(bf16[256,256]{1,0:T(8,128)(2,1)} %param.16) | copy-start | bytes 393220
where the time goes:
time: 282 us; the launch traced here: 281 us
  blocking collectives  90.8 us (32%)
  waiting for transfers between devices  88.4 us (31%)
  local copies, waits for them, and re-layouts  32.2 us (11%)
  matrix products  29.2 us (10%)
  starting transfers between devices  22.5 us (8%)
  other arithmetic  17.1 us (6%)
    all_to_all x1, blocking collectives, flip_blocks(): lax.all_to_all(block.reshape(1, rows_i, cols_j, width, width), 'occj', sp...  61.2 us
    all_to_all x1, waiting for transfers between devices, flip_blocks(): lax.all_to_all(moved, 'occj', split_axis=1, concat_axis=4, tiled=True)  49.1 us
    ppermute x2, waiting for transfers between devices, extended_2(): lax.ppermute(lax.slice_in_dim(block, block.shape[dim] - width, None, axis...  39.3 us
    all_to_all x1, blocking collectives, flip_blocks(): lax.all_to_all(moved.reshape(count_j, 1, rows_i, cols_j, slab, width), 'o...  29.6 us
    dot_general x1, matrix products, per_device(): jnp.einsum('rsab,bc->rsac', b1, intersection_full, preferred_element_type...  10 us
    gather x2, local copies, waits for them, and re-layouts, mix_columns(): picked = jnp.take(extended, local[:, slot], axis=1).astype(jnp.float32)  9.58 us
    concatenate x2, other arithmetic, extended_2(): block = jnp.concatenate([low, block, high], axis=dim)  9.47 us
    all_to_all x1, starting transfers between devices, flip_blocks(): lax.all_to_all(moved, 'occj', split_axis=1, concat_axis=4, tiled=True)  7.93 us
  transfers between devices with their start and end apart: 5, of which 2 were waited for; matrix products, arithmetic and copies ran while one was open for 8% of the time, Pallas kernels for 0%

commit v1 on v0

v1 whole, which is shorter than its diff:
```python
import functools

import jax
import jax.numpy as jnp
from jax import lax
from jax.experimental import pallas as pl
from jax.experimental.pallas import tpu as pltpu
from jax.sharding import Mesh
from jax.sharding import PartitionSpec as P

REACH = 2
SR = 16
SL = 128


def _cut(block):
    w = block.shape[0]
    parts = [
        block[SR * u : SR * u + SR, SL * v : SL * v + SL][None]
        for u in range(w // SR)
        for v in range(w // SL)
    ]
    return jnp.concatenate(parts, axis=0)


def _glue(slabs, w):
    halves = w // SL
    cols = [
        jnp.concatenate([slabs[u * halves + v] for u in range(w // SR)], axis=0)
        for v in range(halves)
    ]
    return jnp.concatenate(cols, axis=1)


def pack_kernel(x_ref, o_ref, *, flip):
    for r in range(x_ref.shape[0]):
        for s in range(x_ref.shape[1]):
            block = x_ref[r, s]
            if flip:
                block = block.astype(jnp.float32).T.astype(jnp.bfloat16)
            w = block.shape[0]
            for u in range(w // SR):
                for v in range(w // SL):
                    o_ref[u * (w // SL) + v, r, s] = block[
                        SR * u : SR * u + SR, SL * v : SL * v + SL
                    ]


def pack(x, flip):
    rows, cols, w, _ = x.shape
    n = (w // SR) * (w // SL)
    step = 2
    return pl.pallas_call(
        functools.partial(pack_kernel, flip=flip),
        grid=(rows // step,),
        in_specs=[pl.BlockSpec((step, cols, w, w), lambda k: (k, 0, 0, 0))],
        out_specs=pl.BlockSpec((n, step, cols, SR, SL), lambda k: (0, k, 0, 0, 0)),
        out_shape=jax.ShapeDtypeStruct((n, rows, cols, SR, SL), jnp.bfloat16),
        name="pack_flip" if flip else "pack",
    )(x)


def sym_kernel(a_ref, b_ref, o_ref, lo_ref, hi_ref):
    _, g_n, r_n, s_n, _, _ = a_ref.shape
    j_n = g_n * s_n
    for g in range(g_n):
        for s in range(s_n):
            j = g * s_n + s
            for i in range(r_n):
                own = a_ref[0, g, i, s].astype(jnp.float32)
                mir = b_ref[0, i // s_n, j, i % s_n].astype(jnp.float32)
                val = (0.5 * (own + mir)).astype(jnp.bfloat16)
                o_ref[j, i] = val
                if j < REACH:
                    lo_ref[j, i] = val
                if j >= j_n - REACH:
                    hi_ref[j - j_n + REACH, i] = val


def symmetrize(a, b):
    t_n, g_n, r_n, s_n, _, _ = a.shape
    j_n = g_n * s_n
    spec = pl.BlockSpec((1, g_n, r_n, s_n, SR, SL), lambda t: (t, 0, 0, 0, 0, 0))
    out = lambda n: pl.BlockSpec((n, r_n, SR, SL), lambda t: (0, t, 0, 0))
    shape = lambda n: jax.ShapeDtypeStruct((n, t_n * r_n, SR, SL), jnp.bfloat16)
    return pl.pallas_call(
        sym_kernel,
        grid=(t_n,),
        in_specs=[spec, spec],
        out_specs=[out(j_n), out(REACH), out(REACH)],
        out_shape=[shape(j_n), shape(REACH), shape(REACH)],
        name="sym",
    )(a, b)


def coup_kernel(
    lists_ref, weights_ref, start_ref, sym_ref, left_ref, right_ref, o_ref, ext_ref, sems
):
    t = pl.program_id(0)
    j_n = sym_ref.shape[0]
    copies = [
        pltpu.make_async_copy(left_ref, ext_ref.at[pl.ds(0, REACH)], sems.at[0]),
        pltpu.make_async_copy(sym_ref, ext_ref.at[pl.ds(REACH, j_n)], sems.at[1]),
        pltpu.make_async_copy(right_ref, ext_ref.at[pl.ds(REACH + j_n, REACH)], sems.at[2]),
    ]

    @pl.when(t == 0)
    def _():
        for c in copies:
            c.start()
        for c in copies:
            c.wait()

    _, g_n, r_n, s_n, _, _ = o_ref.shape
    start = start_ref[0]
    for j in range(j_n):
        gj = start + j
        p0 = lists_ref[gj, 0] - start + REACH
        p1 = lists_ref[gj, 1] - start + REACH
        w0 = weights_ref[gj, 0]
        w1 = weights_ref[gj, 1]
        for r in range(r_n):
            i = t * r_n + r
            row = weights_ref[i, 0] * ext_ref[j + REACH, lists_ref[i, 0]].astype(jnp.float32)
            row = row + weights_ref[i, 1] * ext_ref[j + REACH, lists_ref[i, 1]].astype(jnp.float32)
            col = w0 * ext_ref[p0, i].astype(jnp.float32)
            col = col + w1 * ext_ref[p1, i].astype(jnp.float32)
            total = row.astype(jnp.bfloat16).astype(jnp.float32) + col.astype(jnp.bfloat16).astype(
                jnp.float32
            )
            o_ref[0, j // s_n, r, j % s_n] = total.astype(jnp.bfloat16)


def couple(lists, weights, start, sym, left, right, r_n, s_n):
    j_n, i_n = sym.shape[:2]
    g_n = j_n // s_n
    t_n = i_n // r_n
    hbm = pl.BlockSpec(memory_space=pl.ANY)
    return pl.pallas_call(
        coup_kernel,
        grid_spec=pltpu.PrefetchScalarGridSpec(
            num_scalar_prefetch=3,
            grid=(t_n,),
            in_specs=[hbm, hbm, hbm],
            out_specs=pl.BlockSpec((1, g_n, r_n, s_n, SR, SL), lambda t, *_: (t, 0, 0, 0, 0, 0)),
            scratch_shapes=[
                pltpu.VMEM((j_n + 2 * REACH, i_n, SR, SL), jnp.bfloat16),
                pltpu.SemaphoreType.DMA((3,)),
            ],
        ),
        out_shape=jax.ShapeDtypeStruct((t_n, g_n, r_n, s_n, SR, SL), jnp.bfloat16),
        name="couple",
    )(lists, weights, start, sym, left, right)


def _dot(x, y):
    return jnp.dot(x, y, preferred_element_type=jnp.float32)


def pre_kernel(amp_ref, exch_ref, fock_ref, over_ref, o_ref):
    fock = fock_ref[...]
    over = over_ref[...]
    for s in range(amp_ref.shape[1]):
        amp = amp_ref[0, s]
        first = _dot(_dot(fock, amp).astype(jnp.bfloat16), over)
        second = _dot(_dot(over, amp).astype(jnp.bfloat16), fock)
        o_ref[0, s] = exch_ref[0, s].astype(jnp.float32) + first + second


def precompute(amp, exch, fock, over):
    rows, cols, w, _ = amp.shape
    big = pl.BlockSpec((1, cols, w, w), lambda k: (k, 0, 0, 0))
    mat = pl.BlockSpec((w, w), lambda k: (0, 0))
    return pl.pallas_call(
        pre_kernel,
        grid=(rows,),
        in_specs=[big, big, mat, mat],
        out_specs=big,
        out_shape=jax.ShapeDtypeStruct(amp.shape, jnp.float32),
        name="precompute",
    )(amp, exch, fock, over)


def post_kernel(
    occ_ref,
    base_ref,
    amp_ref,
    coup_ref,
    mrow_i_ref,
    mrow_j_ref,
    mcol_i_ref,
    mcol_j_ref,
    over_ref,
    trans_ref,
    tt_ref,
    erow_ref,
    ecol_ref,
    res_ref,
    new_ref,
):
    k = pl.program_id(0)
    w = amp_ref.shape[2]
    rows = pl.num_programs(0)
    over = over_ref[...]
    trans = trans_ref[...]
    tt = tt_ref[...]
    for s in range(amp_ref.shape[1]):
        row = jnp.maximum(mrow_i_ref[0], mrow_j_ref[s])
        col = jnp.maximum(mcol_i_ref[0], mcol_j_ref[s])
        two = col * row
        cm = (_glue([coup_ref[n, 0, s] for n in range(coup_ref.shape[0])], w).astype(jnp.float32) * two).astype(
            jnp.bfloat16
        )
        third = _dot(_dot(over, cm).astype(jnp.bfloat16), over)
        res = two * (base_ref[0, s] - third)
        res_ref[0, s] = res
        q = _dot(_dot(tt, res.astype(jnp.bfloat16)).astype(jnp.bfloat16), trans)
        denom = ecol_ref[...] + erow_ref[...] - (occ_ref[k] + occ_ref[rows + s])
        z = (q / denom).astype(jnp.bfloat16)
        u = _dot(_dot(trans, z).astype(jnp.bfloat16), tt)
        new_ref[0, s] = (amp_ref[0, s].astype(jnp.float32) - u).astype(jnp.bfloat16)


def finish(occ, base, amp, coup, mask_i, mask_j, over, trans, energy):
    rows, cols, w, _ = amp.shape
    n = coup.shape[0]
    big = pl.BlockSpec((1, cols, w, w), lambda k, *_: (k, 0, 0, 0))
    mat = pl.BlockSpec((w, w), lambda k, *_: (0, 0))
    return pl.pallas_call(
        post_kernel,
        grid_spec=pltpu.PrefetchScalarGridSpec(
            num_scalar_prefetch=1,
            grid=(rows,),
            in_specs=[
                big,
                big,
                pl.BlockSpec((n, 1, cols, SR, SL), lambda k, *_: (0, k, 0, 0, 0)),
                pl.BlockSpec((1, 1, w), lambda k, *_: (k, 0, 0)),
                pl.BlockSpec((cols, 1, w), lambda k, *_: (0, 0, 0)),
                pl.BlockSpec((1, w, 1), lambda k, *_: (k, 0, 0)),
                pl.BlockSpec((cols, w, 1), lambda k, *_: (0, 0, 0)),
                mat,
                mat,
                mat,
                pl.BlockSpec((1, w), lambda k, *_: (0, 0)),
                pl.BlockSpec((w, 1), lambda k, *_: (0, 0)),
            ],
            out_specs=[big, big],
        ),
        out_shape=[
            jax.ShapeDtypeStruct(amp.shape, jnp.float32),
            jax.ShapeDtypeStruct(amp.shape, jnp.bfloat16),
        ],
        name="finish",
    )(
        occ,
        base,
        amp,
        coup,
        mask_i[:, None, :],
        mask_j[:, None, :],
        mask_i[:, :, None],
        mask_j[:, :, None],
        over,
        trans,
        trans.T,
        energy[None, :],
        energy[:, None],
    )


def per_device(
    amplitudes,
    exchange,
    fock_virt,
    intersection,
    transform,
    virt_energy,
    occ_energy,
    partners,
    coupling,
    domain,
):
    rows, cols, width, _ = amplitudes.shape
    tiles = domain.shape[1]
    a_n = lax.axis_size("a")
    z_n = lax.axis_size("z")
    g_n = lax.axis_size("g")
    start_i = lax.axis_index("a") * rows
    start_z = lax.axis_index("z") * (g_n * cols)
    start_j = start_z + lax.axis_index("g") * cols
    plane = ("a", "g")
    n = a_n * g_n

    over = (jnp.eye(width, dtype=jnp.float32) + intersection.astype(jnp.float32)).astype(
        jnp.bfloat16
    )
    flipped = pack(amplitudes, True)
    flipped = lax.all_to_all(flipped, plane, 0, 0, tiled=True)
    flipped = lax.all_to_all(flipped, "z", 0, 0, tiled=True)
    own = lax.all_to_all(pack(amplitudes, False), plane, 0, 0, tiled=True)
    shape = (a_n, g_n, rows, cols, SR, SL)
    sym, low, high = symmetrize(own.reshape(shape), flipped.reshape(shape))
    up = [(k, k + 1) for k in range(z_n - 1)]
    down = [(k + 1, k) for k in range(z_n - 1)]
    left = lax.ppermute(high, "z", up)
    right = lax.ppermute(low, "z", down)
    base = precompute(amplitudes, exchange, fock_virt, over)
    coup = couple(partners, coupling, start_z[None], sym, left, right, rows, cols)
    coup = lax.all_to_all(coup.reshape(n, rows, cols, SR, SL), plane, 0, 0, tiled=True)

    masks = jnp.repeat(domain.astype(jnp.float32), width // tiles, axis=1)
    mask_i = lax.dynamic_slice_in_dim(masks, start_i, rows, 0)
    mask_j = lax.dynamic_slice_in_dim(masks, start_j, cols, 0)
    occ = jnp.concatenate(
        [
            lax.dynamic_slice_in_dim(occ_energy, start_i, rows, 0),
            lax.dynamic_slice_in_dim(occ_energy, start_j, cols, 0),
        ]
    )
    return tuple(
        finish(occ, base, amplitudes, coup, mask_i, mask_j, over, transform, virt_energy)
    )


def solution(mesh):
    i_n, j_n = mesh.shape["occi"], mesh.shape["occj"]
    group = j_n // i_n
    inner = Mesh(mesh.devices.reshape(i_n, j_n // group, group), ("a", "z", "g"))
    pairs = P("a", ("z", "g"), None, None)
    return jax.shard_map(
        per_device,
        mesh=inner,
        in_specs=(pairs, pairs, P(), P(), P(), P(), P(), P(), P(), P()),
        out_specs=(pairs, pairs),
        check_vma=False,
    )
```

time: 282 us -> 220 us (0.78)
  Pallas kernels: 0 us -> 47.6 us
  waiting for transfers between devices: 88.4 us -> 44.8 us
  matrix products: 29.2 us -> 0 us
  local copies, waits for them, and re-layouts: 32.2 us -> 9.02 us
  other arithmetic: 17.1 us -> 1.27 us
    pallas_call x0 -> x6, Pallas kernels: none -> 47.6 us  [the longest x1 16.9 us: finish(): pl.pallas_call(post_kernel, grid_spec=pltpu.PrefetchScalarGridSpec(num_sc...]
    ppermute x4 -> x2, waiting for transfers between devices: 39.3 us -> 9.97 us  [the longest x1 6.21 us: per_device(): left = lax.ppermute(high, 'z', up)]
    dot_general x5 -> x0, matrix products: 29.2 us -> none  [the longest x1 10 us: per_device(): jnp.einsum('rsab,bc->rsac', b1, intersection_full, preferred_element_type...]
    gather x4 -> x0, local copies, waits for them, and re-layouts: 17.4 us -> none  [the longest x2 9.58 us: mix_columns(): picked = jnp.take(extended, local[:, slot], axis=1).astype(jnp.float32)]
    all_to_all x1 -> x2, waiting for transfers between devices: 49.1 us -> 34.8 us  [the longest x1 23 us: per_device(): own = lax.all_to_all(pack(amplitudes, False), plane, 0, 0, tiled=True)]
    ppermute x4 -> x2, starting transfers between devices: 14.6 us -> 2.6 us  [the longest x1 1.31 us: per_device(): left = lax.ppermute(high, 'z', up)]
    all_to_all x1 -> x2, starting transfers between devices: 7.93 us -> 18.3 us  [the longest x1 10.4 us: per_device(): lax.all_to_all(coup.reshape(n, rows, cols, SR, SL), plane, 0, 0, tiled=True)]
    concatenate x2 -> x1, other arithmetic: 9.47 us -> 0.59 us  [per_device(): jnp.concatenate([lax.dynamic_slice_in_dim(occ_energy, start_i, rows, 0),...]
  transfers between devices with their start and end apart: 5 -> 4, of which waited for: 2 -> 4; matrix products, arithmetic and copies ran while one was open for 8% -> 4% of each run, Pallas kernels for 0% -> 6%
where the time goes in v1:
time: 220 us; the launch traced here: 217 us
  blocking collectives  92.7 us (42%)
  Pallas kernels  47.6 us (22%)
  waiting for transfers between devices  44.8 us (20%)
  starting transfers between devices  20.9 us (10%)
  local copies, waits for them, and re-layouts  9.02 us (4%)
    all_to_all x1, blocking collectives, per_device(): flipped = lax.all_to_all(flipped, 'z', 0, 0, tiled=True)  58.5 us
    all_to_all x1, blocking collectives, per_device(): flipped = lax.all_to_all(flipped, plane, 0, 0, tiled=True)  34.2 us
    all_to_all x1, waiting for transfers between devices, per_device(): own = lax.all_to_all(pack(amplitudes, False), plane, 0, 0, tiled=True)  23 us
    pallas_call x1, Pallas kernels, finish(): pl.pallas_call(post_kernel, grid_spec=pltpu.PrefetchScalarGridSpec(num_sc...  16.9 us
    all_to_all x1, waiting for transfers between devices, per_device(): lax.all_to_all(coup.reshape(n, rows, cols, SR, SL), plane, 0, 0, tiled=True)  11.9 us
    all_to_all x1, starting transfers between devices, per_device(): lax.all_to_all(coup.reshape(n, rows, cols, SR, SL), plane, 0, 0, tiled=True)  10.4 us
    pallas_call x1, Pallas kernels, precompute(): pl.pallas_call(pre_kernel, grid=(rows,), in_specs=[big, big, mat, mat], o...  8.46 us
    pallas_call x2, Pallas kernels, pack(): pl.pallas_call(functools.partial(pack_kernel, flip=flip), grid=(rows // s...  8.01 us
  transfers between devices with their start and end apart: 4, of which 4 were waited for; matrix products, arithmetic and copies ran while one was open for 4% of the time, Pallas kernels for 6%

profile of v1, /device:TPU:3, one launch (start us, length us, event | category | flops | bytes accessed | tf_op | source)
XLA Modules:
  0.0 217.1 jit_solution(759042444155874491)
XLA Ops:
  0.6 3.9 %pack.1 = bf16[32,8,2,16,128]{4,3,2,1,0:T(8,128)(2,1)} custom-call(bf16[8,2,256,256]{3,2,1,0:T(8,128)(2,1)} %amp_ref.3), custom_call_target="tpu_custom_call" | custom-call | tf_op jit(solution)/shard_map/pack/pallas_call | solution.py:53
  4.5 7.9 %all-to-all-start = ((bf16[32,8,2,16,128]{4,3,2,1,0:T(8,128)(2,1)}), bf16[32,8,2,16,128]{4,3,2,1,0:T(8,128)(2,1)S(1)}, u32[]{:S(2)}, u32[]{:S(2)}) async-start(bf16[32,8,2,16,128]{4,3,2,1,0:T(8,128)(2,1)} %pack.1), calls=%async_computation | async-start | bytes 4194304 | tf_op jit(solution)/shard_map/all_to_all | solution.py:301
  12.4 4.1 %pack_flip.1 = bf16[32,8,2,16,128]{4,3,2,1,0:T(8,128)(2,1)} custom-call(bf16[8,2,256,256]{3,2,1,0:T(8,128)(2,1)} %amp_ref.3), custom_call_target="tpu_custom_call" | custom-call | tf_op jit(solution)/shard_map/pack_flip/pallas_call | solution.py:53
  16.5 23.0 %all-to-all-done = bf16[32,8,2,16,128]{4,3,2,1,0:T(8,128)(2,1)S(1)} async-done(((bf16[32,8,2,16,128]{4,3,2,1,0:T(8,128)(2,1)}), bf16[32,8,2,16,128]{4,3,2,1,0:T(8,128)(2,1)S(1)}, u32[]{:S(2)}, u32[]{:S(2)}) %all-to-all-start) | async-done | bytes 2097184 | tf_op jit(solution)/shard_map/all_to_all | solution.py:301
  39.5 0.0 copy-start
  39.5 34.2 %all_to_all.20 = bf16[32,8,2,16,128]{4,3,2,1,0:T(8,128)(2,1)S(1)} all-to-all(bf16[32,8,2,16,128]{4,3,2,1,0:T(8,128)(2,1)} %pack_flip.1), channel_id=1, replica_groups=mesh['a'=8,'z'=8,'g'=4] {'a','g'}, dimensions={0} | all-to-all | bytes 4194304 | tf_op jit(solution)/shard_map/all_to_all | solution.py:299
  73.7 58.5 %all_to_all.21 = bf16[32,8,2,16,128]{4,3,2,1,0:T(8,128)(2,1)} all-to-all(bf16[32,8,2,16,128]{4,3,2,1,0:T(8,128)(2,1)S(1)} %all_to_all.20), channel_id=1, replica_groups=mesh['a'=8,'z'=8,'g'=4] {'z'}, dimensions={0} | all-to-all | bytes 4194304 | tf_op jit(solution)/shard_map/all_to_all | solution.py:300
  132.2 0.0 copy-done
  132.2 0.0 copy-start.8
  132.2 0.0 copy-start.9
  132.2 6.5 %sym.1 = (bf16[8,64,16,128]{3,2,1,0:T(8,128)(2,1)}, bf16[2,64,16,128]{3,2,1,0:T(8,128)(2,1)}, bf16[2,64,16,128]{3,2,1,0:T(8,128)(2,1)}) custom-call(bf16[8,4,8,2,16,128]{5,4,3,2,1,0:T(8,128)(2,1)} %bitcast.11, bf16[8,4,8,2,16,128]{5,4,3,2,1,0:T(8,128)(2,1)} %bitcast.12), custom_call_target="tpu_custom_call" | custom-call | tf_op jit(solution)/shard_map/sym/pallas_call | solution.py:86
  138.7 1.3 collective-permute-start
  140.0 1.3 collective-permute-start.1
  141.3 0.0 copy-done.8
  141.3 0.7 copy.16.lists_ref
  142.0 0.0 copy-done.9
  142.0 0.7 copy.17.weights_ref
  142.7 6.2 %collective-permute-done.left_ref = bf16[2,64,16,128]{3,2,1,0:T(8,128)(2,1)S(1)} collective-permute-done((bf16[2,64,16,128]{3,2,1,0:T(8,128)(2,1)}, bf16[2,64,16,128]{3,2,1,0:T(8,128)(2,1)S(1)}, u32[]{:S(2)}, u32[]{:S(2)}) %collective-permute-start) | collective-permute-done | bytes 524320 | tf_op jit(solution)/shard_map/ppermute | solution.py:306
  148.9 0.0 copy-start.2
  148.9 3.8 %collective-permute-done.1.right_ref = bf16[2,64,16,128]{3,2,1,0:T(8,128)(2,1)S(1)} collective-permute-done((bf16[2,64,16,128]{3,2,1,0:T(8,128)(2,1)}, bf16[2,64,16,128]{3,2,1,0:T(8,128)(2,1)S(1)}, u32[]{:S(2)}, u32[]{:S(2)}) %collective-permute-start.1) | collective-permute-done | bytes 524320 | tf_op jit(solution)/shard_map/ppermute | solution.py:307
  152.7 0.0 copy-start.3
  152.7 0.0 copy-done.2
  152.7 0.8 copy-done.3
  153.5 7.8 %couple.1 = bf16[8,4,8,2,16,128]{5,4,3,2,1,0:T(8,128)(2,1)} custom-call(s32[64,2]{1,0:T(8,128)} %copy.16.lists_ref, f32[64,2]{1,0:T(8,128)} %copy.17.weights_ref, s32[1]{0:T(128)} %bitcast.start_ref, bf16[8,64,16,128]{3,2,1,0:T(8,128)(2,1)} %get-tuple-element.5.sym_ref, bf16[2,64,16,128]{3,2,1,0:T(8,128)(2,1)} %copy-done.2, bf16[2,64,16,128]{3,2,1,0:T(8,128)(2,1)} %copy-done.3), custom_call_target="tpu_custom_call" | custom-call | tf_op jit(solution)/shard_map/couple/pallas_call | solution.py:139
  161.3 0.0 copy-start.10
  161.3 0.0 copy-start.6
  161.3 0.0 copy-start.7
  161.3 0.0 copy-start.4
  161.3 10.4 %all-to-all-start.3 = ((bf16[32,8,2,16,128]{4,3,2,1,0:T(8,128)(2,1)}), bf16[32,8,2,16,128]{4,3,2,1,0:T(8,128)(2,1)S(1)}, u32[]{:S(2)}, u32[]{:S(2)}) async-start(bf16[32,8,2,16,128]{4,3,2,1,0:T(8,128)(2,1)} %bitcast.10), calls=%async_computation.3 | async-start | bytes 4194304 | tf_op jit(solution)/shard_map/all_to_all | solution.py:310
  171.7 0.0 copy-start.5
  171.8 0.0 copy-done.10
  171.8 0.1 dynamic_slice.13
  171.9 0.1 dynamic_slice.12
  171.9 0.0 copy-done.6
  171.9 0.1 constant_dynamic-slice_fusion
  172.0 0.1 copy.19
  172.1 0.1 constant_dynamic-slice_fusion.1
  172.2 0.1 copy.18
  172.3 0.6 broadcast_in_dim.27.mrow_j_ref
  172.9 0.6 broadcast_in_dim.26.mrow_i_ref
  173.5 0.0 copy-done.7
  173.5 0.8 copy.25.ecol_ref
  174.3 0.0 copy-done.4
  174.3 0.8 copy.22
  175.0 0.9 copy.24.mcol_j_ref
  175.9 1.4 copy.23.mcol_i_ref
  177.2 0.0 copy-done.5
  177.2 0.7 add_convert_fusion.over_ref
  177.9 8.5 %precompute.1.base_ref = f32[8,2,256,256]{3,2,1,0:T(8,128)} custom-call(bf16[8,2,256,256]{3,2,1,0:T(8,128)(2,1)} %amp_ref.3, bf16[8,2,256,256]{3,2,1,0:T(8,128)(2,1)} %exch_ref.1, bf16[256,256]{1,0:T(8,128)(2,1)} %fock_ref.1, bf16[256,256]{1,0:T(8,128)(2,1)} %add_convert_fusion.over_ref), custom_call_target="tpu_custom_call" | custom-call | tf_op jit(solution)/shard_map/precompute/pallas_call | solution.py:174
  186.4 0.6 pad_maximum_fusion.occ_ref
  187.0 11.9 %all-to-all-done.3.coup_ref = bf16[32,8,2,16,128]{4,3,2,1,0:T(8,128)(2,1)S(1)} async-done(((bf16[32,8,2,16,128]{4,3,2,1,0:T(8,128)(2,1)}), bf16[32,8,2,16,128]{4,3,2,1,0:T(8,128)(2,1)S(1)}, u32[]{:S(2)}, u32[]{:S(2)}) %all-to-all-start.3) | async-done | bytes 2097184 | tf_op jit(solution)/shard_map/all_to_all | solution.py:310
  198.8 0.0 copy-start.1
  198.8 1.3 copy-done.1
  200.2 16.9 %finish.1 = (f32[8,2,256,256]{3,2,1,0:T(8,128)}, bf16[8,2,256,256]{3,2,1,0:T(8,128)(2,1)}) custom-call(f32[10]{0:T(128)} %pad_maximum_fusion.occ_ref, f32[8,2,256,256]{3,2,1,0:T(8,128)} %precompute.1.base_ref, bf16[8,2,256,256]{3,2,1,0:T(8,128)(2,1)} %amp_ref.3, bf16[32,8,2,16,128]{4,3,2,1,0:T(8,128)(2,1)} %copy-done.1, ...), custom_call_target="tpu_custom_call" | custom-call | tf_op jit(solution)/shard_map/finish/pallas_call | solution.py:229
  (2 shorter events, 0.0 us)
Async XLA Ops:
  4.5 35.0 %all-to-all-start = ((bf16[32,8,2,16,128]{4,3,2,1,0:T(8,128)(2,1)}), bf16[32,8,2,16,128]{4,3,2,1,0:T(8,128)(2,1)S(1)}, u32[]{:S(2)}, u32[]{:S(2)}) async-start(bf16[32,8,2,16,128]{4,3,2,1,0:T(8,128)(2,1)} %pack.1), calls=%async_computation | async-start | bytes 4194304 | tf_op jit(solution)/shard_map/all_to_all | solution.py:301
  39.5 92.7 %copy-start = (bf16[32,8,2,16,128]{4,3,2,1,0:T(8,128)(2,1)}, bf16[32,8,2,16,128]{4,3,2,1,0:T(8,128)(2,1)S(1)}, u32[]{:S(2)}) copy-start(bf16[32,8,2,16,128]{4,3,2,1,0:T(8,128)(2,1)S(1)} %all-to-all-done) | copy-start | bytes 6291460
  132.2 9.1 %copy-start.8 = (s32[64,2]{0,1:T(2,128)S(1)}, s32[64,2]{0,1:T(2,128)}, u32[]{:S(2)}) copy-start(s32[64,2]{0,1:T(2,128)} %param.17) | copy-start | bytes 1540
  132.2 9.8 %copy-start.9 = (f32[64,2]{0,1:T(2,128)S(1)}, f32[64,2]{0,1:T(2,128)}, u32[]{:S(2)}) copy-start(f32[64,2]{0,1:T(2,128)} %param.18) | copy-start | bytes 1540
  138.7 10.2 %collective-permute-start = (bf16[2,64,16,128]{3,2,1,0:T(8,128)(2,1)}, bf16[2,64,16,128]{3,2,1,0:T(8,128)(2,1)S(1)}, u32[]{:S(2)}, u32[]{:S(2)}) collective-permute-start(bf16[2,64,16,128]{3,2,1,0:T(8,128)(2,1)} %get-tuple-element.6), channel_id=1, source_target_pairs={{0,4},{4,8},{8,12},{12,16},{16,20},{20,24},{24,28},{1,5},{5,9},{9,... | collective-permute-start | bytes 1572872 | tf_op jit(solution)/shard_map/ppermute | solution.py:306
  140.0 12.7 %collective-permute-start.1 = (bf16[2,64,16,128]{3,2,1,0:T(8,128)(2,1)}, bf16[2,64,16,128]{3,2,1,0:T(8,128)(2,1)S(1)}, u32[]{:S(2)}, u32[]{:S(2)}) collective-permute-start(bf16[2,64,16,128]{3,2,1,0:T(8,128)(2,1)} %get-tuple-element.7), channel_id=1, source_target_pairs={{4,0},{8,4},{12,8},{16,12},{20,16},{24,20},{28,24},{5,1},{9,5},{13... | collective-permute-start | bytes 1572872 | tf_op jit(solution)/shard_map/ppermute | solution.py:307
  148.9 3.8 %copy-start.2 = (bf16[2,64,16,128]{3,2,1,0:T(8,128)(2,1)}, bf16[2,64,16,128]{3,2,1,0:T(8,128)(2,1)S(1)}, u32[]{:S(2)}) copy-start(bf16[2,64,16,128]{3,2,1,0:T(8,128)(2,1)S(1)} %collective-permute-done.left_ref) | copy-start | bytes 1572868
  152.7 0.8 copy-start.3
  161.3 10.5 %copy-start.10 = (f32[64]{0:T(128)S(1)}, f32[64]{0:T(128)}, u32[]{:S(2)}) copy-start(f32[64]{0:T(128)} %param.16) | copy-start | bytes 772
  161.3 10.6 %copy-start.6 = (s32[64,8]{0,1:T(8,128)S(1)}, s32[64,8]{0,1:T(8,128)}, u32[]{:S(2)}) copy-start(s32[64,8]{0,1:T(8,128)} %param.19) | copy-start | bytes 6148
  161.3 12.2 %copy-start.7 = (f32[256]{0:T(256)S(1)}, f32[256]{0:T(256)}, u32[]{:S(2)}) copy-start(f32[256]{0:T(256)} %param.15) | copy-start | bytes 3076
  161.3 13.0 %copy-start.4 = (bf16[256,256]{1,0:T(8,128)(2,1)S(1)}, bf16[256,256]{1,0:T(8,128)(2,1)}, u32[]{:S(2)}) copy-start(bf16[256,256]{1,0:T(8,128)(2,1)} %trans_ref.1) | copy-start | bytes 393220
  161.3 37.5 %all-to-all-start.3 = ((bf16[32,8,2,16,128]{4,3,2,1,0:T(8,128)(2,1)}), bf16[32,8,2,16,128]{4,3,2,1,0:T(8,128)(2,1)S(1)}, u32[]{:S(2)}, u32[]{:S(2)}) async-start(bf16[32,8,2,16,128]{4,3,2,1,0:T(8,128)(2,1)} %bitcast.10), calls=%async_computation.3 | async-start | bytes 4194304 | tf_op jit(solution)/shard_map/all_to_all | solution.py:310
  171.7 5.5 %copy-start.5 = (bf16[256,256]{1,0:T(8,128)(2,1)S(1)}, bf16[256,256]{1,0:T(8,128)(2,1)}, u32[]{:S(2)}) copy-start(bf16[256,256]{1,0:T(8,128)(2,1)} %param.13) | copy-start | bytes 393220
  198.8 1.4 copy-start.1

commit v2 on v1

v2 whole, which is shorter than its diff:
```python
import functools

import jax
import jax.numpy as jnp
from jax import lax
from jax.experimental import pallas as pl
from jax.experimental.pallas import tpu as pltpu
from jax.sharding import Mesh
from jax.sharding import PartitionSpec as P

REACH = 2
CHUNKS = 2
VMEM = pl.BlockSpec(memory_space=pltpu.VMEM)
SMEM = pl.BlockSpec(memory_space=pltpu.SMEM)


def pack_kernel(x_ref, *o_refs, flip):
    n, _, _, sr, sl = o_refs[0].shape
    for r in range(x_ref.shape[0]):
        for s in range(x_ref.shape[1]):
            block = x_ref[r, s].astype(jnp.float32)
            if flip:
                block = block.T
            for h, o_ref in enumerate(o_refs):
                for u in range(n):
                    o_ref[u, r, s] = block[sr * u : sr * u + sr, sl * h : sl * h + sl].astype(
                        jnp.bfloat16
                    )


def pack(x, n, flip):
    rows, cols, w, _ = x.shape
    sr, sl = w // n, w // CHUNKS
    step = 2
    return pl.pallas_call(
        functools.partial(pack_kernel, flip=flip),
        grid=(rows // step,),
        in_specs=[pl.BlockSpec((step, cols, w, w), lambda k: (k, 0, 0, 0))],
        out_specs=[pl.BlockSpec((n, step, cols, sr, sl), lambda k: (0, k, 0, 0, 0))] * CHUNKS,
        out_shape=[jax.ShapeDtypeStruct((n, rows, cols, sr, sl), jnp.bfloat16)] * CHUNKS,
        name="pack_flip" if flip else "pack",
    )(x)


def sym_kernel(z_ref, a_ref, *refs):
    got, (o_ref, lo_ref, hi_ref) = refs[:-3], refs[-3:]
    t_n, g_n, r_n, s_n, _, _ = a_ref.shape
    j_n = g_n * s_n
    for k, b_ref in enumerate(got):
        t = lax.rem(z_ref[0] + (t_n - k), t_n)
        for j in range(j_n):
            for i in range(r_n):
                own = a_ref[t, j // s_n, i, j % s_n].astype(jnp.float32)
                mir = b_ref[i // s_n, j, i % s_n].astype(jnp.float32)
                val = (0.5 * (own + mir)).astype(jnp.bfloat16)
                o_ref[j, t * r_n + i] = val
                if j < REACH:
                    lo_ref[j, t * r_n + i] = val
                if j >= j_n - REACH:
                    hi_ref[j - j_n + REACH, t * r_n + i] = val


def symmetrize(z, own, got):
    t_n, g_n, r_n, s_n, sr, sl = own.shape
    shape = lambda n: jax.ShapeDtypeStruct((n, t_n * r_n, sr, sl), jnp.bfloat16)
    return pl.pallas_call(
        sym_kernel,
        in_specs=[SMEM, VMEM] + [VMEM] * len(got),
        out_specs=[VMEM] * 3,
        out_shape=[shape(g_n * s_n), shape(REACH), shape(REACH)],
        name="sym",
    )(z[None], own, *got)


def coup_kernel(lists_ref, weights_ref, start_ref, sym_ref, left_ref, right_ref, o_ref, ext_ref):
    j_n = sym_ref.shape[0]
    ext_ref[0:REACH] = left_ref[...]
    ext_ref[REACH : REACH + j_n] = sym_ref[...]
    ext_ref[REACH + j_n :] = right_ref[...]
    t_n, _, r_n, s_n, _, _ = o_ref.shape
    start = start_ref[0]

    def tile(t, carry):
        for j in range(j_n):
            gj = start + j
            p0 = lists_ref[gj, 0] - start + REACH
            p1 = lists_ref[gj, 1] - start + REACH
            w0 = weights_ref[gj, 0]
            w1 = weights_ref[gj, 1]
            for r in range(r_n):
                i = t * r_n + r
                row = weights_ref[i, 0] * sym_ref[j, lists_ref[i, 0]].astype(jnp.float32)
                row = row + weights_ref[i, 1] * sym_ref[j, lists_ref[i, 1]].astype(jnp.float32)
                col = w0 * ext_ref[p0, i].astype(jnp.float32)
                col = col + w1 * ext_ref[p1, i].astype(jnp.float32)
                total = row.astype(jnp.bfloat16).astype(jnp.float32) + col.astype(
                    jnp.bfloat16
                ).astype(jnp.float32)
                o_ref[t, j // s_n, r, j % s_n] = total.astype(jnp.bfloat16)
        return carry

    lax.fori_loop(0, t_n, tile, 0)


def couple(lists, weights, start, sym, left, right, r_n, s_n):
    j_n, i_n, sr, sl = sym.shape
    return pl.pallas_call(
        coup_kernel,
        in_specs=[SMEM, SMEM, SMEM, VMEM, VMEM, VMEM],
        out_specs=VMEM,
        out_shape=jax.ShapeDtypeStruct((i_n // r_n, j_n // s_n, r_n, s_n, sr, sl), jnp.bfloat16),
        scratch_shapes=[pltpu.VMEM((j_n + 2 * REACH, i_n, sr, sl), jnp.bfloat16)],
        name="couple",
    )(lists, weights, start, sym, left, right)


def _dot(x, y):
    return jnp.dot(x, y, preferred_element_type=jnp.float32)


def pre_kernel(amp_ref, exch_ref, fock_ref, over_ref, o_ref):
    fock = fock_ref[...]
    over = over_ref[...]
    for s in range(amp_ref.shape[1]):
        amp = amp_ref[0, s]
        first = _dot(_dot(fock, amp).astype(jnp.bfloat16), over)
        second = _dot(_dot(over, amp).astype(jnp.bfloat16), fock)
        o_ref[0, s] = exch_ref[0, s].astype(jnp.float32) + first + second


def precompute(amp, exch, fock, over):
    rows, cols, w, _ = amp.shape
    big = pl.BlockSpec((1, cols, w, w), lambda k: (k, 0, 0, 0))
    mat = pl.BlockSpec((w, w), lambda k: (0, 0))
    return pl.pallas_call(
        pre_kernel,
        grid=(rows,),
        in_specs=[big, big, mat, mat],
        out_specs=big,
        out_shape=jax.ShapeDtypeStruct(amp.shape, jnp.float32),
        name="precompute",
    )(amp, exch, fock, over)


def post_kernel(
    occ_ref,
    base_ref,
    amp_ref,
    mask_i_ref,
    mask_j_ref,
    over_ref,
    trans_ref,
    tt_ref,
    energy_ref,
    *refs,
):
    coup_refs, (res_ref, new_ref) = refs[:-2], refs[-2:]
    k = pl.program_id(0)
    step, cols, w, _ = amp_ref.shape
    rows = pl.num_programs(0) * step
    over = over_ref[...]
    trans = trans_ref[...]
    tt = tt_ref[...]
    pairs = [(r, s) for r in range(step) for s in range(cols)]
    bf = lambda xs: [x.astype(jnp.bfloat16) for x in xs]

    def left(m, xs):
        return [_dot(m, x) for x in xs]

    def right(xs, m):
        return [_dot(x, m) for x in xs]

    two = []
    cm = []
    for r, s in pairs:
        row = jnp.maximum(mask_i_ref[r], mask_j_ref[s])
        two.append(row.T * row)
        coup = [c_ref[:, r, s].astype(jnp.float32).reshape(w, -1) for c_ref in coup_refs]
        cm.append(jnp.concatenate(coup, axis=1) * two[-1])
    third = right(bf(left(over, bf(cm))), over)
    res = [m * (base_ref[r, s] - t) for m, t, (r, s) in zip(two, third, pairs)]
    for x, (r, s) in zip(res, pairs):
        res_ref[r, s] = x
    q = right(bf(left(tt, bf(res))), trans)
    energy = energy_ref[...].T + energy_ref[...]
    z = [
        x / (energy - (occ_ref[k * step + r] + occ_ref[rows + s])) for x, (r, s) in zip(q, pairs)
    ]
    u = right(bf(left(trans, bf(z))), tt)
    for x, (r, s) in zip(u, pairs):
        new_ref[r, s] = (amp_ref[r, s].astype(jnp.float32) - x).astype(jnp.bfloat16)


def finish(occ, base, amp, coup, mask_i, mask_j, over, trans, energy):
    rows, cols, w, _ = amp.shape
    n, _, _, sr, sl = coup[0].shape
    step = 2
    big = pl.BlockSpec((step, cols, w, w), lambda k, *_: (k, 0, 0, 0))
    mat = pl.BlockSpec((w, w), lambda k, *_: (0, 0))
    return pl.pallas_call(
        post_kernel,
        grid_spec=pltpu.PrefetchScalarGridSpec(
            num_scalar_prefetch=1,
            grid=(rows // step,),
            in_specs=[
                big,
                big,
                pl.BlockSpec((step, 1, w), lambda k, *_: (k, 0, 0)),
                pl.BlockSpec((cols, 1, w), lambda k, *_: (0, 0, 0)),
                mat,
                mat,
                mat,
                pl.BlockSpec((1, w), lambda k, *_: (0, 0)),
            ]
            + [pl.BlockSpec((n, step, cols, sr, sl), lambda k, *_: (0, k, 0, 0, 0))] * len(coup),
            out_specs=[big, big],
        ),
        out_shape=[
            jax.ShapeDtypeStruct(amp.shape, jnp.float32),
            jax.ShapeDtypeStruct(amp.shape, jnp.bfloat16),
        ],
        name="finish",
    )(
        occ,
        base,
        amp,
        mask_i[:, None, :],
        mask_j[:, None, :],
        over,
        trans,
        trans.T,
        energy[None, :],
        *coup,
    )


def per_device(
    amplitudes,
    exchange,
    fock_virt,
    intersection,
    transform,
    virt_energy,
    occ_energy,
    partners,
    coupling,
    domain,
):
    rows, cols, width, _ = amplitudes.shape
    blocks = domain.shape[1]
    a_n = lax.axis_size("a")
    z_n = lax.axis_size("z")
    g_n = lax.axis_size("g")
    start_i = lax.axis_index("a") * rows
    start_z = lax.axis_index("z") * (g_n * cols)
    start_j = start_z + lax.axis_index("g") * cols
    plane = ("a", "g")
    n = a_n * g_n

    over = (jnp.eye(width, dtype=jnp.float32) + intersection.astype(jnp.float32)).astype(
        jnp.bfloat16
    )
    shape = (a_n, g_n, rows, cols, width // n, width // CHUNKS)
    z = lax.axis_index("z")

    def spread(x):
        return lax.all_to_all(x, plane, 0, 0, tiled=True)

    flipped = pack(amplitudes, n, True)
    own = pack(amplitudes, n, False)
    got = []
    last = None
    for h in range(CHUNKS):
        part = flipped[h]
        if h:
            part, last = lax.optimization_barrier((part, last))
        part = spread(part).reshape(shape)
        tiles = []
        for k in range(z_n):
            tile = lax.dynamic_index_in_dim(part, lax.rem(z + k, z_n), 0, keepdims=False)
            if k:
                tile = lax.ppermute(tile, "z", [(q, (q + k) % z_n) for q in range(z_n)])
            else:
                last = tile
            tiles.append(tile)
        got.append(tiles)
    up = [(k, k + 1) for k in range(z_n - 1)]
    down = [(k + 1, k) for k in range(z_n - 1)]
    base = precompute(amplitudes, exchange, fock_virt, over)
    coup = []
    for h in range(CHUNKS):
        part, last = lax.optimization_barrier((own[h], last))
        part = spread(part).reshape(shape)
        last = part
        sym, low, high = symmetrize(z, part, got[h])
        left = lax.ppermute(high, "z", up)
        right = lax.ppermute(low, "z", down)
        part = couple(partners, coupling, start_z[None], sym, left, right, rows, cols)
        coup.append(spread(part.reshape(own[h].shape)))

    masks = jnp.repeat(domain.astype(jnp.float32), width // blocks, axis=1)
    mask_i = lax.dynamic_slice_in_dim(masks, start_i, rows, 0)
    mask_j = lax.dynamic_slice_in_dim(masks, start_j, cols, 0)
    occ = jnp.concatenate(
        [
            lax.dynamic_slice_in_dim(occ_energy, start_i, rows, 0),
            lax.dynamic_slice_in_dim(occ_energy, start_j, cols, 0),
        ]
    )
    return tuple(
        finish(occ, base, amplitudes, coup, mask_i, mask_j, over, transform, virt_energy)
    )


def solution(mesh):
    i_n, j_n = mesh.shape["occi"], mesh.shape["occj"]
    group = j_n // i_n
    z_n = j_n // group
    inner = Mesh(mesh.devices.reshape(i_n, z_n, group), ("a", "z", "g"))
    pairs = P("a", ("z", "g"), None, None)
    return jax.shard_map(
        per_device,
        mesh=inner,
        in_specs=(pairs, pairs, P(), P(), P(), P(), P(), P(), P(), P()),
        out_specs=(pairs, pairs),
        check_vma=False,
    )
```

time: 220 us -> 233 us (1.059)
  blocking collectives: 92.7 us -> 20.9 us
  starting transfers between devices: 20.9 us -> 69.8 us
  waiting for transfers between devices: 44.8 us -> 85.6 us
  Pallas kernels: 47.6 us -> 41.5 us
    all_to_all x2 -> x1, blocking collectives: 92.7 us -> 20.9 us  [spread(): return lax.all_to_all(x, plane, 0, 0, tiled=True)]
    ppermute x0 -> x14, waiting for transfers between devices: none -> 41.4 us  [per_device(): tile = lax.ppermute(tile, 'z', [(q, (q + k) % z_n) for q in range(z_n)])]
    ppermute x0 -> x14, starting transfers between devices: none -> 26 us  [per_device(): tile = lax.ppermute(tile, 'z', [(q, (q + k) % z_n) for q in range(z_n)])]
    all_to_all x2 -> x5, starting transfers between devices: 18.3 us -> 36.9 us  [spread(): return lax.all_to_all(x, plane, 0, 0, tiled=True)]
    pallas_call x1, Pallas kernels: 16.9 us -> 9.31 us  [finish(): pl.pallas_call(post_kernel, grid_spec=pltpu.PrefetchScalarGridSpec(num_sc...]
    all_to_all x2 -> x5, waiting for transfers between devices: 34.8 us -> 30.6 us  [spread(): return lax.all_to_all(x, plane, 0, 0, tiled=True)]
    ppermute x1 -> x2, waiting for transfers between devices: 3.76 us -> 7.85 us  [per_device(): right = lax.ppermute(low, 'z', down)]
    ppermute x1 -> x2, starting transfers between devices: 1.31 us -> 4.33 us  [per_device(): left = lax.ppermute(high, 'z', up)]
  transfers between devices with their start and end apart: 4 -> 23, of which waited for: 4 -> 16; matrix products, arithmetic and copies ran while one was open for 4% -> 2% of each run, Pallas kernels for 6% -> 12%
where the time goes in v2:
time: 233 us; the launch traced here: 230 us
  waiting for transfers between devices  85.6 us (37%)
  starting transfers between devices  69.8 us (30%)
  Pallas kernels  41.5 us (18%)
  blocking collectives  20.9 us (9%)
  local copies, waits for them, and re-layouts  9.59 us (4%)
    ppermute x14, waiting for transfers between devices, per_device(): tile = lax.ppermute(tile, 'z', [(q, (q + k) % z_n) for q in range(z_n)])  41.4 us
    all_to_all x5, starting transfers between devices, spread(): return lax.all_to_all(x, plane, 0, 0, tiled=True)  36.9 us
    all_to_all x5, waiting for transfers between devices, spread(): return lax.all_to_all(x, plane, 0, 0, tiled=True)  30.6 us
    ppermute x14, starting transfers between devices, per_device(): tile = lax.ppermute(tile, 'z', [(q, (q + k) % z_n) for q in range(z_n)])  26 us
    all_to_all x1, blocking collectives, spread(): return lax.all_to_all(x, plane, 0, 0, tiled=True)  20.9 us
    pallas_call x2, Pallas kernels, couple(): pl.pallas_call(coup_kernel, in_specs=[SMEM, SMEM, SMEM, VMEM, VMEM, VMEM]...  9.58 us
    pallas_call x1, Pallas kernels, finish(): pl.pallas_call(post_kernel, grid_spec=pltpu.PrefetchScalarGridSpec(num_sc...  9.31 us
    pallas_call x1, Pallas kernels, precompute(): pl.pallas_call(pre_kernel, grid=(rows,), in_specs=[big, big, mat, mat], o...  8.5 us
  transfers between devices with their start and end apart: 23, of which 16 were waited for; matrix products, arithmetic and copies ran while one was open for 2% of the time, Pallas kernels for 12%

profile of v2, /device:TPU:3, one launch (start us, length us, event | category | flops | bytes accessed | tf_op | source)
XLA Modules:
  0.0 229.7 jit_solution(9145821951266940950)
XLA Ops:
  0.6 4.1 %pack_flip.1 = (bf16[32,8,2,8,128]{4,3,2,1,0:T(8,128)(2,1)}, bf16[32,8,2,8,128]{4,3,2,1,0:T(8,128)(2,1)}) custom-call(bf16[8,2,256,256]{3,2,1,0:T(8,128)(2,1)} %amp_ref.3), custom_call_target="tpu_custom_call" | custom-call | tf_op jit(solution)/shard_map/pack_flip/pallas_call | solution.py:35
  4.8 7.9 %all-to-all-start = ((bf16[32,8,2,8,128]{4,3,2,1,0:T(8,128)(2,1)}), bf16[32,8,2,8,128]{4,3,2,1,0:T(8,128)(2,1)S(1)}, u32[]{:S(2)}, u32[]{:S(2)}) async-start(bf16[32,8,2,8,128]{4,3,2,1,0:T(8,128)(2,1)} %get-tuple-element.17), calls=%async_computation | async-start | bytes 2097152 | tf_op jit(solution)/shard_map/all_to_all | solution.py:267
  12.7 15.5 %all-to-all-done = bf16[32,8,2,8,128]{4,3,2,1,0:T(8,128)(2,1)S(1)} async-done(((bf16[32,8,2,8,128]{4,3,2,1,0:T(8,128)(2,1)}), bf16[32,8,2,8,128]{4,3,2,1,0:T(8,128)(2,1)S(1)}, u32[]{:S(2)}, u32[]{:S(2)}) %all-to-all-start) | async-done | bytes 1048608 | tf_op jit(solution)/shard_map/all_to_all | solution.py:267
  28.3 1.0 dynamic-slice_bitcast_fusion.7
  29.3 5.3 %all-to-all-start.1 = ((bf16[32,8,2,8,128]{4,3,2,1,0:T(8,128)(2,1)}), bf16[32,8,2,8,128]{4,3,2,1,0:T(8,128)(2,1)S(1)}, u32[]{:S(2)}, u32[]{:S(2)}) async-start(bf16[32,8,2,8,128]{4,3,2,1,0:T(8,128)(2,1)} %get-tuple-element.18), calls=%async_computation.1 | async-start | bytes 2097152 | tf_op jit(solution)/shard_map/all_to_all | solution.py:267
  34.6 3.9 %pack.1 = (bf16[32,8,2,8,128]{4,3,2,1,0:T(8,128)(2,1)}, bf16[32,8,2,8,128]{4,3,2,1,0:T(8,128)(2,1)}) custom-call(bf16[8,2,256,256]{3,2,1,0:T(8,128)(2,1)} %amp_ref.3), custom_call_target="tpu_custom_call" | custom-call | tf_op jit(solution)/shard_map/pack/pallas_call | solution.py:35
  38.5 11.7 %all-to-all-done.1 = bf16[32,8,2,8,128]{4,3,2,1,0:T(8,128)(2,1)S(1)} async-done(((bf16[32,8,2,8,128]{4,3,2,1,0:T(8,128)(2,1)}), bf16[32,8,2,8,128]{4,3,2,1,0:T(8,128)(2,1)S(1)}, u32[]{:S(2)}, u32[]{:S(2)}) %all-to-all-start.1) | async-done | bytes 1048608 | tf_op jit(solution)/shard_map/all_to_all | solution.py:267
  50.2 1.0 dynamic-slice_bitcast_fusion
  51.1 20.9 %all_to_all.30 = bf16[32,8,2,8,128]{4,3,2,1,0:T(8,128)(2,1)} all-to-all(bf16[32,8,2,8,128]{4,3,2,1,0:T(8,128)(2,1)S(1)} %copy-done.3), channel_id=1, replica_groups=mesh['a'=8,'z'=8,'g'=4] {'a','g'}, dimensions={0} | all-to-all | bytes 2097152 | tf_op jit(solution)/shard_map/all_to_all | solution.py:267
  72.1 5.5 %all-to-all-start.4 = ((bf16[32,8,2,8,128]{4,3,2,1,0:T(8,128)(2,1)}), bf16[32,8,2,8,128]{4,3,2,1,0:T(8,128)(2,1)S(1)}, u32[]{:S(2)}, u32[]{:S(2)}) async-start(bf16[32,8,2,8,128]{4,3,2,1,0:T(8,128)(2,1)} %get-tuple-element.24), calls=%async_computation.4 | async-start | bytes 2097152 | tf_op jit(solution)/shard_map/all_to_all | solution.py:267
  77.6 5.7 %collective-permute-start.6 = (bf16[4,8,2,8,128]{4,3,2,1,0:T(8,128)(2,1)S(1)}, bf16[4,8,2,8,128]{4,3,2,1,0:T(8,128)(2,1)S(1)}, u32[]{:S(2)}, u32[]{:S(2)}) collective-permute-start(bf16[4,8,2,8,128]{4,3,2,1,0:T(8,128)(2,1)S(1)} %copy-done.11), channel_id=1, source_target_pairs={{0,28},{4,0},{8,4},{12,8},{16,12},{20,16},{24,20},{28,24},{1,29},{... | collective-permute-start | bytes 393224 | tf_op jit(solution)/shard_map/ppermute | solution.py:282
  83.2 1.2 collective-permute-start.5
  84.4 0.5 collective-permute-start.4
  84.9 4.4 %collective-permute-start.3 = (bf16[4,8,2,8,128]{4,3,2,1,0:T(8,128)(2,1)S(1)}, bf16[4,8,2,8,128]{4,3,2,1,0:T(8,128)(2,1)S(1)}, u32[]{:S(2)}, u32[]{:S(2)}) collective-permute-start(bf16[4,8,2,8,128]{4,3,2,1,0:T(8,128)(2,1)S(1)} %get-tuple-element.39), channel_id=1, source_target_pairs={{0,16},{4,20},{8,24},{12,28},{16,0},{20,4},{24,8},{28,12},{1,17},{... | collective-permute-start | bytes 393224 | tf_op jit(solution)/shard_map/ppermute | solution.py:282
  89.3 2.2 collective-permute-start.1
  91.5 2.3 %collective-permute-done.5.refs_6_ = bf16[4,8,2,8,128]{4,3,2,1,0:T(8,128)(2,1)S(1)} collective-permute-done((bf16[4,8,2,8,128]{4,3,2,1,0:T(8,128)(2,1)S(1)}, bf16[4,8,2,8,128]{4,3,2,1,0:T(8,128)(2,1)S(1)}, u32[]{:S(2)}, u32[]{:S(2)}) %collective-permute-start.5) | collective-permute-done | bytes 131104 | tf_op jit(solution)/shard_map/ppermute | solution.py:282
  93.8 2.9 %collective-permute-done.4.refs_5_ = bf16[4,8,2,8,128]{4,3,2,1,0:T(8,128)(2,1)S(1)} collective-permute-done((bf16[4,8,2,8,128]{4,3,2,1,0:T(8,128)(2,1)S(1)}, bf16[4,8,2,8,128]{4,3,2,1,0:T(8,128)(2,1)S(1)}, u32[]{:S(2)}, u32[]{:S(2)}) %collective-permute-start.4) | collective-permute-done | bytes 131104 | tf_op jit(solution)/shard_map/ppermute | solution.py:282
  96.7 2.7 %collective-permute-done.3.refs_4_ = bf16[4,8,2,8,128]{4,3,2,1,0:T(8,128)(2,1)S(1)} collective-permute-done((bf16[4,8,2,8,128]{4,3,2,1,0:T(8,128)(2,1)S(1)}, bf16[4,8,2,8,128]{4,3,2,1,0:T(8,128)(2,1)S(1)}, u32[]{:S(2)}, u32[]{:S(2)}) %collective-permute-start.3) | collective-permute-done | bytes 131104 | tf_op jit(solution)/shard_map/ppermute | solution.py:282
  99.4 9.4 %collective-permute-done.1.refs_2_ = bf16[4,8,2,8,128]{4,3,2,1,0:T(8,128)(2,1)S(1)} collective-permute-done((bf16[4,8,2,8,128]{4,3,2,1,0:T(8,128)(2,1)S(1)}, bf16[4,8,2,8,128]{4,3,2,1,0:T(8,128)(2,1)S(1)}, u32[]{:S(2)}, u32[]{:S(2)}) %collective-permute-start.1) | collective-permute-done | bytes 131104 | tf_op jit(solution)/shard_map/ppermute | solution.py:282
  108.8 4.5 %collective-permute-done.refs_1_ = bf16[4,8,2,8,128]{4,3,2,1,0:T(8,128)(2,1)S(1)} collective-permute-done((bf16[4,8,2,8,128]{4,3,2,1,0:T(8,128)(2,1)S(1)}, bf16[4,8,2,8,128]{4,3,2,1,0:T(8,128)(2,1)S(1)}, u32[]{:S(2)}, u32[]{:S(2)}) %collective-permute-start) | collective-permute-done | bytes 131104 | tf_op jit(solution)/shard_map/ppermute | solution.py:282
  113.3 0.6 copy-done.25
  113.9 3.1 %sym.2 = (bf16[8,64,8,128]{3,2,1,0:T(8,128)(2,1)}, bf16[2,64,8,128]{3,2,1,0:T(8,128)(2,1)}, bf16[2,64,8,128]{3,2,1,0:T(8,128)(2,1)}) custom-call(s32[1]{0:T(128)} %bitcast.6.z_ref, bf16[8,4,8,2,8,128]{5,4,3,2,1,0:T(8,128)(2,1)} %bitcast.48, bf16[4,8,2,8,128]{4,3,2,1,0:T(8,128)(2,1)} %get-tuple-element.43.refs_0_, bf16[4,8,2,8,128]{4,3,2,1,0:T(8,128)(2,1)} %copy-done.25, ...), custom_call_target="tpu_custom_call" | custom-call | tf_op jit(solution)/shard_map/sym/pallas_call | solution.py:66
  116.9 2.7 %collective-permute-start.7 = (bf16[2,64,8,128]{3,2,1,0:T(8,128)(2,1)}, bf16[2,64,8,128]{3,2,1,0:T(8,128)(2,1)S(1)}, u32[]{:S(2)}, u32[]{:S(2)}) collective-permute-start(bf16[2,64,8,128]{3,2,1,0:T(8,128)(2,1)} %get-tuple-element.21), channel_id=1, source_target_pairs={{0,4},{4,8},{8,12},{12,16},{16,20},{20,24},{24,28},{1,5},{5,9},{9,... | collective-permute-start | bytes 786440 | tf_op jit(solution)/shard_map/ppermute | solution.py:296
  119.6 1.3 collective-permute-start.8
  121.0 0.7 copy.21.lists_ref
  121.7 0.7 copy.22.weights_ref
  122.4 2.3 collective-permute-done.7.left_ref
  124.7 4.0 %collective-permute-done.8.right_ref = bf16[2,64,8,128]{3,2,1,0:T(8,128)(2,1)S(1)} collective-permute-done((bf16[2,64,8,128]{3,2,1,0:T(8,128)(2,1)}, bf16[2,64,8,128]{3,2,1,0:T(8,128)(2,1)S(1)}, u32[]{:S(2)}, u32[]{:S(2)}) %collective-permute-start.8) | collective-permute-done | bytes 262176 | tf_op jit(solution)/shard_map/ppermute | solution.py:297
  128.6 0.7 copy-done.7
  129.4 4.8 %couple.2 = bf16[8,4,8,2,8,128]{5,4,3,2,1,0:T(8,128)(2,1)} custom-call(s32[64,2]{1,0:T(8,128)} %copy.21.lists_ref, f32[64,2]{1,0:T(8,128)} %copy.22.weights_ref, s32[1]{0:T(128)} %bitcast.5.start_ref, bf16[8,64,8,128]{3,2,1,0:T(8,128)(2,1)} %get-tuple-element.20.sym_ref, bf16[2,64,8,128]{3,2,1,0:T(8,128)(2,1)} %copy-done.5, bf16[2,64,8,128]{3,2,1,0:T(8,128)(2,1)} %copy-done.7), custom_call_target="tpu_custom_call" | custom-call | tf_op jit(solution)/shard_map/couple/pallas_call | solution.py:107
  134.2 8.9 %all-to-all-start.3 = ((bf16[32,8,2,8,128]{4,3,2,1,0:T(8,128)(2,1)}), bf16[32,8,2,8,128]{4,3,2,1,0:T(8,128)(2,1)S(1)}, u32[]{:S(2)}, u32[]{:S(2)}) async-start(bf16[32,8,2,8,128]{4,3,2,1,0:T(8,128)(2,1)} %bitcast.50), calls=%async_computation.3 | async-start | bytes 2097152 | tf_op jit(solution)/shard_map/all_to_all | solution.py:267
  143.1 0.1 collective-permute-start.15
  143.2 1.4 collective-permute-start.14
  144.6 3.9 %collective-permute-start.13 = (bf16[4,8,2,8,128]{4,3,2,1,0:T(8,128)(2,1)S(1)}, bf16[4,8,2,8,128]{4,3,2,1,0:T(8,128)(2,1)S(1)}, u32[]{:S(2)}, u32[]{:S(2)}) collective-permute-start(bf16[4,8,2,8,128]{4,3,2,1,0:T(8,128)(2,1)S(1)} %get-tuple-element.30), channel_id=1, source_target_pairs={{0,20},{4,24},{8,28},{12,0},{16,4},{20,8},{24,12},{28,16},{1,21},{... | collective-permute-start | bytes 393224 | tf_op jit(solution)/shard_map/ppermute | solution.py:282
  148.5 1.7 collective-permute-start.12
  150.2 2.2 collective-permute-start.11
  152.4 2.9 %collective-permute-start.10 = (bf16[4,8,2,8,128]{4,3,2,1,0:T(8,128)(2,1)S(1)}, bf16[4,8,2,8,128]{4,3,2,1,0:T(8,128)(2,1)S(1)}, u32[]{:S(2)}, u32[]{:S(2)}) collective-permute-start(bf16[4,8,2,8,128]{4,3,2,1,0:T(8,128)(2,1)S(1)} %get-tuple-element.33), channel_id=1, source_target_pairs={{0,8},{4,12},{8,16},{12,20},{16,24},{20,28},{24,0},{28,4},{1,9},{5... | collective-permute-start | bytes 393224 | tf_op jit(solution)/shard_map/ppermute | solution.py:282
  155.3 1.8 collective-permute-done.14.refs_6_
  157.0 4.1 %collective-permute-done.12.refs_4_ = bf16[4,8,2,8,128]{4,3,2,1,0:T(8,128)(2,1)S(1)} collective-permute-done((bf16[4,8,2,8,128]{4,3,2,1,0:T(8,128)(2,1)S(1)}, bf16[4,8,2,8,128]{4,3,2,1,0:T(8,128)(2,1)S(1)}, u32[]{:S(2)}, u32[]{:S(2)}) %collective-permute-start.12) | collective-permute-done | bytes 131104 | tf_op jit(solution)/shard_map/ppermute | solution.py:282
  161.1 8.8 %collective-permute-done.11.refs_3_ = bf16[4,8,2,8,128]{4,3,2,1,0:T(8,128)(2,1)S(1)} collective-permute-done((bf16[4,8,2,8,128]{4,3,2,1,0:T(8,128)(2,1)S(1)}, bf16[4,8,2,8,128]{4,3,2,1,0:T(8,128)(2,1)S(1)}, u32[]{:S(2)}, u32[]{:S(2)}) %collective-permute-start.11) | collective-permute-done | bytes 131104 | tf_op jit(solution)/shard_map/ppermute | solution.py:282
  169.9 0.0 collective-permute-done.10.refs_2_
  169.9 5.0 %collective-permute-done.9.refs_1_ = bf16[4,8,2,8,128]{4,3,2,1,0:T(8,128)(2,1)S(1)} collective-permute-done((bf16[4,8,2,8,128]{4,3,2,1,0:T(8,128)(2,1)S(1)}, bf16[4,8,2,8,128]{4,3,2,1,0:T(8,128)(2,1)S(1)}, u32[]{:S(2)}, u32[]{:S(2)}) %collective-permute-start.9) | collective-permute-done | bytes 131104 | tf_op jit(solution)/shard_map/ppermute | solution.py:282
  175.0 0.6 copy-done.24
  175.6 3.1 %sym.3 = (bf16[8,64,8,128]{3,2,1,0:T(8,128)(2,1)}, bf16[2,64,8,128]{3,2,1,0:T(8,128)(2,1)}, bf16[2,64,8,128]{3,2,1,0:T(8,128)(2,1)}) custom-call(s32[1]{0:T(128)} %bitcast.6.z_ref, bf16[8,4,8,2,8,128]{5,4,3,2,1,0:T(8,128)(2,1)} %bitcast.47, bf16[4,8,2,8,128]{4,3,2,1,0:T(8,128)(2,1)} %get-tuple-element.35.refs_0_, bf16[4,8,2,8,128]{4,3,2,1,0:T(8,128)(2,1)} %copy-done.24, ...), custom_call_target="tpu_custom_call" | custom-call | tf_op jit(solution)/shard_map/sym/pallas_call | solution.py:66
  178.7 1.6 collective-permute-start.16
  180.3 1.3 collective-permute-start.17
  181.6 3.6 %collective-permute-done.16.left_ref = bf16[2,64,8,128]{3,2,1,0:T(8,128)(2,1)S(1)} collective-permute-done((bf16[2,64,8,128]{3,2,1,0:T(8,128)(2,1)}, bf16[2,64,8,128]{3,2,1,0:T(8,128)(2,1)S(1)}, u32[]{:S(2)}, u32[]{:S(2)}) %collective-permute-start.16) | collective-permute-done | bytes 262176 | tf_op jit(solution)/shard_map/ppermute | solution.py:296
  185.2 3.9 %collective-permute-done.17.right_ref = bf16[2,64,8,128]{3,2,1,0:T(8,128)(2,1)S(1)} collective-permute-done((bf16[2,64,8,128]{3,2,1,0:T(8,128)(2,1)}, bf16[2,64,8,128]{3,2,1,0:T(8,128)(2,1)S(1)}, u32[]{:S(2)}, u32[]{:S(2)}) %collective-permute-start.17) | collective-permute-done | bytes 262176 | tf_op jit(solution)/shard_map/ppermute | solution.py:297
  189.0 0.7 copy-done.8
  189.8 4.8 %couple.3 = bf16[8,4,8,2,8,128]{5,4,3,2,1,0:T(8,128)(2,1)} custom-call(s32[64,2]{1,0:T(8,128)} %copy.21.lists_ref, f32[64,2]{1,0:T(8,128)} %copy.22.weights_ref, s32[1]{0:T(128)} %bitcast.5.start_ref, bf16[8,64,8,128]{3,2,1,0:T(8,128)(2,1)} %get-tuple-element.25.sym_ref, bf16[2,64,8,128]{3,2,1,0:T(8,128)(2,1)} %copy-done.6, bf16[2,64,8,128]{3,2,1,0:T(8,128)(2,1)} %copy-done.8), custom_call_target="tpu_custom_call" | custom-call | tf_op jit(solution)/shard_map/couple/pallas_call | solution.py:107
  194.6 9.3 %all-to-all-start.5 = ((bf16[32,8,2,8,128]{4,3,2,1,0:T(8,128)(2,1)}), bf16[32,8,2,8,128]{4,3,2,1,0:T(8,128)(2,1)S(1)}, u32[]{:S(2)}, u32[]{:S(2)}) async-start(bf16[32,8,2,8,128]{4,3,2,1,0:T(8,128)(2,1)} %bitcast.51), calls=%async_computation.5 | async-start | bytes 2097152 | tf_op jit(solution)/shard_map/all_to_all | solution.py:267
  203.9 0.1 dynamic_slice.62
  203.9 0.1 dynamic_slice.61
  204.0 0.1 dynamic-slice_bitcast_fusion.16
  204.1 0.7 copy.26.mask_j_ref
  204.8 0.1 dynamic-slice_bitcast_fusion.17
  204.9 0.7 copy.25.mask_i_ref
  205.5 0.8 copy.20
  206.3 0.7 add_convert_fusion.over_ref
  207.0 8.5 %precompute.1.base_ref = f32[8,2,256,256]{3,2,1,0:T(8,128)} custom-call(bf16[8,2,256,256]{3,2,1,0:T(8,128)(2,1)} %amp_ref.3, bf16[8,2,256,256]{3,2,1,0:T(8,128)(2,1)} %exch_ref.1, bf16[256,256]{1,0:T(8,128)(2,1)} %fock_ref.1, bf16[256,256]{1,0:T(8,128)(2,1)} %add_convert_fusion.over_ref), custom_call_target="tpu_custom_call" | custom-call | tf_op jit(solution)/shard_map/precompute/pallas_call | solution.py:135
  215.5 0.6 pad_maximum_fusion.occ_ref
  216.1 3.3 %all-to-all-done.5.refs_1_ = bf16[32,8,2,8,128]{4,3,2,1,0:T(8,128)(2,1)S(1)} async-done(((bf16[32,8,2,8,128]{4,3,2,1,0:T(8,128)(2,1)}), bf16[32,8,2,8,128]{4,3,2,1,0:T(8,128)(2,1)S(1)}, u32[]{:S(2)}, u32[]{:S(2)}) %all-to-all-start.5) | async-done | bytes 1048608 | tf_op jit(solution)/shard_map/all_to_all | solution.py:267
  219.4 1.0 copy-done.1
  220.4 9.3 %finish.1 = (f32[8,2,256,256]{3,2,1,0:T(8,128)}, bf16[8,2,256,256]{3,2,1,0:T(8,128)(2,1)}) custom-call(f32[10]{0:T(128)} %pad_maximum_fusion.occ_ref, f32[8,2,256,256]{3,2,1,0:T(8,128)} %precompute.1.base_ref, bf16[8,2,256,256]{3,2,1,0:T(8,128)(2,1)} %amp_ref.3, f32[8,1,256]{2,1,0:T(1,128)} %copy.25.mask_i_ref, f32[2,1,256]{2,1,0:T(1,128)} %copy.26.mask_j_ref, ...), custom_call_target="tpu_custom_call" | custom-call | tf_op jit(solution)/shard_map/finish/pallas_call | solution.py:200
  (68 shorter events, 0.1 us)
Async XLA Ops:
  4.8 23.5 %all-to-all-start = ((bf16[32,8,2,8,128]{4,3,2,1,0:T(8,128)(2,1)}), bf16[32,8,2,8,128]{4,3,2,1,0:T(8,128)(2,1)S(1)}, u32[]{:S(2)}, u32[]{:S(2)}) async-start(bf16[32,8,2,8,128]{4,3,2,1,0:T(8,128)(2,1)} %get-tuple-element.17), calls=%async_computation | async-start | bytes 2097152 | tf_op jit(solution)/shard_map/all_to_all | solution.py:267
  29.3 20.9 %all-to-all-start.1 = ((bf16[32,8,2,8,128]{4,3,2,1,0:T(8,128)(2,1)}), bf16[32,8,2,8,128]{4,3,2,1,0:T(8,128)(2,1)S(1)}, u32[]{:S(2)}, u32[]{:S(2)}) async-start(bf16[32,8,2,8,128]{4,3,2,1,0:T(8,128)(2,1)} %get-tuple-element.18), calls=%async_computation.1 | async-start | bytes 2097152 | tf_op jit(solution)/shard_map/all_to_all | solution.py:267
  38.5 12.7 %copy-start.3 = (bf16[32,8,2,8,128]{4,3,2,1,0:T(8,128)(2,1)S(1)}, bf16[32,8,2,8,128]{4,3,2,1,0:T(8,128)(2,1)}, u32[]{:S(2)}) copy-start(bf16[32,8,2,8,128]{4,3,2,1,0:T(8,128)(2,1)} %get-tuple-element.19) | copy-start | bytes 3145732
  51.1 26.4 %copy-start.11 = (bf16[4,8,2,8,128]{4,3,2,1,0:T(8,128)(2,1)S(1)}, bf16[4,8,2,8,128]{4,3,2,1,0:T(8,128)(2,1)}, u32[]{:S(2)}) copy-start(bf16[4,8,2,8,128]{4,3,2,1,0:T(8,128)(2,1)} %get-tuple-element.36) | copy-start | bytes 393220
  51.1 32.1 %copy-start.10 = (bf16[4,8,2,8,128]{4,3,2,1,0:T(8,128)(2,1)S(1)}, bf16[4,8,2,8,128]{4,3,2,1,0:T(8,128)(2,1)}, u32[]{:S(2)}) copy-start(bf16[4,8,2,8,128]{4,3,2,1,0:T(8,128)(2,1)} %get-tuple-element.37) | copy-start | bytes 393220
  51.1 33.2 %copy-start.9 = (bf16[4,8,2,8,128]{4,3,2,1,0:T(8,128)(2,1)S(1)}, bf16[4,8,2,8,128]{4,3,2,1,0:T(8,128)(2,1)}, u32[]{:S(2)}) copy-start(bf16[4,8,2,8,128]{4,3,2,1,0:T(8,128)(2,1)} %get-tuple-element.38) | copy-start | bytes 393220
  72.1 48.9 %copy-start.28 = (s32[64,2]{0,1:T(2,128)S(1)}, s32[64,2]{0,1:T(2,128)}, u32[]{:S(2)}) copy-start(s32[64,2]{0,1:T(2,128)} %param.17) | copy-start | bytes 1540
  72.1 49.6 %copy-start.29 = (f32[64,2]{0,1:T(2,128)S(1)}, f32[64,2]{0,1:T(2,128)}, u32[]{:S(2)}) copy-start(f32[64,2]{0,1:T(2,128)} %param.18) | copy-start | bytes 1540
  72.1 62.1 %all-to-all-start.4 = ((bf16[32,8,2,8,128]{4,3,2,1,0:T(8,128)(2,1)}), bf16[32,8,2,8,128]{4,3,2,1,0:T(8,128)(2,1)S(1)}, u32[]{:S(2)}, u32[]{:S(2)}) async-start(bf16[32,8,2,8,128]{4,3,2,1,0:T(8,128)(2,1)} %get-tuple-element.24), calls=%async_computation.4 | async-start | bytes 2097152 | tf_op jit(solution)/shard_map/all_to_all | solution.py:267
  77.6 11.8 %collective-permute-start.6 = (bf16[4,8,2,8,128]{4,3,2,1,0:T(8,128)(2,1)S(1)}, bf16[4,8,2,8,128]{4,3,2,1,0:T(8,128)(2,1)S(1)}, u32[]{:S(2)}, u32[]{:S(2)}) collective-permute-start(bf16[4,8,2,8,128]{4,3,2,1,0:T(8,128)(2,1)S(1)} %copy-done.11), channel_id=1, source_target_pairs={{0,28},{4,0},{8,4},{12,8},{16,12},{20,16},{24,20},{28,24},{1,29},{... | collective-permute-start | bytes 393224 | tf_op jit(solution)/shard_map/ppermute | solution.py:282
  83.2 10.6 %collective-permute-start.5 = (bf16[4,8,2,8,128]{4,3,2,1,0:T(8,128)(2,1)S(1)}, bf16[4,8,2,8,128]{4,3,2,1,0:T(8,128)(2,1)S(1)}, u32[]{:S(2)}, u32[]{:S(2)}) collective-permute-start(bf16[4,8,2,8,128]{4,3,2,1,0:T(8,128)(2,1)S(1)} %copy-done.10), channel_id=1, source_target_pairs={{0,24},{4,28},{8,0},{12,4},{16,8},{20,12},{24,16},{28,20},{1,25},{... | collective-permute-start | bytes 393224 | tf_op jit(solution)/shard_map/ppermute | solution.py:282
  84.4 12.3 %collective-permute-start.4 = (bf16[4,8,2,8,128]{4,3,2,1,0:T(8,128)(2,1)S(1)}, bf16[4,8,2,8,128]{4,3,2,1,0:T(8,128)(2,1)S(1)}, u32[]{:S(2)}, u32[]{:S(2)}) collective-permute-start(bf16[4,8,2,8,128]{4,3,2,1,0:T(8,128)(2,1)S(1)} %copy-done.9), channel_id=1, source_target_pairs={{0,20},{4,24},{8,28},{12,0},{16,4},{20,8},{24,12},{28,16},{1,21},{... | collective-permute-start | bytes 393224 | tf_op jit(solution)/shard_map/ppermute | solution.py:282
  84.9 14.5 %collective-permute-start.3 = (bf16[4,8,2,8,128]{4,3,2,1,0:T(8,128)(2,1)S(1)}, bf16[4,8,2,8,128]{4,3,2,1,0:T(8,128)(2,1)S(1)}, u32[]{:S(2)}, u32[]{:S(2)}) collective-permute-start(bf16[4,8,2,8,128]{4,3,2,1,0:T(8,128)(2,1)S(1)} %get-tuple-element.39), channel_id=1, source_target_pairs={{0,16},{4,20},{8,24},{12,28},{16,0},{20,4},{24,8},{28,12},{1,17},{... | collective-permute-start | bytes 393224 | tf_op jit(solution)/shard_map/ppermute | solution.py:282
  89.3 10.1 %collective-permute-start.2 = (bf16[4,8,2,8,128]{4,3,2,1,0:T(8,128)(2,1)S(1)}, bf16[4,8,2,8,128]{4,3,2,1,0:T(8,128)(2,1)S(1)}, u32[]{:S(2)}, u32[]{:S(2)}) collective-permute-start(bf16[4,8,2,8,128]{4,3,2,1,0:T(8,128)(2,1)S(1)} %get-tuple-element.40), channel_id=1, source_target_pairs={{0,12},{4,16},{8,20},{12,24},{16,28},{20,0},{24,4},{28,8},{1,13},{... | collective-permute-start | bytes 393224 | tf_op jit(solution)/shard_map/ppermute | solution.py:282
  89.3 23.9 %copy-start.13 = (bf16[4,8,2,8,128]{4,3,2,1,0:T(8,128)(2,1)}, bf16[4,8,2,8,128]{4,3,2,1,0:T(8,128)(2,1)S(1)}, u32[]{:S(2)}) copy-start(bf16[4,8,2,8,128]{4,3,2,1,0:T(8,128)(2,1)S(1)} %collective-permute-done.6.refs_7_) | copy-start | bytes 393220
  89.3 19.4 %collective-permute-start.1 = (bf16[4,8,2,8,128]{4,3,2,1,0:T(8,128)(2,1)S(1)}, bf16[4,8,2,8,128]{4,3,2,1,0:T(8,128)(2,1)S(1)}, u32[]{:S(2)}, u32[]{:S(2)}) collective-permute-start(bf16[4,8,2,8,128]{4,3,2,1,0:T(8,128)(2,1)S(1)} %get-tuple-element.41), channel_id=1, source_target_pairs={{0,8},{4,12},{8,16},{12,20},{16,24},{20,28},{24,0},{28,4},{1,9},{5... | collective-permute-start | bytes 393224 | tf_op jit(solution)/shard_map/ppermute | solution.py:282
  93.8 19.4 %copy-start.15 = (bf16[4,8,2,8,128]{4,3,2,1,0:T(8,128)(2,1)}, bf16[4,8,2,8,128]{4,3,2,1,0:T(8,128)(2,1)S(1)}, u32[]{:S(2)}) copy-start(bf16[4,8,2,8,128]{4,3,2,1,0:T(8,128)(2,1)S(1)} %collective-permute-done.5.refs_6_) | copy-start | bytes 393220
  93.8 19.4 %collective-permute-start = (bf16[4,8,2,8,128]{4,3,2,1,0:T(8,128)(2,1)S(1)}, bf16[4,8,2,8,128]{4,3,2,1,0:T(8,128)(2,1)S(1)}, u32[]{:S(2)}, u32[]{:S(2)}) collective-permute-start(bf16[4,8,2,8,128]{4,3,2,1,0:T(8,128)(2,1)S(1)} %get-tuple-element.42), channel_id=1, source_target_pairs={{0,4},{4,8},{8,12},{12,16},{16,20},{20,24},{24,28},{28,0},{1,5},{5... | collective-permute-start | bytes 393224 | tf_op jit(solution)/shard_map/ppermute | solution.py:282
  96.7 16.5 %copy-start.17 = (bf16[4,8,2,8,128]{4,3,2,1,0:T(8,128)(2,1)}, bf16[4,8,2,8,128]{4,3,2,1,0:T(8,128)(2,1)S(1)}, u32[]{:S(2)}) copy-start(bf16[4,8,2,8,128]{4,3,2,1,0:T(8,128)(2,1)S(1)} %collective-permute-done.4.refs_5_) | copy-start | bytes 393220
  99.4 13.8 %copy-start.19 = (bf16[4,8,2,8,128]{4,3,2,1,0:T(8,128)(2,1)}, bf16[4,8,2,8,128]{4,3,2,1,0:T(8,128)(2,1)S(1)}, u32[]{:S(2)}) copy-start(bf16[4,8,2,8,128]{4,3,2,1,0:T(8,128)(2,1)S(1)} %collective-permute-done.3.refs_4_) | copy-start | bytes 393220
  99.4 13.8 %copy-start.21 = (bf16[4,8,2,8,128]{4,3,2,1,0:T(8,128)(2,1)}, bf16[4,8,2,8,128]{4,3,2,1,0:T(8,128)(2,1)S(1)}, u32[]{:S(2)}) copy-start(bf16[4,8,2,8,128]{4,3,2,1,0:T(8,128)(2,1)S(1)} %collective-permute-done.2.refs_3_) | copy-start | bytes 393220
  108.8 4.5 %copy-start.23 = (bf16[4,8,2,8,128]{4,3,2,1,0:T(8,128)(2,1)}, bf16[4,8,2,8,128]{4,3,2,1,0:T(8,128)(2,1)S(1)}, u32[]{:S(2)}) copy-start(bf16[4,8,2,8,128]{4,3,2,1,0:T(8,128)(2,1)S(1)} %collective-permute-done.1.refs_2_) | copy-start | bytes 393220
  113.2 0.6 copy-start.25
  116.9 7.7 %collective-permute-start.7 = (bf16[2,64,8,128]{3,2,1,0:T(8,128)(2,1)}, bf16[2,64,8,128]{3,2,1,0:T(8,128)(2,1)S(1)}, u32[]{:S(2)}, u32[]{:S(2)}) collective-permute-start(bf16[2,64,8,128]{3,2,1,0:T(8,128)(2,1)} %get-tuple-element.21), channel_id=1, source_target_pairs={{0,4},{4,8},{8,12},{12,16},{16,20},{20,24},{24,28},{1,5},{5,9},{9,... | collective-permute-start | bytes 786440 | tf_op jit(solution)/shard_map/ppermute | solution.py:296
  119.6 9.0 %collective-permute-start.8 = (bf16[2,64,8,128]{3,2,1,0:T(8,128)(2,1)}, bf16[2,64,8,128]{3,2,1,0:T(8,128)(2,1)S(1)}, u32[]{:S(2)}, u32[]{:S(2)}) collective-permute-start(bf16[2,64,8,128]{3,2,1,0:T(8,128)(2,1)} %get-tuple-element.22), channel_id=1, source_target_pairs={{4,0},{8,4},{12,8},{16,12},{20,16},{24,20},{28,24},{5,1},{9,5},{13... | collective-permute-start | bytes 786440 | tf_op jit(solution)/shard_map/ppermute | solution.py:297
  124.7 4.0 %copy-start.5 = (bf16[2,64,8,128]{3,2,1,0:T(8,128)(2,1)}, bf16[2,64,8,128]{3,2,1,0:T(8,128)(2,1)S(1)}, u32[]{:S(2)}) copy-start(bf16[2,64,8,128]{3,2,1,0:T(8,128)(2,1)S(1)} %collective-permute-done.7.left_ref) | copy-start | bytes 786436
  128.6 0.7 copy-start.7
  134.2 40.8 %copy-start.2 = (bf16[32,8,2,8,128]{4,3,2,1,0:T(8,128)(2,1)}, bf16[32,8,2,8,128]{4,3,2,1,0:T(8,128)(2,1)S(1)}, u32[]{:S(2)}) copy-start(bf16[32,8,2,8,128]{4,3,2,1,0:T(8,128)(2,1)S(1)} %all-to-all-done.4) | copy-start | bytes 3145732
  134.2 60.3 %all-to-all-start.3 = ((bf16[32,8,2,8,128]{4,3,2,1,0:T(8,128)(2,1)}), bf16[32,8,2,8,128]{4,3,2,1,0:T(8,128)(2,1)S(1)}, u32[]{:S(2)}, u32[]{:S(2)}) async-start(bf16[32,8,2,8,128]{4,3,2,1,0:T(8,128)(2,1)} %bitcast.50), calls=%async_computation.3 | async-start | bytes 2097152 | tf_op jit(solution)/shard_map/all_to_all | solution.py:267
  143.1 9.3 %collective-permute-start.15 = (bf16[4,8,2,8,128]{4,3,2,1,0:T(8,128)(2,1)S(1)}, bf16[4,8,2,8,128]{4,3,2,1,0:T(8,128)(2,1)S(1)}, u32[]{:S(2)}, u32[]{:S(2)}) collective-permute-start(bf16[4,8,2,8,128]{4,3,2,1,0:T(8,128)(2,1)S(1)} %get-tuple-element.28), channel_id=1, source_target_pairs={{0,28},{4,0},{8,4},{12,8},{16,12},{20,16},{24,20},{28,24},{1,29},{... | collective-permute-start | bytes 393224 | tf_op jit(solution)/shard_map/ppermute | solution.py:282
  143.2 13.8 %collective-permute-start.14 = (bf16[4,8,2,8,128]{4,3,2,1,0:T(8,128)(2,1)S(1)}, bf16[4,8,2,8,128]{4,3,2,1,0:T(8,128)(2,1)S(1)}, u32[]{:S(2)}, u32[]{:S(2)}) collective-permute-start(bf16[4,8,2,8,128]{4,3,2,1,0:T(8,128)(2,1)S(1)} %get-tuple-element.29), channel_id=1, source_target_pairs={{0,24},{4,28},{8,0},{12,4},{16,8},{20,12},{24,16},{28,20},{1,25},{... | collective-permute-start | bytes 393224 | tf_op jit(solution)/shard_map/ppermute | solution.py:282
  144.6 12.4 %collective-permute-start.13 = (bf16[4,8,2,8,128]{4,3,2,1,0:T(8,128)(2,1)S(1)}, bf16[4,8,2,8,128]{4,3,2,1,0:T(8,128)(2,1)S(1)}, u32[]{:S(2)}, u32[]{:S(2)}) collective-permute-start(bf16[4,8,2,8,128]{4,3,2,1,0:T(8,128)(2,1)S(1)} %get-tuple-element.30), channel_id=1, source_target_pairs={{0,20},{4,24},{8,28},{12,0},{16,4},{20,8},{24,12},{28,16},{1,21},{... | collective-permute-start | bytes 393224 | tf_op jit(solution)/shard_map/ppermute | solution.py:282
  148.5 12.6 %collective-permute-start.12 = (bf16[4,8,2,8,128]{4,3,2,1,0:T(8,128)(2,1)S(1)}, bf16[4,8,2,8,128]{4,3,2,1,0:T(8,128)(2,1)S(1)}, u32[]{:S(2)}, u32[]{:S(2)}) collective-permute-start(bf16[4,8,2,8,128]{4,3,2,1,0:T(8,128)(2,1)S(1)} %get-tuple-element.31), channel_id=1, source_target_pairs={{0,16},{4,20},{8,24},{12,28},{16,0},{20,4},{24,8},{28,12},{1,17},{... | collective-permute-start | bytes 393224 | tf_op jit(solution)/shard_map/ppermute | solution.py:282
  150.2 19.7 %collective-permute-start.11 = (bf16[4,8,2,8,128]{4,3,2,1,0:T(8,128)(2,1)S(1)}, bf16[4,8,2,8,128]{4,3,2,1,0:T(8,128)(2,1)S(1)}, u32[]{:S(2)}, u32[]{:S(2)}) collective-permute-start(bf16[4,8,2,8,128]{4,3,2,1,0:T(8,128)(2,1)S(1)} %get-tuple-element.32), channel_id=1, source_target_pairs={{0,12},{4,16},{8,20},{12,24},{16,28},{20,0},{24,4},{28,8},{1,13},{... | collective-permute-start | bytes 393224 | tf_op jit(solution)/shard_map/ppermute | solution.py:282
  152.4 22.6 %copy-start.12 = (bf16[4,8,2,8,128]{4,3,2,1,0:T(8,128)(2,1)}, bf16[4,8,2,8,128]{4,3,2,1,0:T(8,128)(2,1)S(1)}, u32[]{:S(2)}) copy-start(bf16[4,8,2,8,128]{4,3,2,1,0:T(8,128)(2,1)S(1)} %collective-permute-done.15.refs_7_) | copy-start | bytes 393220
  152.4 17.5 %collective-permute-start.10 = (bf16[4,8,2,8,128]{4,3,2,1,0:T(8,128)(2,1)S(1)}, bf16[4,8,2,8,128]{4,3,2,1,0:T(8,128)(2,1)S(1)}, u32[]{:S(2)}, u32[]{:S(2)}) collective-permute-start(bf16[4,8,2,8,128]{4,3,2,1,0:T(8,128)(2,1)S(1)} %get-tuple-element.33), channel_id=1, source_target_pairs={{0,8},{4,12},{8,16},{12,20},{16,24},{20,28},{24,0},{28,4},{1,9},{5... | collective-permute-start | bytes 393224 | tf_op jit(solution)/shard_map/ppermute | solution.py:282
  157.0 18.0 %copy-start.14 = (bf16[4,8,2,8,128]{4,3,2,1,0:T(8,128)(2,1)}, bf16[4,8,2,8,128]{4,3,2,1,0:T(8,128)(2,1)S(1)}, u32[]{:S(2)}) copy-start(bf16[4,8,2,8,128]{4,3,2,1,0:T(8,128)(2,1)S(1)} %collective-permute-done.14.refs_6_) | copy-start | bytes 393220
  157.0 17.9 %collective-permute-start.9 = (bf16[4,8,2,8,128]{4,3,2,1,0:T(8,128)(2,1)S(1)}, bf16[4,8,2,8,128]{4,3,2,1,0:T(8,128)(2,1)S(1)}, u32[]{:S(2)}, u32[]{:S(2)}) collective-permute-start(bf16[4,8,2,8,128]{4,3,2,1,0:T(8,128)(2,1)S(1)} %get-tuple-element.34), channel_id=1, source_target_pairs={{0,4},{4,8},{8,12},{12,16},{16,20},{20,24},{24,28},{28,0},{1,5},{5... | collective-permute-start | bytes 393224 | tf_op jit(solution)/shard_map/ppermute | solution.py:282
  157.0 18.0 %copy-start.16 = (bf16[4,8,2,8,128]{4,3,2,1,0:T(8,128)(2,1)}, bf16[4,8,2,8,128]{4,3,2,1,0:T(8,128)(2,1)S(1)}, u32[]{:S(2)}) copy-start(bf16[4,8,2,8,128]{4,3,2,1,0:T(8,128)(2,1)S(1)} %collective-permute-done.13.refs_5_) | copy-start | bytes 393220
  161.1 13.9 %copy-start.18 = (bf16[4,8,2,8,128]{4,3,2,1,0:T(8,128)(2,1)}, bf16[4,8,2,8,128]{4,3,2,1,0:T(8,128)(2,1)S(1)}, u32[]{:S(2)}) copy-start(bf16[4,8,2,8,128]{4,3,2,1,0:T(8,128)(2,1)S(1)} %collective-permute-done.12.refs_4_) | copy-start | bytes 393220
  169.9 5.0 %copy-start.20 = (bf16[4,8,2,8,128]{4,3,2,1,0:T(8,128)(2,1)}, bf16[4,8,2,8,128]{4,3,2,1,0:T(8,128)(2,1)S(1)}, u32[]{:S(2)}) copy-start(bf16[4,8,2,8,128]{4,3,2,1,0:T(8,128)(2,1)S(1)} %collective-permute-done.11.refs_3_) | copy-start | bytes 393220
  169.9 5.1 %copy-start.22 = (bf16[4,8,2,8,128]{4,3,2,1,0:T(8,128)(2,1)}, bf16[4,8,2,8,128]{4,3,2,1,0:T(8,128)(2,1)S(1)}, u32[]{:S(2)}) copy-start(bf16[4,8,2,8,128]{4,3,2,1,0:T(8,128)(2,1)S(1)} %collective-permute-done.10.refs_2_) | copy-start | bytes 393220
  175.0 0.6 copy-start.24
  178.7 6.5 %collective-permute-start.16 = (bf16[2,64,8,128]{3,2,1,0:T(8,128)(2,1)}, bf16[2,64,8,128]{3,2,1,0:T(8,128)(2,1)S(1)}, u32[]{:S(2)}, u32[]{:S(2)}) collective-permute-start(bf16[2,64,8,128]{3,2,1,0:T(8,128)(2,1)} %get-tuple-element.26), channel_id=1, source_target_pairs={{0,4},{4,8},{8,12},{12,16},{16,20},{20,24},{24,28},{1,5},{5,9},{9,... | collective-permute-start | bytes 786440 | tf_op jit(solution)/shard_map/ppermute | solution.py:296
  180.3 8.7 %collective-permute-start.17 = (bf16[2,64,8,128]{3,2,1,0:T(8,128)(2,1)}, bf16[2,64,8,128]{3,2,1,0:T(8,128)(2,1)S(1)}, u32[]{:S(2)}, u32[]{:S(2)}) collective-permute-start(bf16[2,64,8,128]{3,2,1,0:T(8,128)(2,1)} %get-tuple-element.27), channel_id=1, source_target_pairs={{4,0},{8,4},{12,8},{16,12},{20,16},{24,20},{28,24},{5,1},{9,5},{13... | collective-permute-start | bytes 786440 | tf_op jit(solution)/shard_map/ppermute | solution.py:297
  185.2 3.9 %copy-start.6 = (bf16[2,64,8,128]{3,2,1,0:T(8,128)(2,1)}, bf16[2,64,8,128]{3,2,1,0:T(8,128)(2,1)S(1)}, u32[]{:S(2)}) copy-start(bf16[2,64,8,128]{3,2,1,0:T(8,128)(2,1)S(1)} %collective-permute-done.16.left_ref) | copy-start | bytes 786436
  189.0 0.7 copy-start.8
  189.8 14.1 %copy-start.30 = (f32[64]{0:T(128)S(1)}, f32[64]{0:T(128)}, u32[]{:S(2)}) copy-start(f32[64]{0:T(128)} %param.16) | copy-start | bytes 772
  189.8 14.2 %copy-start.27 = (s32[64,8]{0,1:T(8,128)S(1)}, s32[64,8]{0,1:T(8,128)}, u32[]{:S(2)}) copy-start(s32[64,8]{0,1:T(8,128)} %param.19) | copy-start | bytes 6148
  194.5 11.0 %copy-start.4 = (bf16[256,256]{1,0:T(8,128)(2,1)S(1)}, bf16[256,256]{1,0:T(8,128)(2,1)}, u32[]{:S(2)}) copy-start(bf16[256,256]{1,0:T(8,128)(2,1)} %trans_ref.1) | copy-start | bytes 393220
  194.5 11.8 %copy-start.26 = (bf16[256,256]{1,0:T(8,128)(2,1)S(1)}, bf16[256,256]{1,0:T(8,128)(2,1)}, u32[]{:S(2)}) copy-start(bf16[256,256]{1,0:T(8,128)(2,1)} %param.13) | copy-start | bytes 393220
  194.5 21.0 %copy-start = (bf16[32,8,2,8,128]{4,3,2,1,0:T(8,128)(2,1)}, bf16[32,8,2,8,128]{4,3,2,1,0:T(8,128)(2,1)S(1)}, u32[]{:S(2)}) copy-start(bf16[32,8,2,8,128]{4,3,2,1,0:T(8,128)(2,1)S(1)} %all-to-all-done.3.refs_0_) | copy-start | bytes 3145732
  194.6 24.9 %all-to-all-start.5 = ((bf16[32,8,2,8,128]{4,3,2,1,0:T(8,128)(2,1)}), bf16[32,8,2,8,128]{4,3,2,1,0:T(8,128)(2,1)S(1)}, u32[]{:S(2)}, u32[]{:S(2)}) async-start(bf16[32,8,2,8,128]{4,3,2,1,0:T(8,128)(2,1)} %bitcast.51), calls=%async_computation.5 | async-start | bytes 2097152 | tf_op jit(solution)/shard_map/all_to_all | solution.py:267
  219.4 1.0 copy-start.1

commit v3 on v2

v3 whole, which is shorter than its diff:
```python
import functools

import jax
import jax.numpy as jnp
from jax import lax
from jax.experimental import pallas as pl
from jax.experimental.pallas import tpu as pltpu
from jax.sharding import Mesh
from jax.sharding import PartitionSpec as P

REACH = 2
VMEM = pl.BlockSpec(memory_space=pltpu.VMEM)
SMEM = pl.BlockSpec(memory_space=pltpu.SMEM)


def pack_kernel(x_ref, o_ref, *, flip):
    n, _, _, sr, _ = o_ref.shape
    for r in range(x_ref.shape[0]):
        for s in range(x_ref.shape[1]):
            block = x_ref[r, s].astype(jnp.float32)
            if flip:
                block = block.T
            for u in range(n):
                o_ref[u, r, s] = block[sr * u : sr * u + sr].astype(jnp.bfloat16)


def pack(x, n, flip):
    rows, cols, w, _ = x.shape
    sr = w // n
    step = 2
    return pl.pallas_call(
        functools.partial(pack_kernel, flip=flip),
        grid=(rows // step,),
        in_specs=[pl.BlockSpec((step, cols, w, w), lambda k: (k, 0, 0, 0))],
        out_specs=pl.BlockSpec((n, step, cols, sr, w), lambda k: (0, k, 0, 0, 0)),
        out_shape=jax.ShapeDtypeStruct((n, rows, cols, sr, w), jnp.bfloat16),
        name="pack_flip" if flip else "pack",
    )(x)


def sym_kernel(z_ref, a_ref, *refs, split):
    got, (o_ref, lo_ref, hi_ref) = refs[:-3], refs[-3:]
    t_n, g_n, r_n, s_n, _, _ = a_ref.shape
    j_n = g_n * s_n
    at = 0
    for k, parts in enumerate(split):
        tile = got[at : at + parts]
        at += parts
        t = lax.rem(z_ref[0] + (t_n - k), t_n)
        for j in range(j_n):
            for i in range(r_n):
                own = a_ref[t, j // s_n, i, j % s_n].astype(jnp.float32)
                g = i // s_n
                b_ref = tile[g * parts // g_n]
                mir = b_ref[g % (g_n // parts), j, i % s_n].astype(jnp.float32)
                val = (0.5 * (own + mir)).astype(jnp.bfloat16)
                o_ref[j, t * r_n + i] = val
                if j < REACH:
                    lo_ref[j, t * r_n + i] = val
                if j >= j_n - REACH:
                    hi_ref[j - j_n + REACH, t * r_n + i] = val


def symmetrize(z, own, got):
    t_n, g_n, r_n, s_n, sr, sl = own.shape
    shape = lambda n: jax.ShapeDtypeStruct((n, t_n * r_n, sr, sl), jnp.bfloat16)
    flat = [part for tile in got for part in tile]
    return pl.pallas_call(
        functools.partial(sym_kernel, split=[len(tile) for tile in got]),
        in_specs=[SMEM, VMEM] + [VMEM] * len(flat),
        out_specs=[VMEM] * 3,
        out_shape=[shape(g_n * s_n), shape(REACH), shape(REACH)],
        name="sym",
    )(z[None], own, *flat)


def _couple_pair(lists_ref, weights_ref, row_of, col_of, gj, i):
    row = weights_ref[i, 0] * row_of(lists_ref[i, 0]).astype(jnp.float32)
    row = row + weights_ref[i, 1] * row_of(lists_ref[i, 1]).astype(jnp.float32)
    col = weights_ref[gj, 0] * col_of(lists_ref[gj, 0]).astype(jnp.float32)
    col = col + weights_ref[gj, 1] * col_of(lists_ref[gj, 1]).astype(jnp.float32)
    total = row.astype(jnp.bfloat16).astype(jnp.float32) + col.astype(jnp.bfloat16).astype(
        jnp.float32
    )
    return total.astype(jnp.bfloat16)


def inner_kernel(lists_ref, weights_ref, start_ref, sym_ref, o_ref):
    t_n, _, r_n, s_n, _, _ = o_ref.shape
    start = start_ref[0]
    first = (pl.program_id(0) + REACH // s_n) * s_n

    def tile(t, carry):
        for s in range(s_n):
            j = first + s
            for r in range(r_n):
                i = t * r_n + r
                o_ref[t, 0, r, s] = _couple_pair(
                    lists_ref,
                    weights_ref,
                    lambda p: sym_ref[j, p],
                    lambda p: sym_ref[p - start, i],
                    start + j,
                    i,
                )
        return carry

    lax.fori_loop(0, t_n, tile, 0)


def edge_kernel(
    lists_ref, weights_ref, start_ref, sym_ref, left_ref, right_ref, _, o_ref, ext_ref
):
    t_n, _, r_n, s_n, _, _ = o_ref.shape
    j_n = sym_ref.shape[0]
    per = REACH // s_n
    k = pl.program_id(0)
    start = start_ref[0]
    high = k >= per
    base = jnp.where(high, j_n - 2 * REACH, -REACH)
    j0 = jnp.where(high, j_n - REACH, 0) + lax.rem(k, per) * s_n

    @pl.when(k == 0)
    def _():
        ext_ref[0:REACH] = left_ref[...]
        ext_ref[REACH:] = sym_ref[0 : 2 * REACH]

    @pl.when(k == per)
    def _():
        ext_ref[0 : 2 * REACH] = sym_ref[j_n - 2 * REACH :]
        ext_ref[2 * REACH :] = right_ref[...]

    def tile(t, carry):
        for s in range(s_n):
            j = j0 + s
            for r in range(r_n):
                i = t * r_n + r
                o_ref[t, 0, r, s] = _couple_pair(
                    lists_ref,
                    weights_ref,
                    lambda p: sym_ref[j, p],
                    lambda p: ext_ref[p - start - base, i],
                    start + j,
                    i,
                )
        return carry

    lax.fori_loop(0, t_n, tile, 0)


def couple(lists, weights, start, sym, left, right, r_n, s_n):
    j_n, i_n, sr, sl = sym.shape
    t_n, g_n = i_n // r_n, j_n // s_n
    per = REACH // s_n
    out = jax.ShapeDtypeStruct((t_n, g_n, r_n, s_n, sr, sl), jnp.bfloat16)
    block = (t_n, 1, r_n, s_n, sr, sl)
    part = pl.pallas_call(
        inner_kernel,
        grid=(g_n - 2 * per,),
        in_specs=[SMEM, SMEM, SMEM, VMEM],
        out_specs=pl.BlockSpec(block, lambda k: (0, k + per, 0, 0, 0, 0)),
        out_shape=out,
        name="inner",
    )(lists, weights, start, sym)
    return pl.pallas_call(
        edge_kernel,
        grid=(2 * per,),
        in_specs=[SMEM, SMEM, SMEM, VMEM, VMEM, VMEM, pl.BlockSpec(memory_space=pl.ANY)],
        out_specs=pl.BlockSpec(
            block, lambda k: (0, k + jnp.where(k >= per, g_n - 2 * per, 0), 0, 0, 0, 0)
        ),
        out_shape=out,
        scratch_shapes=[pltpu.VMEM((3 * REACH, i_n, sr, sl), jnp.bfloat16)],
        input_output_aliases={6: 0},
        name="edge",
    )(lists, weights, start, sym, left, right, part)


def _dot(x, y):
    return jnp.dot(x, y, preferred_element_type=jnp.float32)


def pre_kernel(amp_ref, exch_ref, fock_ref, over_ref, o_ref):
    fock = fock_ref[...]
    over = over_ref[...]
    for s in range(amp_ref.shape[1]):
        amp = amp_ref[0, s]
        first = _dot(_dot(fock, amp).astype(jnp.bfloat16), over)
        second = _dot(_dot(over, amp).astype(jnp.bfloat16), fock)
        o_ref[0, s] = exch_ref[0, s].astype(jnp.float32) + first + second


def precompute(amp, exch, fock, over):
    rows, cols, w, _ = amp.shape
    big = pl.BlockSpec((1, cols, w, w), lambda k: (k, 0, 0, 0))
    mat = pl.BlockSpec((w, w), lambda k: (0, 0))
    return pl.pallas_call(
        pre_kernel,
        grid=(rows,),
        in_specs=[big, big, mat, mat],
        out_specs=big,
        out_shape=jax.ShapeDtypeStruct(amp.shape, jnp.float32),
        name="precompute",
    )(amp, exch, fock, over)


def post_kernel(
    occ_ref,
    base_ref,
    amp_ref,
    mask_i_ref,
    mask_j_ref,
    over_ref,
    trans_ref,
    tt_ref,
    energy_ref,
    coup_ref,
    res_ref,
    new_ref,
):
    k = pl.program_id(0)
    step, cols, w, _ = amp_ref.shape
    rows = pl.num_programs(0) * step
    over = over_ref[...]
    trans = trans_ref[...]
    tt = tt_ref[...]
    pairs = [(r, s) for r in range(step) for s in range(cols)]
    bf = lambda xs: [x.astype(jnp.bfloat16) for x in xs]

    def left(m, xs):
        return [_dot(m, x) for x in xs]

    def right(xs, m):
        return [_dot(x, m) for x in xs]

    two = []
    cm = []
    for r, s in pairs:
        row = jnp.maximum(mask_i_ref[r], mask_j_ref[s])
        two.append(row.T * row)
        coup = coup_ref[:, k * step + r, s].astype(jnp.float32).reshape(w, w)
        cm.append(coup * two[-1])
    third = right(bf(left(over, bf(cm))), over)
    res = [m * (base_ref[r, s] - t) for m, t, (r, s) in zip(two, third, pairs)]
    for x, (r, s) in zip(res, pairs):
        res_ref[r, s] = x
    q = right(bf(left(tt, bf(res))), trans)
    energy = energy_ref[...].T + energy_ref[...]
    z = [
        x / (energy - (occ_ref[k * step + r] + occ_ref[rows + s])) for x, (r, s) in zip(q, pairs)
    ]
    u = right(bf(left(trans, bf(z))), tt)
    for x, (r, s) in zip(u, pairs):
        new_ref[r, s] = (amp_ref[r, s].astype(jnp.float32) - x).astype(jnp.bfloat16)


def finish(occ, base, amp, coup, mask_i, mask_j, over, trans, energy):
    rows, cols, w, _ = amp.shape
    step = 2
    big = pl.BlockSpec((step, cols, w, w), lambda k, *_: (k, 0, 0, 0))
    mat = pl.BlockSpec((w, w), lambda k, *_: (0, 0))
    return pl.pallas_call(
        post_kernel,
        grid_spec=pltpu.PrefetchScalarGridSpec(
            num_scalar_prefetch=1,
            grid=(rows // step,),
            in_specs=[
                big,
                big,
                pl.BlockSpec((step, 1, w), lambda k, *_: (k, 0, 0)),
                pl.BlockSpec((cols, 1, w), lambda k, *_: (0, 0, 0)),
                mat,
                mat,
                mat,
                pl.BlockSpec((1, w), lambda k, *_: (0, 0)),
                VMEM,
            ],
            out_specs=[big, big],
        ),
        out_shape=[
            jax.ShapeDtypeStruct(amp.shape, jnp.float32),
            jax.ShapeDtypeStruct(amp.shape, jnp.bfloat16),
        ],
        name="finish",
    )(
        occ,
        base,
        amp,
        mask_i[:, None, :],
        mask_j[:, None, :],
        over,
        trans,
        trans.T,
        energy[None, :],
        coup,
    )


def per_device(
    amplitudes,
    exchange,
    fock_virt,
    intersection,
    transform,
    virt_energy,
    occ_energy,
    partners,
    coupling,
    domain,
):
    rows, cols, width, _ = amplitudes.shape
    blocks = domain.shape[1]
    a_n = lax.axis_size("a")
    z_n = lax.axis_size("z")
    g_n = lax.axis_size("g")
    start_i = lax.axis_index("a") * rows
    start_z = lax.axis_index("z") * (g_n * cols)
    start_j = start_z + lax.axis_index("g") * cols
    plane = ("a", "g")
    n = a_n * g_n

    over = (jnp.eye(width, dtype=jnp.float32) + intersection.astype(jnp.float32)).astype(
        jnp.bfloat16
    )
    shape = (a_n, g_n, rows, cols, width // n, width)
    z = lax.axis_index("z")

    def spread(x):
        return lax.all_to_all(x, plane, 0, 0, tiled=True)

    def shift(x, k):
        return lax.ppermute(x, "z", [(q, (q + k) % z_n) for q in range(z_n)])

    part = spread(pack(amplitudes, n, True)).reshape(shape)
    own = pack(amplitudes, n, False)
    tiles = [
        lax.dynamic_index_in_dim(part, lax.rem(z + k, z_n), 0, keepdims=False) for k in range(z_n)
    ]
    half = g_n // 2
    far = z_n // 2
    relay = shift(tiles[far][half:], z_n - 1)
    got = []
    for k in range(z_n):
        if k == 0:
            got.append([tiles[k]])
        elif k == far:
            got.append([shift(tiles[k][:half], k)])
        else:
            got.append([shift(tiles[k], k)])
    got[far].append(shift(relay, far + 1))
    base = precompute(amplitudes, exchange, fock_virt, over)
    own, _ = lax.optimization_barrier((own, tiles[0]))
    own = spread(own).reshape(shape)
    sym, low, high = symmetrize(z, own, got)
    left = lax.ppermute(high, "z", [(k, k + 1) for k in range(z_n - 1)])
    right = lax.ppermute(low, "z", [(k + 1, k) for k in range(z_n - 1)])
    part = couple(partners, coupling, start_z[None], sym, left, right, rows, cols)
    coup = spread(part.reshape(n, rows, cols, width // n, width))

    masks = jnp.repeat(domain.astype(jnp.float32), width // blocks, axis=1)
    mask_i = lax.dynamic_slice_in_dim(masks, start_i, rows, 0)
    mask_j = lax.dynamic_slice_in_dim(masks, start_j, cols, 0)
    occ = jnp.concatenate(
        [
            lax.dynamic_slice_in_dim(occ_energy, start_i, rows, 0),
            lax.dynamic_slice_in_dim(occ_energy, start_j, cols, 0),
        ]
    )
    return tuple(
        finish(occ, base, amplitudes, coup, mask_i, mask_j, over, transform, virt_energy)
    )


def solution(mesh):
    i_n, j_n = mesh.shape["occi"], mesh.shape["occj"]
    group = j_n // i_n
    z_n = j_n // group
    inner = Mesh(mesh.devices.reshape(i_n, z_n, group), ("a", "z", "g"))
    pairs = P("a", ("z", "g"), None, None)
    return jax.shard_map(
        per_device,
        mesh=inner,
        in_specs=(pairs, pairs, P(), P(), P(), P(), P(), P(), P(), P()),
        out_specs=(pairs, pairs),
        check_vma=False,
    )
```

time: 233 us -> 185 us (0.79)
  starting transfers between devices: 69.8 us -> 43.3 us
  blocking collectives: 20.9 us -> 0 us
    all_to_all x1 -> x0, blocking collectives: 20.9 us -> none  [spread(): return lax.all_to_all(x, plane, 0, 0, tiled=True)]
    ppermute x18 -> x11, starting transfers between devices: 33 us -> 18.8 us  [the longest x9 16.2 us: shift(): return lax.ppermute(x, 'z', [(q, (q + k) % z_n) for q in range(z_n)])]
    all_to_all x5 -> x3, starting transfers between devices: 36.9 us -> 24.5 us  [spread(): return lax.all_to_all(x, plane, 0, 0, tiled=True)]
    all_to_all x5 -> x3, waiting for transfers between devices: 30.6 us -> 38 us  [spread(): return lax.all_to_all(x, plane, 0, 0, tiled=True)]
    ppermute x18 -> x11, waiting for transfers between devices: 55.1 us -> 49.1 us  [the longest x9 39.8 us: shift(): return lax.ppermute(x, 'z', [(q, (q + k) % z_n) for q in range(z_n)])]
    unnamed x65 -> x37, local copies, waits for them, and re-layouts: 5.96 us -> 5 us
    pallas_call x4 -> x3, Pallas kernels: 15.7 us -> 15.3 us  [the longest x1 5.71 us: couple(): pl.pallas_call(edge_kernel, grid=(2 * per,), in_specs=[SMEM, SMEM, SMEM,...]
  transfers between devices with their start and end apart: 23 -> 14, of which waited for: 16 -> 8; matrix products, arithmetic and copies ran while one was open for 2% -> 3% of each run, Pallas kernels for 12% -> 10%
where the time goes in v3:
time: 185 us; the launch traced here: 182 us
  waiting for transfers between devices  87.2 us (47%)
  starting transfers between devices  43.3 us (23%)
  Pallas kernels  41.6 us (22%)
  local copies, waits for them, and re-layouts  7.64 us (4%)
    ppermute x9, waiting for transfers between devices, shift(): return lax.ppermute(x, 'z', [(q, (q + k) % z_n) for q in range(z_n)])  39.8 us
    all_to_all x3, waiting for transfers between devices, spread(): return lax.all_to_all(x, plane, 0, 0, tiled=True)  38 us
    all_to_all x3, starting transfers between devices, spread(): return lax.all_to_all(x, plane, 0, 0, tiled=True)  24.5 us
    ppermute x9, starting transfers between devices, shift(): return lax.ppermute(x, 'z', [(q, (q + k) % z_n) for q in range(z_n)])  16.2 us
    pallas_call x1, Pallas kernels, finish(): pl.pallas_call(post_kernel, grid_spec=pltpu.PrefetchScalarGridSpec(num_sc...  9.84 us
    pallas_call x1, Pallas kernels, precompute(): pl.pallas_call(pre_kernel, grid=(rows,), in_specs=[big, big, mat, mat], o...  8.48 us
    pallas_call x2, Pallas kernels, pack(): pl.pallas_call(functools.partial(pack_kernel, flip=flip), grid=(rows // s...  7.97 us
    ppermute x1, waiting for transfers between devices, per_device(): right = lax.ppermute(low, 'z', [(k + 1, k) for k in range(z_n - 1)])  6.75 us
  transfers between devices with their start and end apart: 14, of which 8 were waited for; matrix products, arithmetic and copies ran while one was open for 3% of the time, Pallas kernels for 10%

profile of v3, /device:TPU:3, one launch (start us, length us, event | category | flops | bytes accessed | tf_op | source)
XLA Modules:
  0.0 182.0 jit_solution(14873882675844358426)
XLA Ops:
  0.6 4.1 %pack_flip.1 = bf16[32,8,2,8,256]{4,3,2,1,0:T(8,128)(2,1)} custom-call(bf16[8,2,256,256]{3,2,1,0:T(8,128)(2,1)} %amp_ref.3), custom_call_target="tpu_custom_call" | custom-call | tf_op jit(solution)/shard_map/pack_flip/pallas_call | solution.py:31
  4.8 7.9 %all-to-all-start = ((bf16[32,8,2,8,256]{4,3,2,1,0:T(8,128)(2,1)}), bf16[32,8,2,8,256]{4,3,2,1,0:T(8,128)(2,1)S(1)}, u32[]{:S(2)}, u32[]{:S(2)}) async-start(bf16[32,8,2,8,256]{4,3,2,1,0:T(8,128)(2,1)} %pack_flip.1), calls=%async_computation | async-start | bytes 4194304 | tf_op jit(solution)/shard_map/all_to_all | solution.py:329
  12.7 3.8 %pack.1 = bf16[32,8,2,8,256]{4,3,2,1,0:T(8,128)(2,1)} custom-call(bf16[8,2,256,256]{3,2,1,0:T(8,128)(2,1)} %amp_ref.3), custom_call_target="tpu_custom_call" | custom-call | tf_op jit(solution)/shard_map/pack/pallas_call | solution.py:31
  16.6 23.2 %all-to-all-done = bf16[32,8,2,8,256]{4,3,2,1,0:T(8,128)(2,1)S(1)} async-done(((bf16[32,8,2,8,256]{4,3,2,1,0:T(8,128)(2,1)}), bf16[32,8,2,8,256]{4,3,2,1,0:T(8,128)(2,1)S(1)}, u32[]{:S(2)}, u32[]{:S(2)}) %all-to-all-start) | async-done | bytes 2097184 | tf_op jit(solution)/shard_map/all_to_all | solution.py:329
  39.8 1.0 dynamic-slice_bitcast_fusion
  40.7 7.4 %all-to-all-start.1 = ((bf16[32,8,2,8,256]{4,3,2,1,0:T(8,128)(2,1)}), bf16[32,8,2,8,256]{4,3,2,1,0:T(8,128)(2,1)}, u32[]{:S(2)}, u32[]{:S(2)}) async-start(bf16[32,8,2,8,256]{4,3,2,1,0:T(8,128)(2,1)} %pack.1), calls=%async_computation.1 | async-start | bytes 4194304 | tf_op jit(solution)/shard_map/all_to_all | solution.py:329
  48.1 5.7 %collective-permute-start.8 = (bf16[4,8,2,8,256]{4,3,2,1,0:T(8,128)(2,1)}, bf16[4,8,2,8,256]{4,3,2,1,0:T(8,128)(2,1)S(1)}, u32[]{:S(2)}, u32[]{:S(2)}) collective-permute-start(bf16[4,8,2,8,256]{4,3,2,1,0:T(8,128)(2,1)} %get-tuple-element.10), channel_id=1, source_target_pairs={{0,28},{4,0},{8,4},{12,8},{16,12},{20,16},{24,20},{28,24},{1,29},{... | collective-permute-start | bytes 786440 | tf_op jit(solution)/shard_map/ppermute | solution.py:332
  53.8 0.8 collective-permute-start.4
  54.6 0.7 collective-permute-start.3
  55.4 0.4 collective-permute-start.7
  55.8 4.9 %collective-permute-start.6 = (bf16[4,8,2,8,256]{4,3,2,1,0:T(8,128)(2,1)S(1)}, bf16[4,8,2,8,256]{4,3,2,1,0:T(8,128)(2,1)S(1)}, u32[]{:S(2)}, u32[]{:S(2)}) collective-permute-start(bf16[4,8,2,8,256]{4,3,2,1,0:T(8,128)(2,1)S(1)} %get-tuple-element.12), channel_id=1, source_target_pairs={{0,20},{4,24},{8,28},{12,0},{16,4},{20,8},{24,12},{28,16},{1,21},{... | collective-permute-start | bytes 786440 | tf_op jit(solution)/shard_map/ppermute | solution.py:332
  60.7 7.3 %collective-permute-done.4 = bf16[2,8,2,8,256]{4,3,2,1,0:T(8,128)(2,1)S(1)} collective-permute-done((bf16[2,8,2,8,256]{4,3,2,1,0:T(8,128)(2,1)S(1)}, bf16[2,8,2,8,256]{4,3,2,1,0:T(8,128)(2,1)S(1)}, u32[]{:S(2)}, u32[]{:S(2)}) %collective-permute-start.4) | collective-permute-done | bytes 131104 | tf_op jit(solution)/shard_map/ppermute | solution.py:332
  68.0 0.0 collective-permute-start.2
  68.0 0.0 collective-permute-done.3.refs_4_
  68.0 0.1 collective-permute-start.1
  68.1 0.0 collective-permute-done.8.refs_8_
  68.1 0.0 copy-start.4
  68.2 3.6 %collective-permute-start = (bf16[4,8,2,8,256]{4,3,2,1,0:T(8,128)(2,1)S(1)}, bf16[4,8,2,8,256]{4,3,2,1,0:T(8,128)(2,1)S(1)}, u32[]{:S(2)}, u32[]{:S(2)}) collective-permute-start(bf16[4,8,2,8,256]{4,3,2,1,0:T(8,128)(2,1)S(1)} %get-tuple-element.15), channel_id=1, source_target_pairs={{0,4},{4,8},{8,12},{12,16},{16,20},{20,24},{24,28},{28,0},{1,5},{5... | collective-permute-start | bytes 786440 | tf_op jit(solution)/shard_map/ppermute | solution.py:332
  71.7 14.6 %collective-permute-done.7.refs_7_ = bf16[4,8,2,8,256]{4,3,2,1,0:T(8,128)(2,1)S(1)} collective-permute-done((bf16[4,8,2,8,256]{4,3,2,1,0:T(8,128)(2,1)}, bf16[4,8,2,8,256]{4,3,2,1,0:T(8,128)(2,1)S(1)}, u32[]{:S(2)}, u32[]{:S(2)}) %collective-permute-start.7) | collective-permute-done | bytes 262176 | tf_op jit(solution)/shard_map/ppermute | solution.py:332
  86.4 0.0 collective-permute-start.5
  86.4 13.5 %collective-permute-done.6.refs_6_ = bf16[4,8,2,8,256]{4,3,2,1,0:T(8,128)(2,1)S(1)} collective-permute-done((bf16[4,8,2,8,256]{4,3,2,1,0:T(8,128)(2,1)S(1)}, bf16[4,8,2,8,256]{4,3,2,1,0:T(8,128)(2,1)S(1)}, u32[]{:S(2)}, u32[]{:S(2)}) %collective-permute-start.6) | collective-permute-done | bytes 262176 | tf_op jit(solution)/shard_map/ppermute | solution.py:332
  99.9 0.0 collective-permute-done.2.refs_3_
  99.9 0.0 collective-permute-done.1.refs_2_
  99.9 0.0 copy-start.8
  99.9 0.0 collective-permute-done.refs_1_
  99.9 0.0 copy-start.9
  99.9 4.3 %collective-permute-done.5.refs_5_ = bf16[2,8,2,8,256]{4,3,2,1,0:T(8,128)(2,1)S(1)} collective-permute-done((bf16[2,8,2,8,256]{4,3,2,1,0:T(8,128)(2,1)S(1)}, bf16[2,8,2,8,256]{4,3,2,1,0:T(8,128)(2,1)S(1)}, u32[]{:S(2)}, u32[]{:S(2)}) %collective-permute-start.5) | collective-permute-done | bytes 131104 | tf_op jit(solution)/shard_map/ppermute | solution.py:332
  104.2 0.0 all-to-all-done.1
  104.2 0.0 copy-done.10
  104.2 0.0 copy-done.4
  104.2 0.0 copy-done.5
  104.2 0.0 copy-done.6
  104.2 0.0 copy-done.7
  104.2 0.0 copy-done.8
  104.3 0.0 copy-done.9
  104.3 0.6 copy-done.11
  104.9 4.4 %sym.1 = (bf16[8,64,8,256]{3,2,1,0:T(8,128)(2,1)}, bf16[2,64,8,256]{3,2,1,0:T(8,128)(2,1)}, bf16[2,64,8,256]{3,2,1,0:T(8,128)(2,1)}) custom-call(s32[1]{0:T(128)} %bitcast.6.z_ref, bf16[8,4,8,2,8,256]{5,4,3,2,1,0:T(8,128)(2,1)} %bitcast.9.a_ref, bf16[4,8,2,8,256]{4,3,2,1,0:T(8,128)(2,1)} %get-tuple-element.16.refs_0_, bf16[4,8,2,8,256]{4,3,2,1,0:T(8,128)(2,1)} %copy-done.9, ...), custom_call_target="tpu_custom_call" | custom-call | tf_op jit(solution)/shard_map/sym/pallas_call | solution.py:68
  109.2 1.3 collective-permute-start.9
  110.5 1.3 collective-permute-start.10
  111.8 0.0 copy-done.14
  111.8 0.7 copy.24.lists_ref
  112.6 0.0 copy-done.15
  112.6 0.7 copy.25.weights_ref
  113.3 5.2 %inner.1._ = bf16[8,4,8,2,8,256]{5,4,3,2,1,0:T(8,128)(2,1)} custom-call(s32[64,2]{1,0:T(8,128)} %copy.24.lists_ref, f32[64,2]{1,0:T(8,128)} %copy.25.weights_ref, s32[1]{0:T(128)} %bitcast.5.start_ref, bf16[8,64,8,256]{3,2,1,0:T(8,128)(2,1)} %get-tuple-element.7.sym_ref), custom_call_target="tpu_custom_call" | custom-call | tf_op jit(solution)/shard_map/inner/pallas_call | solution.py:157
  118.5 2.6 %collective-permute-done.9.left_ref = bf16[2,64,8,256]{3,2,1,0:T(8,128)(2,1)S(1)} collective-permute-done((bf16[2,64,8,256]{3,2,1,0:T(8,128)(2,1)}, bf16[2,64,8,256]{3,2,1,0:T(8,128)(2,1)S(1)}, u32[]{:S(2)}, u32[]{:S(2)}) %collective-permute-start.9) | collective-permute-done | bytes 524320 | tf_op jit(solution)/shard_map/ppermute | solution.py:355
  121.1 6.8 %collective-permute-done.10.right_ref = bf16[2,64,8,256]{3,2,1,0:T(8,128)(2,1)S(1)} collective-permute-done((bf16[2,64,8,256]{3,2,1,0:T(8,128)(2,1)}, bf16[2,64,8,256]{3,2,1,0:T(8,128)(2,1)S(1)}, u32[]{:S(2)}, u32[]{:S(2)}) %collective-permute-start.10) | collective-permute-done | bytes 524320 | tf_op jit(solution)/shard_map/ppermute | solution.py:356
  127.9 0.8 copy-done.3
  128.7 5.7 %edge.1 = bf16[8,4,8,2,8,256]{5,4,3,2,1,0:T(8,128)(2,1)} custom-call(s32[64,2]{1,0:T(8,128)} %copy.24.lists_ref, f32[64,2]{1,0:T(8,128)} %copy.25.weights_ref, s32[1]{0:T(128)} %bitcast.5.start_ref, bf16[8,64,8,256]{3,2,1,0:T(8,128)(2,1)} %get-tuple-element.7.sym_ref, bf16[2,64,8,256]{3,2,1,0:T(8,128)(2,1)} %copy-done.2, ...), custom_call_target="tpu_custom_call", output_to_operand_aliasing={{}: (6, {})} | custom-call | tf_op jit(solution)/shard_map/edge/pallas_call | solution.py:165
  134.4 0.0 copy-start.12
  134.4 9.2 %all-to-all-start.2 = ((bf16[32,8,2,8,256]{4,3,2,1,0:T(8,128)(2,1)}), bf16[32,8,2,8,256]{4,3,2,1,0:T(8,128)(2,1)S(1)}, u32[]{:S(2)}, u32[]{:S(2)}) async-start(bf16[32,8,2,8,256]{4,3,2,1,0:T(8,128)(2,1)} %bitcast.30), calls=%async_computation.2 | async-start | bytes 4194304 | tf_op jit(solution)/shard_map/all_to_all | solution.py:329
  143.7 0.1 dynamic_slice.38
  143.7 0.1 dynamic_slice.37
  143.8 0.1 dynamic-slice_bitcast_fusion.9
  143.9 0.7 copy.27.mask_j_ref
  144.6 0.1 dynamic-slice_bitcast_fusion.10
  144.7 0.7 copy.26.mask_i_ref
  145.4 0.7 copy.21
  146.1 0.0 copy-done.12
  146.1 0.7 add_convert_fusion.over_ref
  146.8 8.5 %precompute.1.base_ref = f32[8,2,256,256]{3,2,1,0:T(8,128)} custom-call(bf16[8,2,256,256]{3,2,1,0:T(8,128)(2,1)} %amp_ref.3, bf16[8,2,256,256]{3,2,1,0:T(8,128)(2,1)} %exch_ref.1, bf16[256,256]{1,0:T(8,128)(2,1)} %fock_ref.1, bf16[256,256]{1,0:T(8,128)(2,1)} %add_convert_fusion.over_ref), custom_call_target="tpu_custom_call" | custom-call | tf_op jit(solution)/shard_map/precompute/pallas_call | solution.py:197
  155.3 0.6 pad_maximum_fusion.occ_ref
  155.9 14.8 %all-to-all-done.2.coup_ref = bf16[32,8,2,8,256]{4,3,2,1,0:T(8,128)(2,1)S(1)} async-done(((bf16[32,8,2,8,256]{4,3,2,1,0:T(8,128)(2,1)}), bf16[32,8,2,8,256]{4,3,2,1,0:T(8,128)(2,1)S(1)}, u32[]{:S(2)}, u32[]{:S(2)}) %all-to-all-start.2) | async-done | bytes 2097184 | tf_op jit(solution)/shard_map/all_to_all | solution.py:329
  170.7 1.4 copy-done
  172.1 9.8 %finish.1 = (f32[8,2,256,256]{3,2,1,0:T(8,128)}, bf16[8,2,256,256]{3,2,1,0:T(8,128)(2,1)}) custom-call(f32[10]{0:T(128)} %pad_maximum_fusion.occ_ref, f32[8,2,256,256]{3,2,1,0:T(8,128)} %precompute.1.base_ref, bf16[8,2,256,256]{3,2,1,0:T(8,128)(2,1)} %amp_ref.3, f32[8,1,256]{2,1,0:T(1,128)} %copy.26.mask_i_ref, f32[2,1,256]{2,1,0:T(1,128)} %copy.27.mask_j_ref, ...), custom_call_target="tpu_custom_call" | custom-call | tf_op jit(solution)/shard_map/finish/pallas_call | solution.py:262
  (20 shorter events, 0.1 us)
Async XLA Ops:
  4.8 35.0 %all-to-all-start = ((bf16[32,8,2,8,256]{4,3,2,1,0:T(8,128)(2,1)}), bf16[32,8,2,8,256]{4,3,2,1,0:T(8,128)(2,1)S(1)}, u32[]{:S(2)}, u32[]{:S(2)}) async-start(bf16[32,8,2,8,256]{4,3,2,1,0:T(8,128)(2,1)} %pack_flip.1), calls=%async_computation | async-start | bytes 4194304 | tf_op jit(solution)/shard_map/all_to_all | solution.py:329
  40.7 63.5 %all-to-all-start.1 = ((bf16[32,8,2,8,256]{4,3,2,1,0:T(8,128)(2,1)}), bf16[32,8,2,8,256]{4,3,2,1,0:T(8,128)(2,1)}, u32[]{:S(2)}, u32[]{:S(2)}) async-start(bf16[32,8,2,8,256]{4,3,2,1,0:T(8,128)(2,1)} %pack.1), calls=%async_computation.1 | async-start | bytes 4194304 | tf_op jit(solution)/shard_map/all_to_all | solution.py:329
  48.1 20.0 %collective-permute-start.8 = (bf16[4,8,2,8,256]{4,3,2,1,0:T(8,128)(2,1)}, bf16[4,8,2,8,256]{4,3,2,1,0:T(8,128)(2,1)S(1)}, u32[]{:S(2)}, u32[]{:S(2)}) collective-permute-start(bf16[4,8,2,8,256]{4,3,2,1,0:T(8,128)(2,1)} %get-tuple-element.10), channel_id=1, source_target_pairs={{0,28},{4,0},{8,4},{12,8},{16,12},{20,16},{24,20},{28,24},{1,29},{... | collective-permute-start | bytes 786440 | tf_op jit(solution)/shard_map/ppermute | solution.py:332
  53.8 14.2 %collective-permute-start.4 = (bf16[2,8,2,8,256]{4,3,2,1,0:T(8,128)(2,1)S(1)}, bf16[2,8,2,8,256]{4,3,2,1,0:T(8,128)(2,1)S(1)}, u32[]{:S(2)}, u32[]{:S(2)}) collective-permute-start(bf16[2,8,2,8,256]{4,3,2,1,0:T(8,128)(2,1)S(1)} %get-tuple-element.17), channel_id=1, source_target_pairs={{0,28},{4,0},{8,4},{12,8},{16,12},{20,16},{24,20},{28,24},{1,29},{... | collective-permute-start | bytes 393224 | tf_op jit(solution)/shard_map/ppermute | solution.py:332
  54.6 13.4 %collective-permute-start.3 = (bf16[2,8,2,8,256]{4,3,2,1,0:T(8,128)(2,1)S(1)}, bf16[2,8,2,8,256]{4,3,2,1,0:T(8,128)(2,1)S(1)}, u32[]{:S(2)}, u32[]{:S(2)}) collective-permute-start(bf16[2,8,2,8,256]{4,3,2,1,0:T(8,128)(2,1)S(1)} %get-tuple-element.18), channel_id=1, source_target_pairs={{0,16},{4,20},{8,24},{12,28},{16,0},{20,4},{24,8},{28,12},{1,17},{... | collective-permute-start | bytes 393224 | tf_op jit(solution)/shard_map/ppermute | solution.py:332
  55.4 31.0 %collective-permute-start.7 = (bf16[4,8,2,8,256]{4,3,2,1,0:T(8,128)(2,1)}, bf16[4,8,2,8,256]{4,3,2,1,0:T(8,128)(2,1)S(1)}, u32[]{:S(2)}, u32[]{:S(2)}) collective-permute-start(bf16[4,8,2,8,256]{4,3,2,1,0:T(8,128)(2,1)} %get-tuple-element.11), channel_id=1, source_target_pairs={{0,24},{4,28},{8,0},{12,4},{16,8},{20,12},{24,16},{28,20},{1,25},{... | collective-permute-start | bytes 786440 | tf_op jit(solution)/shard_map/ppermute | solution.py:332
  55.8 44.1 %collective-permute-start.6 = (bf16[4,8,2,8,256]{4,3,2,1,0:T(8,128)(2,1)S(1)}, bf16[4,8,2,8,256]{4,3,2,1,0:T(8,128)(2,1)S(1)}, u32[]{:S(2)}, u32[]{:S(2)}) collective-permute-start(bf16[4,8,2,8,256]{4,3,2,1,0:T(8,128)(2,1)S(1)} %get-tuple-element.12), channel_id=1, source_target_pairs={{0,20},{4,24},{8,28},{12,0},{16,4},{20,8},{24,12},{28,16},{1,21},{... | collective-permute-start | bytes 786440 | tf_op jit(solution)/shard_map/ppermute | solution.py:332
  68.0 31.8 %collective-permute-start.2 = (bf16[4,8,2,8,256]{4,3,2,1,0:T(8,128)(2,1)S(1)}, bf16[4,8,2,8,256]{4,3,2,1,0:T(8,128)(2,1)S(1)}, u32[]{:S(2)}, u32[]{:S(2)}) collective-permute-start(bf16[4,8,2,8,256]{4,3,2,1,0:T(8,128)(2,1)S(1)} %get-tuple-element.13), channel_id=1, source_target_pairs={{0,12},{4,16},{8,20},{12,24},{16,28},{20,0},{24,4},{28,8},{1,13},{... | collective-permute-start | bytes 786440 | tf_op jit(solution)/shard_map/ppermute | solution.py:332
  68.0 36.2 %copy-start.10 = (bf16[2,8,2,8,256]{4,3,2,1,0:T(8,128)(2,1)}, bf16[2,8,2,8,256]{4,3,2,1,0:T(8,128)(2,1)S(1)}, u32[]{:S(2)}) copy-start(bf16[2,8,2,8,256]{4,3,2,1,0:T(8,128)(2,1)S(1)} %collective-permute-done.3.refs_4_) | copy-start | bytes 393220
  68.0 31.8 %collective-permute-start.1 = (bf16[4,8,2,8,256]{4,3,2,1,0:T(8,128)(2,1)S(1)}, bf16[4,8,2,8,256]{4,3,2,1,0:T(8,128)(2,1)S(1)}, u32[]{:S(2)}, u32[]{:S(2)}) collective-permute-start(bf16[4,8,2,8,256]{4,3,2,1,0:T(8,128)(2,1)S(1)} %get-tuple-element.14), channel_id=1, source_target_pairs={{0,8},{4,12},{8,16},{12,20},{16,24},{20,28},{24,0},{28,4},{1,9},{5... | collective-permute-start | bytes 786440 | tf_op jit(solution)/shard_map/ppermute | solution.py:332
  68.1 36.1 %copy-start.4 = (bf16[4,8,2,8,256]{4,3,2,1,0:T(8,128)(2,1)}, bf16[4,8,2,8,256]{4,3,2,1,0:T(8,128)(2,1)S(1)}, u32[]{:S(2)}) copy-start(bf16[4,8,2,8,256]{4,3,2,1,0:T(8,128)(2,1)S(1)} %collective-permute-done.8.refs_8_) | copy-start | bytes 786436
  68.2 31.8 %collective-permute-start = (bf16[4,8,2,8,256]{4,3,2,1,0:T(8,128)(2,1)S(1)}, bf16[4,8,2,8,256]{4,3,2,1,0:T(8,128)(2,1)S(1)}, u32[]{:S(2)}, u32[]{:S(2)}) collective-permute-start(bf16[4,8,2,8,256]{4,3,2,1,0:T(8,128)(2,1)S(1)} %get-tuple-element.15), channel_id=1, source_target_pairs={{0,4},{4,8},{8,12},{12,16},{16,20},{20,24},{24,28},{28,0},{1,5},{5... | collective-permute-start | bytes 786440 | tf_op jit(solution)/shard_map/ppermute | solution.py:332
  86.4 17.9 %copy-start.5 = (bf16[4,8,2,8,256]{4,3,2,1,0:T(8,128)(2,1)}, bf16[4,8,2,8,256]{4,3,2,1,0:T(8,128)(2,1)S(1)}, u32[]{:S(2)}) copy-start(bf16[4,8,2,8,256]{4,3,2,1,0:T(8,128)(2,1)S(1)} %collective-permute-done.7.refs_7_) | copy-start | bytes 786436
  86.4 17.9 %collective-permute-start.5 = (bf16[2,8,2,8,256]{4,3,2,1,0:T(8,128)(2,1)S(1)}, bf16[2,8,2,8,256]{4,3,2,1,0:T(8,128)(2,1)S(1)}, u32[]{:S(2)}, u32[]{:S(2)}) collective-permute-start(bf16[2,8,2,8,256]{4,3,2,1,0:T(8,128)(2,1)S(1)} %collective-permute-done.4), channel_id=1, source_target_pairs={{0,20},{4,24},{8,28},{12,0},{16,4},{20,8},{24,12},{28,16},{1,21},{... | collective-permute-start | bytes 393224 | tf_op jit(solution)/shard_map/ppermute | solution.py:332
  99.9 4.4 %copy-start.6 = (bf16[4,8,2,8,256]{4,3,2,1,0:T(8,128)(2,1)}, bf16[4,8,2,8,256]{4,3,2,1,0:T(8,128)(2,1)S(1)}, u32[]{:S(2)}) copy-start(bf16[4,8,2,8,256]{4,3,2,1,0:T(8,128)(2,1)S(1)} %collective-permute-done.6.refs_6_) | copy-start | bytes 786436
  99.9 4.4 %copy-start.7 = (bf16[4,8,2,8,256]{4,3,2,1,0:T(8,128)(2,1)}, bf16[4,8,2,8,256]{4,3,2,1,0:T(8,128)(2,1)S(1)}, u32[]{:S(2)}) copy-start(bf16[4,8,2,8,256]{4,3,2,1,0:T(8,128)(2,1)S(1)} %collective-permute-done.2.refs_3_) | copy-start | bytes 786436
  99.9 4.4 %copy-start.8 = (bf16[4,8,2,8,256]{4,3,2,1,0:T(8,128)(2,1)}, bf16[4,8,2,8,256]{4,3,2,1,0:T(8,128)(2,1)S(1)}, u32[]{:S(2)}) copy-start(bf16[4,8,2,8,256]{4,3,2,1,0:T(8,128)(2,1)S(1)} %collective-permute-done.1.refs_2_) | copy-start | bytes 786436
  99.9 4.3 %copy-start.9 = (bf16[4,8,2,8,256]{4,3,2,1,0:T(8,128)(2,1)}, bf16[4,8,2,8,256]{4,3,2,1,0:T(8,128)(2,1)S(1)}, u32[]{:S(2)}) copy-start(bf16[4,8,2,8,256]{4,3,2,1,0:T(8,128)(2,1)S(1)} %collective-permute-done.refs_1_) | copy-start | bytes 786436
  104.2 0.6 copy-start.11
  104.9 7.0 %copy-start.14 = (s32[64,2]{0,1:T(2,128)S(1)}, s32[64,2]{0,1:T(2,128)}, u32[]{:S(2)}) copy-start(s32[64,2]{0,1:T(2,128)} %param.17) | copy-start | bytes 1540
  104.9 7.7 %copy-start.15 = (f32[64,2]{0,1:T(2,128)S(1)}, f32[64,2]{0,1:T(2,128)}, u32[]{:S(2)}) copy-start(f32[64,2]{0,1:T(2,128)} %param.18) | copy-start | bytes 1540
  109.2 11.9 %collective-permute-start.9 = (bf16[2,64,8,256]{3,2,1,0:T(8,128)(2,1)}, bf16[2,64,8,256]{3,2,1,0:T(8,128)(2,1)S(1)}, u32[]{:S(2)}, u32[]{:S(2)}) collective-permute-start(bf16[2,64,8,256]{3,2,1,0:T(8,128)(2,1)} %get-tuple-element.8), channel_id=1, source_target_pairs={{0,4},{4,8},{8,12},{12,16},{16,20},{20,24},{24,28},{1,5},{5,9},{9,... | collective-permute-start | bytes 1572872 | tf_op jit(solution)/shard_map/ppermute | solution.py:355
  110.5 17.3 %collective-permute-start.10 = (bf16[2,64,8,256]{3,2,1,0:T(8,128)(2,1)}, bf16[2,64,8,256]{3,2,1,0:T(8,128)(2,1)S(1)}, u32[]{:S(2)}, u32[]{:S(2)}) collective-permute-start(bf16[2,64,8,256]{3,2,1,0:T(8,128)(2,1)} %get-tuple-element.9), channel_id=1, source_target_pairs={{4,0},{8,4},{12,8},{16,12},{20,16},{24,20},{28,24},{5,1},{9,5},{13... | collective-permute-start | bytes 1572872 | tf_op jit(solution)/shard_map/ppermute | solution.py:356
  121.1 6.8 %copy-start.2 = (bf16[2,64,8,256]{3,2,1,0:T(8,128)(2,1)}, bf16[2,64,8,256]{3,2,1,0:T(8,128)(2,1)S(1)}, u32[]{:S(2)}) copy-start(bf16[2,64,8,256]{3,2,1,0:T(8,128)(2,1)S(1)} %collective-permute-done.9.left_ref) | copy-start | bytes 1572868
  127.9 0.8 copy-start.3
  134.4 9.3 %copy-start.16 = (f32[64]{0:T(128)S(1)}, f32[64]{0:T(128)}, u32[]{:S(2)}) copy-start(f32[64]{0:T(128)} %param.16) | copy-start | bytes 772
  134.4 9.4 %copy-start.13 = (s32[64,8]{0,1:T(8,128)S(1)}, s32[64,8]{0,1:T(8,128)}, u32[]{:S(2)}) copy-start(s32[64,8]{0,1:T(8,128)} %param.19) | copy-start | bytes 6148
  134.4 11.0 %copy-start.1 = (bf16[256,256]{1,0:T(8,128)(2,1)S(1)}, bf16[256,256]{1,0:T(8,128)(2,1)}, u32[]{:S(2)}) copy-start(bf16[256,256]{1,0:T(8,128)(2,1)} %trans_ref.1) | copy-start | bytes 393220
  134.4 11.7 %copy-start.12 = (bf16[256,256]{1,0:T(8,128)(2,1)S(1)}, bf16[256,256]{1,0:T(8,128)(2,1)}, u32[]{:S(2)}) copy-start(bf16[256,256]{1,0:T(8,128)(2,1)} %param.13) | copy-start | bytes 393220
  134.4 36.3 %all-to-all-start.2 = ((bf16[32,8,2,8,256]{4,3,2,1,0:T(8,128)(2,1)}), bf16[32,8,2,8,256]{4,3,2,1,0:T(8,128)(2,1)S(1)}, u32[]{:S(2)}, u32[]{:S(2)}) async-start(bf16[32,8,2,8,256]{4,3,2,1,0:T(8,128)(2,1)} %bitcast.30), calls=%async_computation.2 | async-start | bytes 4194304 | tf_op jit(solution)/shard_map/all_to_all | solution.py:329
  170.7 1.4 copy-start

commit v4 on v3

v4 whole, which is shorter than its diff:
```python
import functools

import jax
import jax.numpy as jnp
from jax import lax
from jax.experimental import pallas as pl
from jax.experimental.pallas import tpu as pltpu
from jax.sharding import Mesh
from jax.sharding import PartitionSpec as P

REACH = 2
VMEM = pl.BlockSpec(memory_space=pltpu.VMEM)
SMEM = pl.BlockSpec(memory_space=pltpu.SMEM)


def pack_kernel(x_ref, o_ref, *, flip):
    n, _, _, sr, _ = o_ref.shape
    for r in range(x_ref.shape[0]):
        for s in range(x_ref.shape[1]):
            block = x_ref[r, s].astype(jnp.float32)
            if flip:
                block = block.T
            for u in range(n):
                o_ref[u, r, s] = block[sr * u : sr * u + sr].astype(jnp.bfloat16)


def pack(x, n, flip):
    rows, cols, w, _ = x.shape
    sr = w // n
    step = 2
    return pl.pallas_call(
        functools.partial(pack_kernel, flip=flip),
        grid=(rows // step,),
        in_specs=[pl.BlockSpec((step, cols, w, w), lambda k: (k, 0, 0, 0))],
        out_specs=pl.BlockSpec((n, step, cols, sr, w), lambda k: (0, k, 0, 0, 0)),
        out_shape=jax.ShapeDtypeStruct((n, rows, cols, sr, w), jnp.bfloat16),
        name="pack_flip" if flip else "pack",
    )(x)


def _mirrored(got, split, k, j, i, g_n, s_n):
    at = sum(split[:k])
    parts = split[k]
    g = i // s_n
    return got[at + g * parts // g_n][g % (g_n // parts), j, i % s_n]


def _sym(own, mir):
    return (0.5 * (own.astype(jnp.float32) + mir.astype(jnp.float32))).astype(jnp.bfloat16)


def halo_kernel(z_ref, a_ref, *refs, split):
    got, (lo_ref, hi_ref) = refs[:-2], refs[-2:]
    t_n, g_n, r_n, s_n, _, _ = a_ref.shape
    j_n = g_n * s_n
    for k in range(t_n):
        t = lax.rem(z_ref[0] + (t_n - k), t_n)
        for o_ref, base in ((lo_ref, 0), (hi_ref, j_n - REACH)):
            for c in range(REACH):
                j = base + c
                for i in range(r_n):
                    mir = _mirrored(got, split, k, j, i, g_n, s_n)
                    o_ref[c, t * r_n + i] = _sym(a_ref[t, j // s_n, i, j % s_n], mir)


def _mix(weights_ref, at, x0, x1):
    total = weights_ref[0, at] * x0.astype(jnp.float32)
    return (total + weights_ref[1, at] * x1.astype(jnp.float32)).astype(jnp.bfloat16)


def inner_kernel(
    z_ref, lists_ref, weights_ref, start_ref, a_ref, lo_ref, hi_ref, *refs, split
):
    got, (mid_ref, o_ref, all_ref) = refs[:-3], refs[-3:]
    t_n, g_n, r_n, s_n, _, _ = a_ref.shape
    j_n = g_n * s_n
    start = start_ref[0]
    all_ref[0:REACH] = lo_ref[...]
    all_ref[j_n - REACH :] = hi_ref[...]
    for k in range(t_n):
        t = lax.rem(z_ref[0] + (t_n - k), t_n)
        for j in range(REACH, j_n - REACH):
            for i in range(r_n):
                mir = _mirrored(got, split, k, j, i, g_n, s_n)
                val = _sym(a_ref[t, j // s_n, i, j % s_n], mir)
                all_ref[j, t * r_n + i] = val
                mid_ref[j - REACH, t * r_n + i] = val

    def tile(t, carry):
        for j in range(j_n):
            gj = start + j
            for r in range(r_n):
                i = t * r_n + r
                out = _mix(weights_ref, i, all_ref[j, lists_ref[0, i]], all_ref[j, lists_ref[1, i]])
                if REACH <= j < j_n - REACH:
                    x0 = all_ref[lists_ref[0, gj] - start, i]
                    x1 = all_ref[lists_ref[1, gj] - start, i]
                    col = _mix(weights_ref, gj, x0, x1)
                    out = (out.astype(jnp.float32) + col.astype(jnp.float32)).astype(jnp.bfloat16)
                o_ref[t, j // s_n, r, j % s_n] = out
        return carry

    lax.fori_loop(0, t_n, tile, 0)


def edge_kernel(
    lists_ref, weights_ref, start_ref, left_ref, lo_ref, mid_ref, hi_ref, right_ref, x_ref, o_ref, ext_ref, sems
):
    t_n, _, r_n, s_n, _, _ = o_ref.shape
    k = pl.program_id(0)
    per = REACH // s_n
    start = start_ref[0]
    copies = []
    at = 0
    for ref, q0, n in (
        (left_ref, 0, REACH),
        (lo_ref, 0, REACH),
        (mid_ref, 0, REACH),
        (mid_ref, REACH, REACH),
        (hi_ref, 0, REACH),
        (right_ref, 0, REACH),
    ):
        src = ref.at[pl.ds(q0, n)]
        copies.append(pltpu.make_async_copy(src, ext_ref.at[pl.ds(at, n)], sems.at[len(copies)]))
        at += n

    @pl.when(k == 0)
    def _():
        for c in copies:
            c.start()
        for c in copies[:3]:
            c.wait()

    @pl.when(k == per)
    def _():
        for c in copies[3:]:
            c.wait()

    high = k >= per
    j0 = k * s_n
    gap = mid_ref.shape[0] - 2 * REACH
    gj0 = start + j0 + jnp.where(high, mid_ref.shape[0], 0)
    base = start - REACH + jnp.where(high, gap, 0)

    def tile(t, carry):
        for s in range(s_n):
            gj = gj0 + s
            for r in range(r_n):
                i = t * r_n + r
                col = _mix(
                    weights_ref,
                    gj,
                    ext_ref[lists_ref[0, gj] - base, i],
                    ext_ref[lists_ref[1, gj] - base, i],
                )
                row = x_ref[t, 0, r, s].astype(jnp.float32)
                o_ref[t, 0, r, s] = (row + col.astype(jnp.float32)).astype(jnp.bfloat16)
        return carry

    lax.fori_loop(0, t_n, tile, 0)


def halo_columns(z, own, got):
    t_n, _, r_n, _, sr, sl = own.shape
    split = [len(tile) for tile in got]
    flat = [part for tile in got for part in tile]
    return pl.pallas_call(
        functools.partial(halo_kernel, split=split),
        in_specs=[SMEM, VMEM] + [VMEM] * len(flat),
        out_specs=[VMEM] * 2,
        out_shape=[jax.ShapeDtypeStruct((REACH, t_n * r_n, sr, sl), jnp.bfloat16)] * 2,
        name="halo",
    )(z[None], own, *flat)


def couple_inner(z, lists, weights, start, own, got, low, high):
    t_n, g_n, r_n, s_n, sr, sl = own.shape
    j_n = g_n * s_n
    split = [len(tile) for tile in got]
    flat = [part for tile in got for part in tile]
    columns = lambda n: (n, t_n * r_n, sr, sl)
    return pl.pallas_call(
        functools.partial(inner_kernel, split=split),
        in_specs=[SMEM] * 4 + [VMEM] * (3 + len(flat)),
        out_specs=[VMEM] * 2,
        out_shape=[
            jax.ShapeDtypeStruct(columns(j_n - 2 * REACH), jnp.bfloat16),
            jax.ShapeDtypeStruct(own.shape, jnp.bfloat16),
        ],
        scratch_shapes=[pltpu.VMEM(columns(j_n), jnp.bfloat16)],
        name="inner",
    )(z[None], lists, weights, start, own, low, high, *flat)


def couple_edge(lists, weights, start, left, low, middle, high, right, part):
    t_n, g_n, r_n, s_n, sr, sl = part.shape
    per = REACH // s_n
    i_n = t_n * r_n
    hbm = pl.BlockSpec(memory_space=pl.ANY)
    block = pl.BlockSpec(
        (t_n, 1, r_n, s_n, sr, sl),
        lambda k: (0, k + jnp.where(k >= per, g_n - 2 * per, 0), 0, 0, 0, 0),
    )
    return pl.pallas_call(
        edge_kernel,
        grid=(2 * per,),
        in_specs=[SMEM, SMEM, SMEM] + [hbm] * 5 + [block],
        out_specs=block,
        out_shape=jax.ShapeDtypeStruct(part.shape, jnp.bfloat16),
        scratch_shapes=[
            pltpu.VMEM((6 * REACH, i_n, sr, sl), jnp.bfloat16),
            pltpu.SemaphoreType.DMA((6,)),
        ],
        input_output_aliases={8: 0},
        name="edge",
    )(lists, weights, start, left, low, middle, high, right, part)


def _dot(x, y):
    return jnp.dot(x, y, preferred_element_type=jnp.float32)


def pre_kernel(x_ref, amp_ref, left_ref, right_ref, o_ref):
    left = left_ref[...]
    right = right_ref[...]
    for s in range(amp_ref.shape[1]):
        term = _dot(_dot(left, amp_ref[0, s]).astype(jnp.bfloat16), right)
        o_ref[0, s] = x_ref[0, s].astype(jnp.float32) + term


def add_term(x, amp, left, right):
    rows, cols, w, _ = amp.shape
    big = pl.BlockSpec((1, cols, w, w), lambda k: (k, 0, 0, 0))
    mat = pl.BlockSpec((w, w), lambda k: (0, 0))
    return pl.pallas_call(
        pre_kernel,
        grid=(rows,),
        in_specs=[big, big, mat, mat],
        out_specs=big,
        out_shape=jax.ShapeDtypeStruct(amp.shape, jnp.float32),
        name="term",
    )(x, amp, left, right)


def post_kernel(
    occ_ref,
    base_ref,
    amp_ref,
    mask_i_ref,
    mask_j_ref,
    over_ref,
    trans_ref,
    tt_ref,
    energy_ref,
    coup_ref,
    res_ref,
    new_ref,
):
    k = pl.program_id(0)
    step, cols, w, _ = amp_ref.shape
    rows = pl.num_programs(0) * step
    over = over_ref[...]
    trans = trans_ref[...]
    tt = tt_ref[...]
    pairs = [(r, s) for r in range(step) for s in range(cols)]
    bf = lambda xs: [x.astype(jnp.bfloat16) for x in xs]

    def left(m, xs):
        return [_dot(m, x) for x in xs]

    def right(xs, m):
        return [_dot(x, m) for x in xs]

    two = []
    cm = []
    for r, s in pairs:
        row = jnp.maximum(mask_i_ref[r], mask_j_ref[s])
        two.append(row.T * row)
        coup = coup_ref[:, r, s].astype(jnp.float32).reshape(w, w)
        cm.append(coup * two[-1])
    third = right(bf(left(over, bf(cm))), over)
    res = [m * (base_ref[r, s] - t) for m, t, (r, s) in zip(two, third, pairs)]
    for x, (r, s) in zip(res, pairs):
        res_ref[r, s] = x
    q = right(bf(left(tt, bf(res))), trans)
    energy = energy_ref[...].T + energy_ref[...]
    z = [
        x / (energy - (occ_ref[k * step + r] + occ_ref[rows + s])) for x, (r, s) in zip(q, pairs)
    ]
    u = right(bf(left(trans, bf(z))), tt)
    for x, (r, s) in zip(u, pairs):
        new_ref[r, s] = (amp_ref[r, s].astype(jnp.float32) - x).astype(jnp.bfloat16)


def finish(occ, base, amp, coup, mask_i, mask_j, over, trans, energy):
    rows, cols, w, _ = amp.shape
    n, _, _, sr, _ = coup.shape
    step = 2
    big = pl.BlockSpec((step, cols, w, w), lambda k, *_: (k, 0, 0, 0))
    mat = pl.BlockSpec((w, w), lambda k, *_: (0, 0))
    return pl.pallas_call(
        post_kernel,
        grid_spec=pltpu.PrefetchScalarGridSpec(
            num_scalar_prefetch=1,
            grid=(rows // step,),
            in_specs=[
                big,
                big,
                pl.BlockSpec((step, 1, w), lambda k, *_: (k, 0, 0)),
                pl.BlockSpec((cols, 1, w), lambda k, *_: (0, 0, 0)),
                mat,
                mat,
                mat,
                pl.BlockSpec((1, w), lambda k, *_: (0, 0)),
                pl.BlockSpec((n, step, cols, sr, w), lambda k, *_: (0, k, 0, 0, 0)),
            ],
            out_specs=[big, big],
        ),
        out_shape=[
            jax.ShapeDtypeStruct(amp.shape, jnp.float32),
            jax.ShapeDtypeStruct(amp.shape, jnp.bfloat16),
        ],
        name="finish",
    )(
        occ,
        base,
        amp,
        mask_i[:, None, :],
        mask_j[:, None, :],
        over,
        trans,
        trans.T,
        energy[None, :],
        coup,
    )


def per_device(
    amplitudes,
    exchange,
    fock_virt,
    intersection,
    transform,
    virt_energy,
    occ_energy,
    partners,
    coupling,
    domain,
):
    rows, cols, width, _ = amplitudes.shape
    blocks = domain.shape[1]
    a_n = lax.axis_size("a")
    z_n = lax.axis_size("z")
    g_n = lax.axis_size("g")
    start_i = lax.axis_index("a") * rows
    start_z = lax.axis_index("z") * (g_n * cols)
    start_j = start_z + lax.axis_index("g") * cols
    plane = ("a", "g")
    n = a_n * g_n

    over = (jnp.eye(width, dtype=jnp.float32) + intersection.astype(jnp.float32)).astype(
        jnp.bfloat16
    )
    shape = (a_n, g_n, rows, cols, width // n, width)
    z = lax.axis_index("z")

    def spread(x):
        return lax.all_to_all(x, plane, 0, 0, tiled=True)

    def shift(x, k):
        return lax.ppermute(x, "z", [(q, (q + k) % z_n) for q in range(z_n)])

    part = spread(pack(amplitudes, n, True)).reshape(shape)
    own = pack(amplitudes, n, False)
    tiles = [
        lax.dynamic_index_in_dim(part, lax.rem(z + k, z_n), 0, keepdims=False) for k in range(z_n)
    ]
    half = g_n // 2
    far = z_n // 2
    relay = shift(tiles[far][half:], far + 1)
    got = []
    for k in range(z_n):
        if k == 0:
            got.append([tiles[k]])
        elif k == far:
            got.append([shift(tiles[k][:half], k)])
        else:
            got.append([shift(tiles[k], k)])
    got[far].append(shift(relay, z_n - 1))
    base = add_term(exchange, amplitudes, fock_virt, over)
    base = add_term(base, amplitudes, over, fock_virt)
    own, _ = lax.optimization_barrier((own, tiles[0]))
    own = spread(own).reshape(shape)
    low, high = halo_columns(z, own, got)
    left = lax.ppermute(high, "z", [(k, k + 1) for k in range(z_n - 1)])
    right = lax.ppermute(low, "z", [(k + 1, k) for k in range(z_n - 1)])
    lists = partners.T
    weights = coupling.T
    middle, part = couple_inner(z, lists, weights, start_z[None], own, got, low, high)
    part = couple_edge(lists, weights, start_z[None], left, low, middle, high, right, part)
    coup = spread(part.reshape(n, rows, cols, width // n, width))

    masks = jnp.repeat(domain.astype(jnp.float32), width // blocks, axis=1)
    mask_i = lax.dynamic_slice_in_dim(masks, start_i, rows, 0)
    mask_j = lax.dynamic_slice_in_dim(masks, start_j, cols, 0)
    occ = jnp.concatenate(
        [
            lax.dynamic_slice_in_dim(occ_energy, start_i, rows, 0),
            lax.dynamic_slice_in_dim(occ_energy, start_j, cols, 0),
        ]
    )
    return tuple(
        finish(occ, base, amplitudes, coup, mask_i, mask_j, over, transform, virt_energy)
    )


def solution(mesh):
    i_n, j_n = mesh.shape["occi"], mesh.shape["occj"]
    group = j_n // i_n
    z_n = j_n // group
    inner = Mesh(mesh.devices.reshape(i_n, z_n, group), ("a", "z", "g"))
    pairs = P("a", ("z", "g"), None, None)
    return jax.shard_map(
        per_device,
        mesh=inner,
        in_specs=(pairs, pairs, P(), P(), P(), P(), P(), P(), P(), P()),
        out_specs=(pairs, pairs),
        check_vma=False,
    )
```

time: 185 us -> 184 us (level)
  waiting for transfers between devices: 87.2 us -> 72.7 us
  Pallas kernels: 41.6 us -> 48.8 us
  starting transfers between devices: 43.3 us -> 48.1 us
  local copies, waits for them, and re-layouts: 7.64 us -> 9.5 us
    pallas_call x4 -> x5, Pallas kernels: 23.8 us -> 31.5 us  [the longest x2 16.2 us: add_term(): pl.pallas_call(pre_kernel, grid=(rows,), in_specs=[big, big, mat, mat], o...]
    all_to_all x3, waiting for transfers between devices: 38 us -> 30.3 us  [spread(): return lax.all_to_all(x, plane, 0, 0, tiled=True)]
    ppermute x9, starting transfers between devices: 16.2 us -> 19.6 us  [shift(): return lax.ppermute(x, 'z', [(q, (q + k) % z_n) for q in range(z_n)])]
    ppermute x1, waiting for transfers between devices: 6.75 us -> 3.76 us  [per_device(): right = lax.ppermute(low, 'z', [(k + 1, k) for k in range(z_n - 1)])]
    ppermute x1, waiting for transfers between devices: 2.62 us -> 0.59 us  [per_device(): left = lax.ppermute(high, 'z', [(k, k + 1) for k in range(z_n - 1)])]
    unnamed x37 -> x33, local copies, waits for them, and re-layouts: 5 us -> 5.55 us
  transfers between devices with their start and end apart: 14 -> 14, of which waited for: 8 -> 8; matrix products, arithmetic and copies ran while one was open for 3% -> 3% of each run, Pallas kernels for 10% -> 15%
where the time goes in v4:
time: 184 us; the launch traced here: 181 us
  waiting for transfers between devices  72.7 us (40%)
  Pallas kernels  48.8 us (27%)
  starting transfers between devices  48.1 us (26%)
  local copies, waits for them, and re-layouts  9.5 us (5%)
    ppermute x9, waiting for transfers between devices, shift(): return lax.ppermute(x, 'z', [(q, (q + k) % z_n) for q in range(z_n)])  38 us
    all_to_all x3, waiting for transfers between devices, spread(): return lax.all_to_all(x, plane, 0, 0, tiled=True)  30.3 us
    all_to_all x3, starting transfers between devices, spread(): return lax.all_to_all(x, plane, 0, 0, tiled=True)  25.9 us
    ppermute x9, starting transfers between devices, shift(): return lax.ppermute(x, 'z', [(q, (q + k) % z_n) for q in range(z_n)])  19.6 us
    pallas_call x2, Pallas kernels, add_term(): pl.pallas_call(pre_kernel, grid=(rows,), in_specs=[big, big, mat, mat], o...  16.2 us
    pallas_call x1, Pallas kernels, finish(): pl.pallas_call(post_kernel, grid_spec=pltpu.PrefetchScalarGridSpec(num_sc...  9.31 us
    pallas_call x2, Pallas kernels, pack(): pl.pallas_call(functools.partial(pack_kernel, flip=flip), grid=(rows // s...  7.97 us
    pallas_call x1, Pallas kernels, couple_inner(): pl.pallas_call(functools.partial(inner_kernel, split=split), in_specs=[SM...  7.29 us
  transfers between devices with their start and end apart: 14, of which 8 were waited for; matrix products, arithmetic and copies ran while one was open for 3% of the time, Pallas kernels for 15%

profile of v4, /device:TPU:3, one launch (start us, length us, event | category | flops | bytes accessed | tf_op | source)
XLA Modules:
  0.0 181.3 jit_solution(9227153350096388879)
XLA Ops:
  0.6 4.1 %pack_flip.1 = bf16[32,8,2,8,256]{4,3,2,1,0:T(8,128)(2,1)} custom-call(bf16[8,2,256,256]{3,2,1,0:T(8,128)(2,1)} %amp_ref.5), custom_call_target="tpu_custom_call" | custom-call | tf_op jit(solution)/shard_map/pack_flip/pallas_call | solution.py:31
  4.8 7.9 %all-to-all-start = ((bf16[32,8,2,8,256]{4,3,2,1,0:T(8,128)(2,1)}), bf16[32,8,2,8,256]{4,3,2,1,0:T(8,128)(2,1)S(1)}, u32[]{:S(2)}, u32[]{:S(2)}) async-start(bf16[32,8,2,8,256]{4,3,2,1,0:T(8,128)(2,1)} %pack_flip.1), calls=%async_computation | async-start | bytes 4194304 | tf_op jit(solution)/shard_map/all_to_all | solution.py:368
  12.7 3.8 %pack.1 = bf16[32,8,2,8,256]{4,3,2,1,0:T(8,128)(2,1)} custom-call(bf16[8,2,256,256]{3,2,1,0:T(8,128)(2,1)} %amp_ref.5), custom_call_target="tpu_custom_call" | custom-call | tf_op jit(solution)/shard_map/pack/pallas_call | solution.py:31
  16.6 23.2 %all-to-all-done = bf16[32,8,2,8,256]{4,3,2,1,0:T(8,128)(2,1)S(1)} async-done(((bf16[32,8,2,8,256]{4,3,2,1,0:T(8,128)(2,1)}), bf16[32,8,2,8,256]{4,3,2,1,0:T(8,128)(2,1)S(1)}, u32[]{:S(2)}, u32[]{:S(2)}) %all-to-all-start) | async-done | bytes 2097184 | tf_op jit(solution)/shard_map/all_to_all | solution.py:368
  39.8 1.3 dynamic-slice_bitcast_fusion
  41.1 0.6 copy-done.2
  41.7 7.3 %all-to-all-start.1 = ((bf16[32,8,2,8,256]{4,3,2,1,0:T(8,128)(2,1)}), bf16[32,8,2,8,256]{4,3,2,1,0:T(8,128)(2,1)S(1)}, u32[]{:S(2)}, u32[]{:S(2)}) async-start(bf16[32,8,2,8,256]{4,3,2,1,0:T(8,128)(2,1)} %pack.1), calls=%async_computation.1 | async-start | bytes 4194304 | tf_op jit(solution)/shard_map/all_to_all | solution.py:368
  49.0 5.7 %collective-permute-start.8 = (bf16[4,8,2,8,256]{4,3,2,1,0:T(8,128)(2,1)}, bf16[4,8,2,8,256]{4,3,2,1,0:T(8,128)(2,1)S(1)}, u32[]{:S(2)}, u32[]{:S(2)}) collective-permute-start(bf16[4,8,2,8,256]{4,3,2,1,0:T(8,128)(2,1)} %get-tuple-element.12), channel_id=1, source_target_pairs={{0,28},{4,0},{8,4},{12,8},{16,12},{20,16},{24,20},{28,24},{1,29},{... | collective-permute-start | bytes 786440 | tf_op jit(solution)/shard_map/ppermute | solution.py:371
  54.7 1.0 dynamic-slice_bitcast_fusion.7
  55.7 1.7 collective-permute-start.4
  57.4 0.0 collective-permute-start.3
  57.4 4.5 %collective-permute-start.7 = (bf16[4,8,2,8,256]{4,3,2,1,0:T(8,128)(2,1)}, bf16[4,8,2,8,256]{4,3,2,1,0:T(8,128)(2,1)S(1)}, u32[]{:S(2)}, u32[]{:S(2)}) collective-permute-start(bf16[4,8,2,8,256]{4,3,2,1,0:T(8,128)(2,1)} %get-tuple-element.13), channel_id=1, source_target_pairs={{0,24},{4,28},{8,0},{12,4},{16,8},{20,12},{24,16},{28,20},{1,25},{... | collective-permute-start | bytes 786440 | tf_op jit(solution)/shard_map/ppermute | solution.py:371
  61.9 0.9 collective-permute-start.6
  62.8 10.5 %collective-permute-done.4 = bf16[2,8,2,8,256]{4,3,2,1,0:T(8,128)(2,1)S(1)} collective-permute-done((bf16[2,8,2,8,256]{4,3,2,1,0:T(8,128)(2,1)S(1)}, bf16[2,8,2,8,256]{4,3,2,1,0:T(8,128)(2,1)S(1)}, u32[]{:S(2)}, u32[]{:S(2)}) %collective-permute-start.4) | collective-permute-done | bytes 131104 | tf_op jit(solution)/shard_map/ppermute | solution.py:371
  73.3 0.0 collective-permute-start.2
  73.3 0.0 collective-permute-done.3.refs_4_
  73.3 6.9 %collective-permute-start.1 = (bf16[4,8,2,8,256]{4,3,2,1,0:T(8,128)(2,1)}, bf16[4,8,2,8,256]{4,3,2,1,0:T(8,128)(2,1)S(1)}, u32[]{:S(2)}, u32[]{:S(2)}) collective-permute-start(bf16[4,8,2,8,256]{4,3,2,1,0:T(8,128)(2,1)} %get-tuple-element.16), channel_id=1, source_target_pairs={{0,8},{4,12},{8,16},{12,20},{16,24},{20,28},{24,0},{28,4},{1,9},{5... | collective-permute-start | bytes 786440 | tf_op jit(solution)/shard_map/ppermute | solution.py:371
  80.2 0.0 collective-permute-done.8.refs_8_
  80.2 0.0 collective-permute-start
  80.2 6.2 %collective-permute-done.7.refs_7_ = bf16[4,8,2,8,256]{4,3,2,1,0:T(8,128)(2,1)S(1)} collective-permute-done((bf16[4,8,2,8,256]{4,3,2,1,0:T(8,128)(2,1)}, bf16[4,8,2,8,256]{4,3,2,1,0:T(8,128)(2,1)S(1)}, u32[]{:S(2)}, u32[]{:S(2)}) %collective-permute-start.7) | collective-permute-done | bytes 262176 | tf_op jit(solution)/shard_map/ppermute | solution.py:371
  86.5 0.0 collective-permute-start.5
  86.5 15.8 %collective-permute-done.6.refs_6_ = bf16[4,8,2,8,256]{4,3,2,1,0:T(8,128)(2,1)S(1)} collective-permute-done((bf16[4,8,2,8,256]{4,3,2,1,0:T(8,128)(2,1)}, bf16[4,8,2,8,256]{4,3,2,1,0:T(8,128)(2,1)S(1)}, u32[]{:S(2)}, u32[]{:S(2)}) %collective-permute-start.6) | collective-permute-done | bytes 262176 | tf_op jit(solution)/shard_map/ppermute | solution.py:371
  102.3 0.0 collective-permute-done.2.refs_3_
  102.3 0.0 collective-permute-done.1.refs_2_
  102.3 0.0 copy-start.7
  102.3 5.4 %collective-permute-done.refs_1_ = bf16[4,8,2,8,256]{4,3,2,1,0:T(8,128)(2,1)S(1)} collective-permute-done((bf16[4,8,2,8,256]{4,3,2,1,0:T(8,128)(2,1)}, bf16[4,8,2,8,256]{4,3,2,1,0:T(8,128)(2,1)S(1)}, u32[]{:S(2)}, u32[]{:S(2)}) %collective-permute-start) | collective-permute-done | bytes 262176 | tf_op jit(solution)/shard_map/ppermute | solution.py:371
  107.7 0.7 copy-done.8
  108.4 0.0 collective-permute-done.5.refs_5_
  108.4 0.0 all-to-all-done.1
  108.4 0.0 copy-done.10
  108.4 0.0 copy-done.3
  108.4 0.0 copy-done.4
  108.4 0.0 copy-done.5
  108.5 0.0 copy-done.6
  108.5 0.0 copy-done.7
  108.5 1.3 copy-done
  109.7 3.4 %halo.1 = (bf16[2,64,8,256]{3,2,1,0:T(8,128)(2,1)}, bf16[2,64,8,256]{3,2,1,0:T(8,128)(2,1)}) custom-call(s32[1]{0:T(128)} %bitcast.8.z_ref, bf16[8,4,8,2,8,256]{5,4,3,2,1,0:T(8,128)(2,1)} %bitcast.32, bf16[4,8,2,8,256]{4,3,2,1,0:T(8,128)(2,1)} %get-tuple-element.18.refs_0_, bf16[4,8,2,8,256]{4,3,2,1,0:T(8,128)(2,1)} %copy-done.8, ...), custom_call_target="tpu_custom_call" | custom-call | tf_op jit(solution)/shard_map/halo/pallas_call | solution.py:167
  113.1 1.3 collective-permute-start.9
  114.5 1.3 collective-permute-start.10
  115.8 7.3 %inner.1 = (bf16[4,64,8,256]{3,2,1,0:T(8,128)(2,1)}, bf16[8,4,8,2,8,256]{5,4,3,2,1,0:T(8,128)(2,1)}) custom-call(s32[1]{0:T(128)} %bitcast.8.z_ref, s32[2,64]{1,0:T(2,128)} %bitcast.40, f32[2,64]{1,0:T(2,128)} %bitcast.42, s32[1]{0:T(128)} %bitcast.7.start_ref, bf16[8,4,8,2,8,256]{5,4,3,2,1,0:T(8,128)(2,1)} %bitcast.33, ...), custom_call_target="tpu_custom_call" | custom-call | tf_op jit(solution)/shard_map/inner/pallas_call | solution.py:182
  123.1 0.6 collective-permute-done.9.left_ref
  123.6 3.8 %collective-permute-done.10.right_ref = bf16[2,64,8,256]{3,2,1,0:T(8,128)(2,1)S(1)} collective-permute-done((bf16[2,64,8,256]{3,2,1,0:T(8,128)(2,1)}, bf16[2,64,8,256]{3,2,1,0:T(8,128)(2,1)S(1)}, u32[]{:S(2)}, u32[]{:S(2)}) %collective-permute-start.10) | collective-permute-done | bytes 524320 | tf_op jit(solution)/shard_map/ppermute | solution.py:396
  127.4 0.0 copy-done.11
  127.4 0.8 copy-done.12
  128.2 4.6 %edge.1 = bf16[8,4,8,2,8,256]{5,4,3,2,1,0:T(8,128)(2,1)} custom-call(s32[2,64]{1,0:T(2,128)} %bitcast.41, f32[2,64]{1,0:T(2,128)} %bitcast.43, s32[1]{0:T(128)} %bitcast.7.start_ref, bf16[2,64,8,256]{3,2,1,0:T(8,128)(2,1)} %copy-done.11, bf16[2,64,8,256]{3,2,1,0:T(8,128)(2,1)} %get-tuple-element.9.lo_ref, ...), custom_call_target="tpu_custom_call", output_to_operand_aliasing={{}: (8, {})} | custom-call | tf_op jit(solution)/shard_map/edge/pallas_call | solution.py:204
  132.8 0.0 copy-start.15
  132.8 0.0 copy-start.14
  132.8 0.0 copy-start.9
  132.9 0.0 copy-start.13
  132.9 10.6 %all-to-all-start.2 = ((bf16[32,8,2,8,256]{4,3,2,1,0:T(8,128)(2,1)}), bf16[32,8,2,8,256]{4,3,2,1,0:T(8,128)(2,1)S(1)}, u32[]{:S(2)}, u32[]{:S(2)}) async-start(bf16[32,8,2,8,256]{4,3,2,1,0:T(8,128)(2,1)} %bitcast.36), calls=%async_computation.2 | async-start | bytes 4194304 | tf_op jit(solution)/shard_map/all_to_all | solution.py:368
  143.5 0.1 dynamic_slice.38
  143.6 0.1 dynamic_slice.37
  143.7 0.1 dynamic-slice_bitcast_fusion.9
  143.8 0.7 copy.19.mask_j_ref
  144.4 0.1 dynamic-slice_bitcast_fusion.10
  144.5 0.7 copy.18.mask_i_ref
  145.2 0.7 copy.17
  146.0 0.7 add_convert_fusion.right_ref.left_ref.over_ref
  146.6 7.9 %term.2.x_ref = f32[8,2,256,256]{3,2,1,0:T(8,128)} custom-call(bf16[8,2,256,256]{3,2,1,0:T(8,128)(2,1)} %x_ref.3, bf16[8,2,256,256]{3,2,1,0:T(8,128)(2,1)} %amp_ref.5, bf16[256,256]{1,0:T(8,128)(2,1)} %right_ref.1, bf16[256,256]{1,0:T(8,128)(2,1)} %add_convert_fusion.right_ref.left_ref.over_ref), custom_call_target="tpu_custom_call" | custom-call | tf_op jit(solution)/shard_map/term/pallas_call | solution.py:235
  154.5 8.3 %term.3.base_ref = f32[8,2,256,256]{3,2,1,0:T(8,128)} custom-call(f32[8,2,256,256]{3,2,1,0:T(8,128)} %term.2.x_ref, bf16[8,2,256,256]{3,2,1,0:T(8,128)(2,1)} %amp_ref.5, bf16[256,256]{1,0:T(8,128)(2,1)} %add_convert_fusion.right_ref.left_ref.over_ref, bf16[256,256]{1,0:T(8,128)(2,1)} %right_ref.1), custom_call_target="tpu_custom_call" | custom-call | tf_op jit(solution)/shard_map/term/pallas_call | solution.py:235
  162.9 0.6 pad_maximum_fusion.occ_ref
  163.5 7.1 %all-to-all-done.2.coup_ref = bf16[32,8,2,8,256]{4,3,2,1,0:T(8,128)(2,1)S(1)} async-done(((bf16[32,8,2,8,256]{4,3,2,1,0:T(8,128)(2,1)}), bf16[32,8,2,8,256]{4,3,2,1,0:T(8,128)(2,1)S(1)}, u32[]{:S(2)}, u32[]{:S(2)}) %all-to-all-start.2) | async-done | bytes 2097184 | tf_op jit(solution)/shard_map/all_to_all | solution.py:368
  170.6 1.4 copy-done.1
  172.0 9.3 %finish.1 = (f32[8,2,256,256]{3,2,1,0:T(8,128)}, bf16[8,2,256,256]{3,2,1,0:T(8,128)(2,1)}) custom-call(f32[10]{0:T(128)} %pad_maximum_fusion.occ_ref, f32[8,2,256,256]{3,2,1,0:T(8,128)} %term.3.base_ref, bf16[8,2,256,256]{3,2,1,0:T(8,128)(2,1)} %amp_ref.5, f32[8,1,256]{2,1,0:T(1,128)} %copy.18.mask_i_ref, f32[2,1,256]{2,1,0:T(1,128)} %copy.19.mask_j_ref, ...), custom_call_target="tpu_custom_call" | custom-call | tf_op jit(solution)/shard_map/finish/pallas_call | solution.py:301
  (17 shorter events, 0.0 us)
Async XLA Ops:
  4.8 35.0 %all-to-all-start = ((bf16[32,8,2,8,256]{4,3,2,1,0:T(8,128)(2,1)}), bf16[32,8,2,8,256]{4,3,2,1,0:T(8,128)(2,1)S(1)}, u32[]{:S(2)}, u32[]{:S(2)}) async-start(bf16[32,8,2,8,256]{4,3,2,1,0:T(8,128)(2,1)} %pack_flip.1), calls=%async_computation | async-start | bytes 4194304 | tf_op jit(solution)/shard_map/all_to_all | solution.py:368
  39.8 1.9 %copy-start.2 = (bf16[32,8,2,8,256]{4,3,2,1,0:T(8,128)(2,1)}, bf16[32,8,2,8,256]{4,3,2,1,0:T(8,128)(2,1)S(1)}, u32[]{:S(2)}) copy-start(bf16[32,8,2,8,256]{4,3,2,1,0:T(8,128)(2,1)S(1)} %all-to-all-done) | copy-start | bytes 6291460
  41.7 66.7 %all-to-all-start.1 = ((bf16[32,8,2,8,256]{4,3,2,1,0:T(8,128)(2,1)}), bf16[32,8,2,8,256]{4,3,2,1,0:T(8,128)(2,1)S(1)}, u32[]{:S(2)}, u32[]{:S(2)}) async-start(bf16[32,8,2,8,256]{4,3,2,1,0:T(8,128)(2,1)} %pack.1), calls=%async_computation.1 | async-start | bytes 4194304 | tf_op jit(solution)/shard_map/all_to_all | solution.py:368
  49.0 31.1 %collective-permute-start.8 = (bf16[4,8,2,8,256]{4,3,2,1,0:T(8,128)(2,1)}, bf16[4,8,2,8,256]{4,3,2,1,0:T(8,128)(2,1)S(1)}, u32[]{:S(2)}, u32[]{:S(2)}) collective-permute-start(bf16[4,8,2,8,256]{4,3,2,1,0:T(8,128)(2,1)} %get-tuple-element.12), channel_id=1, source_target_pairs={{0,28},{4,0},{8,4},{12,8},{16,12},{20,16},{24,20},{28,24},{1,29},{... | collective-permute-start | bytes 786440 | tf_op jit(solution)/shard_map/ppermute | solution.py:371
  55.7 17.6 %collective-permute-start.4 = (bf16[2,8,2,8,256]{4,3,2,1,0:T(8,128)(2,1)S(1)}, bf16[2,8,2,8,256]{4,3,2,1,0:T(8,128)(2,1)S(1)}, u32[]{:S(2)}, u32[]{:S(2)}) collective-permute-start(bf16[2,8,2,8,256]{4,3,2,1,0:T(8,128)(2,1)S(1)} %get-tuple-element.19), channel_id=1, source_target_pairs={{0,20},{4,24},{8,28},{12,0},{16,4},{20,8},{24,12},{28,16},{1,21},{... | collective-permute-start | bytes 393224 | tf_op jit(solution)/shard_map/ppermute | solution.py:371
  57.4 15.9 %collective-permute-start.3 = (bf16[2,8,2,8,256]{4,3,2,1,0:T(8,128)(2,1)S(1)}, bf16[2,8,2,8,256]{4,3,2,1,0:T(8,128)(2,1)S(1)}, u32[]{:S(2)}, u32[]{:S(2)}) collective-permute-start(bf16[2,8,2,8,256]{4,3,2,1,0:T(8,128)(2,1)S(1)} %get-tuple-element.20), channel_id=1, source_target_pairs={{0,16},{4,20},{8,24},{12,28},{16,0},{20,4},{24,8},{28,12},{1,17},{... | collective-permute-start | bytes 393224 | tf_op jit(solution)/shard_map/ppermute | solution.py:371
  57.4 29.1 %collective-permute-start.7 = (bf16[4,8,2,8,256]{4,3,2,1,0:T(8,128)(2,1)}, bf16[4,8,2,8,256]{4,3,2,1,0:T(8,128)(2,1)S(1)}, u32[]{:S(2)}, u32[]{:S(2)}) collective-permute-start(bf16[4,8,2,8,256]{4,3,2,1,0:T(8,128)(2,1)} %get-tuple-element.13), channel_id=1, source_target_pairs={{0,24},{4,28},{8,0},{12,4},{16,8},{20,12},{24,16},{28,20},{1,25},{... | collective-permute-start | bytes 786440 | tf_op jit(solution)/shard_map/ppermute | solution.py:371
  61.9 40.4 %collective-permute-start.6 = (bf16[4,8,2,8,256]{4,3,2,1,0:T(8,128)(2,1)}, bf16[4,8,2,8,256]{4,3,2,1,0:T(8,128)(2,1)S(1)}, u32[]{:S(2)}, u32[]{:S(2)}) collective-permute-start(bf16[4,8,2,8,256]{4,3,2,1,0:T(8,128)(2,1)} %get-tuple-element.14), channel_id=1, source_target_pairs={{0,20},{4,24},{8,28},{12,0},{16,4},{20,8},{24,12},{28,16},{1,21},{... | collective-permute-start | bytes 786440 | tf_op jit(solution)/shard_map/ppermute | solution.py:371
  73.3 29.0 %collective-permute-start.2 = (bf16[4,8,2,8,256]{4,3,2,1,0:T(8,128)(2,1)}, bf16[4,8,2,8,256]{4,3,2,1,0:T(8,128)(2,1)S(1)}, u32[]{:S(2)}, u32[]{:S(2)}) collective-permute-start(bf16[4,8,2,8,256]{4,3,2,1,0:T(8,128)(2,1)} %get-tuple-element.15), channel_id=1, source_target_pairs={{0,12},{4,16},{8,20},{12,24},{16,28},{20,0},{24,4},{28,8},{1,13},{... | collective-permute-start | bytes 786440 | tf_op jit(solution)/shard_map/ppermute | solution.py:371
  73.3 35.1 %copy-start.10 = (bf16[2,8,2,8,256]{4,3,2,1,0:T(8,128)(2,1)}, bf16[2,8,2,8,256]{4,3,2,1,0:T(8,128)(2,1)S(1)}, u32[]{:S(2)}) copy-start(bf16[2,8,2,8,256]{4,3,2,1,0:T(8,128)(2,1)S(1)} %collective-permute-done.3.refs_4_) | copy-start | bytes 393220
  73.3 29.0 %collective-permute-start.1 = (bf16[4,8,2,8,256]{4,3,2,1,0:T(8,128)(2,1)}, bf16[4,8,2,8,256]{4,3,2,1,0:T(8,128)(2,1)S(1)}, u32[]{:S(2)}, u32[]{:S(2)}) collective-permute-start(bf16[4,8,2,8,256]{4,3,2,1,0:T(8,128)(2,1)} %get-tuple-element.16), channel_id=1, source_target_pairs={{0,8},{4,12},{8,16},{12,20},{16,24},{20,28},{24,0},{28,4},{1,9},{5... | collective-permute-start | bytes 786440 | tf_op jit(solution)/shard_map/ppermute | solution.py:371
  80.2 28.2 %copy-start.3 = (bf16[4,8,2,8,256]{4,3,2,1,0:T(8,128)(2,1)}, bf16[4,8,2,8,256]{4,3,2,1,0:T(8,128)(2,1)S(1)}, u32[]{:S(2)}) copy-start(bf16[4,8,2,8,256]{4,3,2,1,0:T(8,128)(2,1)S(1)} %collective-permute-done.8.refs_8_) | copy-start | bytes 786436
  80.2 27.5 %collective-permute-start = (bf16[4,8,2,8,256]{4,3,2,1,0:T(8,128)(2,1)}, bf16[4,8,2,8,256]{4,3,2,1,0:T(8,128)(2,1)S(1)}, u32[]{:S(2)}, u32[]{:S(2)}) collective-permute-start(bf16[4,8,2,8,256]{4,3,2,1,0:T(8,128)(2,1)} %get-tuple-element.17), channel_id=1, source_target_pairs={{0,4},{4,8},{8,12},{12,16},{16,20},{20,24},{24,28},{28,0},{1,5},{5... | collective-permute-start | bytes 786440 | tf_op jit(solution)/shard_map/ppermute | solution.py:371
  86.4 22.0 %copy-start.4 = (bf16[4,8,2,8,256]{4,3,2,1,0:T(8,128)(2,1)}, bf16[4,8,2,8,256]{4,3,2,1,0:T(8,128)(2,1)S(1)}, u32[]{:S(2)}) copy-start(bf16[4,8,2,8,256]{4,3,2,1,0:T(8,128)(2,1)S(1)} %collective-permute-done.7.refs_7_) | copy-start | bytes 786436
  86.5 22.0 %collective-permute-start.5 = (bf16[2,8,2,8,256]{4,3,2,1,0:T(8,128)(2,1)S(1)}, bf16[2,8,2,8,256]{4,3,2,1,0:T(8,128)(2,1)}, u32[]{:S(2)}, u32[]{:S(2)}) collective-permute-start(bf16[2,8,2,8,256]{4,3,2,1,0:T(8,128)(2,1)S(1)} %collective-permute-done.4), channel_id=1, source_target_pairs={{0,28},{4,0},{8,4},{12,8},{16,12},{20,16},{24,20},{28,24},{1,29},{... | collective-permute-start | bytes 393224 | tf_op jit(solution)/shard_map/ppermute | solution.py:371
  102.3 6.2 %copy-start.5 = (bf16[4,8,2,8,256]{4,3,2,1,0:T(8,128)(2,1)}, bf16[4,8,2,8,256]{4,3,2,1,0:T(8,128)(2,1)S(1)}, u32[]{:S(2)}) copy-start(bf16[4,8,2,8,256]{4,3,2,1,0:T(8,128)(2,1)S(1)} %collective-permute-done.6.refs_6_) | copy-start | bytes 786436
  102.3 6.2 %copy-start.6 = (bf16[4,8,2,8,256]{4,3,2,1,0:T(8,128)(2,1)}, bf16[4,8,2,8,256]{4,3,2,1,0:T(8,128)(2,1)S(1)}, u32[]{:S(2)}) copy-start(bf16[4,8,2,8,256]{4,3,2,1,0:T(8,128)(2,1)S(1)} %collective-permute-done.2.refs_3_) | copy-start | bytes 786436
  102.3 6.2 %copy-start.7 = (bf16[4,8,2,8,256]{4,3,2,1,0:T(8,128)(2,1)}, bf16[4,8,2,8,256]{4,3,2,1,0:T(8,128)(2,1)S(1)}, u32[]{:S(2)}) copy-start(bf16[4,8,2,8,256]{4,3,2,1,0:T(8,128)(2,1)S(1)} %collective-permute-done.1.refs_2_) | copy-start | bytes 786436
  107.7 0.7 copy-start.8
  108.4 1.3 copy-start
  113.1 10.5 %collective-permute-start.9 = (bf16[2,64,8,256]{3,2,1,0:T(8,128)(2,1)}, bf16[2,64,8,256]{3,2,1,0:T(8,128)(2,1)S(1)}, u32[]{:S(2)}, u32[]{:S(2)}) collective-permute-start(bf16[2,64,8,256]{3,2,1,0:T(8,128)(2,1)} %get-tuple-element.8.hi_ref), channel_id=1, source_target_pairs={{0,4},{4,8},{8,12},{12,16},{16,20},{20,24},{24,28},{1,5},{5,9},{9,... | collective-permute-start | bytes 1572872 | tf_op jit(solution)/shard_map/ppermute | solution.py:395
  114.5 12.9 %collective-permute-start.10 = (bf16[2,64,8,256]{3,2,1,0:T(8,128)(2,1)}, bf16[2,64,8,256]{3,2,1,0:T(8,128)(2,1)S(1)}, u32[]{:S(2)}, u32[]{:S(2)}) collective-permute-start(bf16[2,64,8,256]{3,2,1,0:T(8,128)(2,1)} %get-tuple-element.9.lo_ref), channel_id=1, source_target_pairs={{4,0},{8,4},{12,8},{16,12},{20,16},{24,20},{28,24},{5,1},{9,5},{13... | collective-permute-start | bytes 1572872 | tf_op jit(solution)/shard_map/ppermute | solution.py:396
  123.6 3.8 %copy-start.11 = (bf16[2,64,8,256]{3,2,1,0:T(8,128)(2,1)}, bf16[2,64,8,256]{3,2,1,0:T(8,128)(2,1)S(1)}, u32[]{:S(2)}) copy-start(bf16[2,64,8,256]{3,2,1,0:T(8,128)(2,1)S(1)} %collective-permute-done.9.left_ref) | copy-start | bytes 1572868
  127.4 0.8 copy-start.12
  132.8 10.7 %copy-start.15 = (f32[64]{0:T(128)S(1)}, f32[64]{0:T(128)}, u32[]{:S(2)}) copy-start(f32[64]{0:T(128)} %param.16) | copy-start | bytes 772
  132.8 10.8 %copy-start.14 = (s32[64,8]{0,1:T(8,128)S(1)}, s32[64,8]{0,1:T(8,128)}, u32[]{:S(2)}) copy-start(s32[64,8]{0,1:T(8,128)} %param.19) | copy-start | bytes 6148
  132.8 12.4 %copy-start.9 = (bf16[256,256]{1,0:T(8,128)(2,1)S(1)}, bf16[256,256]{1,0:T(8,128)(2,1)}, u32[]{:S(2)}) copy-start(bf16[256,256]{1,0:T(8,128)(2,1)} %trans_ref.1) | copy-start | bytes 393220
  132.9 13.1 %copy-start.13 = (bf16[256,256]{1,0:T(8,128)(2,1)S(1)}, bf16[256,256]{1,0:T(8,128)(2,1)}, u32[]{:S(2)}) copy-start(bf16[256,256]{1,0:T(8,128)(2,1)} %param.13) | copy-start | bytes 393220
  132.9 37.7 %all-to-all-start.2 = ((bf16[32,8,2,8,256]{4,3,2,1,0:T(8,128)(2,1)}), bf16[32,8,2,8,256]{4,3,2,1,0:T(8,128)(2,1)S(1)}, u32[]{:S(2)}, u32[]{:S(2)}) async-start(bf16[32,8,2,8,256]{4,3,2,1,0:T(8,128)(2,1)} %bitcast.36), calls=%async_computation.2 | async-start | bytes 4194304 | tf_op jit(solution)/shard_map/all_to_all | solution.py:368
  170.6 1.4 copy-start.1

commit v5 on v4

--- a/solution.py
+++ b/solution.py
@@ -13,21 +13,24 @@
 SMEM = pl.BlockSpec(memory_space=pltpu.SMEM)
 
 
+def near(x):
+    return pltpu.with_memory_space_constraint(x, pltpu.VMEM)
+
+
 def pack_kernel(x_ref, o_ref, *, flip):
-    n, _, _, sr, _ = o_ref.shape
+    n, _, _, sr, w = o_ref.shape
     for r in range(x_ref.shape[0]):
         for s in range(x_ref.shape[1]):
-            block = x_ref[r, s].astype(jnp.float32)
+            block = x_ref[r, s]
             if flip:
                 block = block.T
-            for u in range(n):
-                o_ref[u, r, s] = block[sr * u : sr * u + sr].astype(jnp.bfloat16)
+            o_ref[:, r, s] = block.reshape(n, sr, w)
 
 
 def pack(x, n, flip):
     rows, cols, w, _ = x.shape
     sr = w // n
-    step = 2
+    step = 4
     return pl.pallas_call(
         functools.partial(pack_kernel, flip=flip),
         grid=(rows // step,),
@@ -204,7 +207,7 @@
     return pl.pallas_call(
         edge_kernel,
         grid=(2 * per,),
-        in_specs=[SMEM, SMEM, SMEM] + [hbm] * 5 + [block],
+        in_specs=[SMEM, SMEM, SMEM, VMEM, hbm, hbm, hbm, VMEM, block],
         out_specs=block,
         out_shape=jax.ShapeDtypeStruct(part.shape, jnp.bfloat16),
         scratch_shapes=[
@@ -276,7 +279,7 @@
     for r, s in pairs:
         row = jnp.maximum(mask_i_ref[r], mask_j_ref[s])
         two.append(row.T * row)
-        coup = coup_ref[:, r, s].astype(jnp.float32).reshape(w, w)
+        coup = coup_ref[:, k * step + r, s].astype(jnp.float32).reshape(w, w)
         cm.append(coup * two[-1])
     third = right(bf(left(over, bf(cm))), over)
     res = [m * (base_ref[r, s] - t) for m, t, (r, s) in zip(two, third, pairs)]
@@ -294,7 +297,6 @@
 
 def finish(occ, base, amp, coup, mask_i, mask_j, over, trans, energy):
     rows, cols, w, _ = amp.shape
-    n, _, _, sr, _ = coup.shape
     step = 2
     big = pl.BlockSpec((step, cols, w, w), lambda k, *_: (k, 0, 0, 0))
     mat = pl.BlockSpec((w, w), lambda k, *_: (0, 0))
@@ -312,7 +314,7 @@
                 mat,
                 mat,
                 pl.BlockSpec((1, w), lambda k, *_: (0, 0)),
-                pl.BlockSpec((n, step, cols, sr, w), lambda k, *_: (0, k, 0, 0, 0)),
+                VMEM,
             ],
             out_specs=[big, big],
         ),
@@ -390,15 +392,15 @@
     base = add_term(exchange, amplitudes, fock_virt, over)
     base = add_term(base, amplitudes, over, fock_virt)
     own, _ = lax.optimization_barrier((own, tiles[0]))
-    own = spread(own).reshape(shape)
+    own = near(spread(own).reshape(shape))
     low, high = halo_columns(z, own, got)
     left = lax.ppermute(high, "z", [(k, k + 1) for k in range(z_n - 1)])
     right = lax.ppermute(low, "z", [(k + 1, k) for k in range(z_n - 1)])
     lists = partners.T
     weights = coupling.T
     middle, part = couple_inner(z, lists, weights, start_z[None], own, got, low, high)
-    part = couple_edge(lists, weights, start_z[None], left, low, middle, high, right, part)
-    coup = spread(part.reshape(n, rows, cols, width // n, width))
+    part = couple_edge(lists, weights, start_z[None], near(left), low, middle, high, near(right), part)
+    coup = near(spread(part.reshape(n, rows, cols, width // n, width)))
 
     masks = jnp.repeat(domain.astype(jnp.float32), width // blocks, axis=1)
     mask_i = lax.dynamic_slice_in_dim(masks, start_i, rows, 0)

time: 184 us -> 179 us (0.973)
  Pallas kernels: 48.8 us -> 44.8 us
  local copies, waits for them, and re-layouts: 9.5 us -> 6.13 us
  waiting for transfers between devices: 72.7 us -> 74.6 us
    unnamed x33 -> x25, local copies, waits for them, and re-layouts: 5.55 us -> 2.13 us
    pallas_call x2, Pallas kernels: 7.97 us -> 5.59 us  [pack(): pl.pallas_call(functools.partial(pack_kernel, flip=flip), grid=(rows // s...]
  transfers between devices with their start and end apart: 14 -> 14, of which waited for: 8 -> 8; matrix products, arithmetic and copies ran while one was open for 3% -> 3% of each run, Pallas kernels for 15% -> 14%
where the time goes in v5:
time: 179 us; the launch traced here: 176 us
  waiting for transfers between devices  74.6 us (42%)
  starting transfers between devices  48.1 us (27%)
  Pallas kernels  44.8 us (25%)
  local copies, waits for them, and re-layouts  6.13 us (3%)
    ppermute x9, waiting for transfers between devices, shift(): return lax.ppermute(x, 'z', [(q, (q + k) % z_n) for q in range(z_n)])  38 us
    all_to_all x3, waiting for transfers between devices, spread(): return lax.all_to_all(x, plane, 0, 0, tiled=True)  31.5 us
    all_to_all x3, starting transfers between devices, spread(): return lax.all_to_all(x, plane, 0, 0, tiled=True)  25.9 us
    ppermute x9, starting transfers between devices, shift(): return lax.ppermute(x, 'z', [(q, (q + k) % z_n) for q in range(z_n)])  19.6 us
    pallas_call x2, Pallas kernels, add_term(): pl.pallas_call(pre_kernel, grid=(rows,), in_specs=[big, big, mat, mat], o...  16.2 us
    pallas_call x1, Pallas kernels, finish(): pl.pallas_call(post_kernel, grid_spec=pltpu.PrefetchScalarGridSpec(num_sc...  9.12 us
    pallas_call x1, Pallas kernels, couple_inner(): pl.pallas_call(functools.partial(inner_kernel, split=split), in_specs=[SM...  6.6 us
    pallas_call x2, Pallas kernels, pack(): pl.pallas_call(functools.partial(pack_kernel, flip=flip), grid=(rows // s...  5.59 us
  transfers between devices with their start and end apart: 14, of which 8 were waited for; matrix products, arithmetic and copies ran while one was open for 3% of the time, Pallas kernels for 14%

profile of v5, /device:TPU:3, one launch (start us, length us, event | category | flops | bytes accessed | tf_op | source)
XLA Modules:
  0.0 175.7 jit_solution(16406112913939151949)
XLA Ops:
  0.6 2.9 %pack_flip.1 = bf16[32,8,2,8,256]{4,3,2,1,0:T(8,128)(2,1)} custom-call(bf16[8,2,256,256]{3,2,1,0:T(8,128)(2,1)} %amp_ref.5), custom_call_target="tpu_custom_call" | custom-call | tf_op jit(solution)/shard_map/pack_flip/pallas_call | solution.py:34
  3.5 7.9 %all-to-all-start = ((bf16[32,8,2,8,256]{4,3,2,1,0:T(8,128)(2,1)}), bf16[32,8,2,8,256]{4,3,2,1,0:T(8,128)(2,1)S(1)}, u32[]{:S(2)}, u32[]{:S(2)}) async-start(bf16[32,8,2,8,256]{4,3,2,1,0:T(8,128)(2,1)} %pack_flip.1), calls=%async_computation | async-start | bytes 4194304 | tf_op jit(solution)/shard_map/all_to_all | solution.py:370
  11.5 2.7 %pack.1 = bf16[32,8,2,8,256]{4,3,2,1,0:T(8,128)(2,1)} custom-call(bf16[8,2,256,256]{3,2,1,0:T(8,128)(2,1)} %amp_ref.5), custom_call_target="tpu_custom_call" | custom-call | tf_op jit(solution)/shard_map/pack/pallas_call | solution.py:34
  14.2 24.4 %all-to-all-done = bf16[32,8,2,8,256]{4,3,2,1,0:T(8,128)(2,1)S(1)} async-done(((bf16[32,8,2,8,256]{4,3,2,1,0:T(8,128)(2,1)}), bf16[32,8,2,8,256]{4,3,2,1,0:T(8,128)(2,1)S(1)}, u32[]{:S(2)}, u32[]{:S(2)}) %all-to-all-start) | async-done | bytes 2097184 | tf_op jit(solution)/shard_map/all_to_all | solution.py:370
  38.6 1.3 dynamic-slice_bitcast_fusion
  39.9 0.6 copy-done
  40.5 7.3 %all-to-all-start.1 = ((bf16[32,8,2,8,256]{4,3,2,1,0:T(8,128)(2,1)}), bf16[32,8,2,8,256]{4,3,2,1,0:T(8,128)(2,1)S(1)}, u32[]{:S(2)}, u32[]{:S(2)}) async-start(bf16[32,8,2,8,256]{4,3,2,1,0:T(8,128)(2,1)} %pack.1), calls=%async_computation.1 | async-start | bytes 4194304 | tf_op jit(solution)/shard_map/all_to_all | solution.py:370
  47.8 5.7 %collective-permute-start.8 = (bf16[4,8,2,8,256]{4,3,2,1,0:T(8,128)(2,1)}, bf16[4,8,2,8,256]{4,3,2,1,0:T(8,128)(2,1)S(1)}, u32[]{:S(2)}, u32[]{:S(2)}) collective-permute-start(bf16[4,8,2,8,256]{4,3,2,1,0:T(8,128)(2,1)} %get-tuple-element.12), channel_id=1, source_target_pairs={{0,28},{4,0},{8,4},{12,8},{16,12},{20,16},{24,20},{28,24},{1,29},{... | collective-permute-start | bytes 786440 | tf_op jit(solution)/shard_map/ppermute | solution.py:373
  53.5 1.0 dynamic-slice_bitcast_fusion.7
  54.5 1.7 collective-permute-start.4
  56.2 0.0 collective-permute-start.3
  56.2 4.5 %collective-permute-start.7 = (bf16[4,8,2,8,256]{4,3,2,1,0:T(8,128)(2,1)}, bf16[4,8,2,8,256]{4,3,2,1,0:T(8,128)(2,1)S(1)}, u32[]{:S(2)}, u32[]{:S(2)}) collective-permute-start(bf16[4,8,2,8,256]{4,3,2,1,0:T(8,128)(2,1)} %get-tuple-element.13), channel_id=1, source_target_pairs={{0,24},{4,28},{8,0},{12,4},{16,8},{20,12},{24,16},{28,20},{1,25},{... | collective-permute-start | bytes 786440 | tf_op jit(solution)/shard_map/ppermute | solution.py:373
  60.6 0.9 collective-permute-start.6
  61.6 10.5 %collective-permute-done.4 = bf16[2,8,2,8,256]{4,3,2,1,0:T(8,128)(2,1)S(1)} collective-permute-done((bf16[2,8,2,8,256]{4,3,2,1,0:T(8,128)(2,1)S(1)}, bf16[2,8,2,8,256]{4,3,2,1,0:T(8,128)(2,1)S(1)}, u32[]{:S(2)}, u32[]{:S(2)}) %collective-permute-start.4) | collective-permute-done | bytes 131104 | tf_op jit(solution)/shard_map/ppermute | solution.py:373
  72.1 0.0 collective-permute-start.2
  72.1 0.0 collective-permute-done.3.refs_4_
  72.1 6.9 %collective-permute-start.1 = (bf16[4,8,2,8,256]{4,3,2,1,0:T(8,128)(2,1)}, bf16[4,8,2,8,256]{4,3,2,1,0:T(8,128)(2,1)S(1)}, u32[]{:S(2)}, u32[]{:S(2)}) collective-permute-start(bf16[4,8,2,8,256]{4,3,2,1,0:T(8,128)(2,1)} %get-tuple-element.16), channel_id=1, source_target_pairs={{0,8},{4,12},{8,16},{12,20},{16,24},{20,28},{24,0},{28,4},{1,9},{5... | collective-permute-start | bytes 786440 | tf_op jit(solution)/shard_map/ppermute | solution.py:373
  79.0 0.0 collective-permute-done.8.refs_8_
  79.0 0.0 collective-permute-start
  79.0 6.2 %collective-permute-done.7.refs_7_ = bf16[4,8,2,8,256]{4,3,2,1,0:T(8,128)(2,1)S(1)} collective-permute-done((bf16[4,8,2,8,256]{4,3,2,1,0:T(8,128)(2,1)}, bf16[4,8,2,8,256]{4,3,2,1,0:T(8,128)(2,1)S(1)}, u32[]{:S(2)}, u32[]{:S(2)}) %collective-permute-start.7) | collective-permute-done | bytes 262176 | tf_op jit(solution)/shard_map/ppermute | solution.py:373
  85.2 0.0 collective-permute-start.5
  85.2 15.8 %collective-permute-done.6.refs_6_ = bf16[4,8,2,8,256]{4,3,2,1,0:T(8,128)(2,1)S(1)} collective-permute-done((bf16[4,8,2,8,256]{4,3,2,1,0:T(8,128)(2,1)}, bf16[4,8,2,8,256]{4,3,2,1,0:T(8,128)(2,1)S(1)}, u32[]{:S(2)}, u32[]{:S(2)}) %collective-permute-start.6) | collective-permute-done | bytes 262176 | tf_op jit(solution)/shard_map/ppermute | solution.py:373
  101.1 0.0 collective-permute-done.2.refs_3_
  101.1 0.0 collective-permute-done.1.refs_2_
  101.1 0.0 copy-start.5
  101.1 5.4 %collective-permute-done.refs_1_ = bf16[4,8,2,8,256]{4,3,2,1,0:T(8,128)(2,1)S(1)} collective-permute-done((bf16[4,8,2,8,256]{4,3,2,1,0:T(8,128)(2,1)}, bf16[4,8,2,8,256]{4,3,2,1,0:T(8,128)(2,1)S(1)}, u32[]{:S(2)}, u32[]{:S(2)}) %collective-permute-start) | collective-permute-done | bytes 262176 | tf_op jit(solution)/shard_map/ppermute | solution.py:373
  106.5 0.7 copy-done.6
  107.2 0.0 collective-permute-done.5.refs_5_
  107.2 0.0 all-to-all-done.1
  107.2 0.0 copy-done.8
  107.2 0.0 copy-done.1
  107.2 0.0 copy-done.2
  107.2 0.0 copy-done.3
  107.2 0.0 copy-done.4
  107.3 0.0 copy-done.5
  107.3 2.8 %halo.1 = (bf16[2,64,8,256]{3,2,1,0:T(8,128)(2,1)}, bf16[2,64,8,256]{3,2,1,0:T(8,128)(2,1)}) custom-call(s32[1]{0:T(128)} %bitcast.8.z_ref, bf16[8,4,8,2,8,256]{5,4,3,2,1,0:T(8,128)(2,1)S(1)} %bitcast.32, bf16[4,8,2,8,256]{4,3,2,1,0:T(8,128)(2,1)} %get-tuple-element.18.refs_0_, bf16[4,8,2,8,256]{4,3,2,1,0:T(8,128)(2,1)} %copy-done.6, ...), custom_call_target="tpu_custom_call" | custom-call | tf_op jit(solution)/shard_map/halo/pallas_call | solution.py:170
  110.0 1.3 collective-permute-start.9
  111.4 1.3 collective-permute-start.10
  112.7 6.6 %inner.1 = (bf16[4,64,8,256]{3,2,1,0:T(8,128)(2,1)}, bf16[8,4,8,2,8,256]{5,4,3,2,1,0:T(8,128)(2,1)}) custom-call(s32[1]{0:T(128)} %bitcast.8.z_ref, s32[2,64]{1,0:T(2,128)} %bitcast.40, f32[2,64]{1,0:T(2,128)} %bitcast.42, s32[1]{0:T(128)} %bitcast.7.start_ref, bf16[8,4,8,2,8,256]{5,4,3,2,1,0:T(8,128)(2,1)S(1)} %bitcast.33, ...), custom_call_target="tpu_custom_call" | custom-call | tf_op jit(solution)/shard_map/inner/pallas_call | solution.py:185
  119.3 1.3 collective-permute-done.9.left_ref
  120.5 3.8 %collective-permute-done.10.right_ref = bf16[2,64,8,256]{3,2,1,0:T(8,128)(2,1)S(1)} collective-permute-done((bf16[2,64,8,256]{3,2,1,0:T(8,128)(2,1)}, bf16[2,64,8,256]{3,2,1,0:T(8,128)(2,1)S(1)}, u32[]{:S(2)}, u32[]{:S(2)}) %collective-permute-start.10) | collective-permute-done | bytes 524320 | tf_op jit(solution)/shard_map/ppermute | solution.py:398
  124.3 4.5 %edge.1 = bf16[8,4,8,2,8,256]{5,4,3,2,1,0:T(8,128)(2,1)} custom-call(s32[2,64]{1,0:T(2,128)} %bitcast.41, f32[2,64]{1,0:T(2,128)} %bitcast.43, s32[1]{0:T(128)} %bitcast.7.start_ref, bf16[2,64,8,256]{3,2,1,0:T(8,128)(2,1)S(1)} %collective-permute-done.9.left_ref, bf16[2,64,8,256]{3,2,1,0:T(8,128)(2,1)} %get-tuple-element.9.lo_ref, ...), custom_call_target="tpu_custom_call", output_to_operand_aliasing={{}: (8, {})} | custom-call | tf_op jit(solution)/shard_map/edge/pallas_call | solution.py:207
  128.8 0.0 copy-start.11
  128.8 0.0 copy-start.10
  128.8 0.0 copy-start.7
  128.8 0.0 copy-start.9
  128.8 10.6 %all-to-all-start.2 = ((bf16[32,8,2,8,256]{4,3,2,1,0:T(8,128)(2,1)}), bf16[32,8,2,8,256]{4,3,2,1,0:T(8,128)(2,1)S(1)}, u32[]{:S(2)}, u32[]{:S(2)}) async-start(bf16[32,8,2,8,256]{4,3,2,1,0:T(8,128)(2,1)} %bitcast.36), calls=%async_computation.2 | async-start | bytes 4194304 | tf_op jit(solution)/shard_map/all_to_all | solution.py:370
  139.5 0.0 copy-done.11
  139.5 0.1 dynamic_slice.38
  139.6 0.1 dynamic_slice.37
  139.6 0.0 copy-done.10
  139.7 0.1 dynamic-slice_bitcast_fusion.9
  139.8 0.7 copy.19.mask_j_ref
  140.4 0.1 dynamic-slice_bitcast_fusion.10
  140.5 0.7 copy.18.mask_i_ref
  141.2 0.0 copy-done.7
  141.2 0.8 copy.17
  142.0 0.0 copy-done.9
  142.0 0.7 add_convert_fusion.right_ref.left_ref.over_ref
  142.7 7.9 %term.2.x_ref = f32[8,2,256,256]{3,2,1,0:T(8,128)} custom-call(bf16[8,2,256,256]{3,2,1,0:T(8,128)(2,1)} %x_ref.3, bf16[8,2,256,256]{3,2,1,0:T(8,128)(2,1)} %amp_ref.5, bf16[256,256]{1,0:T(8,128)(2,1)} %right_ref.1, bf16[256,256]{1,0:T(8,128)(2,1)} %add_convert_fusion.right_ref.left_ref.over_ref), custom_call_target="tpu_custom_call" | custom-call | tf_op jit(solution)/shard_map/term/pallas_call | solution.py:238
  150.6 8.3 %term.3.base_ref = f32[8,2,256,256]{3,2,1,0:T(8,128)} custom-call(f32[8,2,256,256]{3,2,1,0:T(8,128)} %term.2.x_ref, bf16[8,2,256,256]{3,2,1,0:T(8,128)(2,1)} %amp_ref.5, bf16[256,256]{1,0:T(8,128)(2,1)} %add_convert_fusion.right_ref.left_ref.over_ref, bf16[256,256]{1,0:T(8,128)(2,1)} %right_ref.1), custom_call_target="tpu_custom_call" | custom-call | tf_op jit(solution)/shard_map/term/pallas_call | solution.py:238
  158.9 0.6 pad_maximum_fusion.occ_ref
  159.5 7.1 %all-to-all-done.2.coup_ref = bf16[32,8,2,8,256]{4,3,2,1,0:T(8,128)(2,1)S(1)} async-done(((bf16[32,8,2,8,256]{4,3,2,1,0:T(8,128)(2,1)}), bf16[32,8,2,8,256]{4,3,2,1,0:T(8,128)(2,1)S(1)}, u32[]{:S(2)}, u32[]{:S(2)}) %all-to-all-start.2) | async-done | bytes 2097184 | tf_op jit(solution)/shard_map/all_to_all | solution.py:370
  166.6 9.1 %finish.1 = (f32[8,2,256,256]{3,2,1,0:T(8,128)}, bf16[8,2,256,256]{3,2,1,0:T(8,128)(2,1)}) custom-call(f32[10]{0:T(128)} %pad_maximum_fusion.occ_ref, f32[8,2,256,256]{3,2,1,0:T(8,128)} %term.3.base_ref, bf16[8,2,256,256]{3,2,1,0:T(8,128)(2,1)} %amp_ref.5, f32[8,1,256]{2,1,0:T(1,128)} %copy.18.mask_i_ref, f32[2,1,256]{2,1,0:T(1,128)} %copy.19.mask_j_ref, ...), custom_call_target="tpu_custom_call" | custom-call | tf_op jit(solution)/shard_map/finish/pallas_call | solution.py:303
  (9 shorter events, 0.0 us)
Async XLA Ops:
  3.5 35.0 %all-to-all-start = ((bf16[32,8,2,8,256]{4,3,2,1,0:T(8,128)(2,1)}), bf16[32,8,2,8,256]{4,3,2,1,0:T(8,128)(2,1)S(1)}, u32[]{:S(2)}, u32[]{:S(2)}) async-start(bf16[32,8,2,8,256]{4,3,2,1,0:T(8,128)(2,1)} %pack_flip.1), calls=%async_computation | async-start | bytes 4194304 | tf_op jit(solution)/shard_map/all_to_all | solution.py:370
  38.6 1.9 %copy-start = (bf16[32,8,2,8,256]{4,3,2,1,0:T(8,128)(2,1)}, bf16[32,8,2,8,256]{4,3,2,1,0:T(8,128)(2,1)S(1)}, u32[]{:S(2)}) copy-start(bf16[32,8,2,8,256]{4,3,2,1,0:T(8,128)(2,1)S(1)} %all-to-all-done) | copy-start | bytes 6291460
  40.5 66.7 %all-to-all-start.1 = ((bf16[32,8,2,8,256]{4,3,2,1,0:T(8,128)(2,1)}), bf16[32,8,2,8,256]{4,3,2,1,0:T(8,128)(2,1)S(1)}, u32[]{:S(2)}, u32[]{:S(2)}) async-start(bf16[32,8,2,8,256]{4,3,2,1,0:T(8,128)(2,1)} %pack.1), calls=%async_computation.1 | async-start | bytes 4194304 | tf_op jit(solution)/shard_map/all_to_all | solution.py:370
  47.8 31.1 %collective-permute-start.8 = (bf16[4,8,2,8,256]{4,3,2,1,0:T(8,128)(2,1)}, bf16[4,8,2,8,256]{4,3,2,1,0:T(8,128)(2,1)S(1)}, u32[]{:S(2)}, u32[]{:S(2)}) collective-permute-start(bf16[4,8,2,8,256]{4,3,2,1,0:T(8,128)(2,1)} %get-tuple-element.12), channel_id=1, source_target_pairs={{0,28},{4,0},{8,4},{12,8},{16,12},{20,16},{24,20},{28,24},{1,29},{... | collective-permute-start | bytes 786440 | tf_op jit(solution)/shard_map/ppermute | solution.py:373
  54.5 17.6 %collective-permute-start.4 = (bf16[2,8,2,8,256]{4,3,2,1,0:T(8,128)(2,1)S(1)}, bf16[2,8,2,8,256]{4,3,2,1,0:T(8,128)(2,1)S(1)}, u32[]{:S(2)}, u32[]{:S(2)}) collective-permute-start(bf16[2,8,2,8,256]{4,3,2,1,0:T(8,128)(2,1)S(1)} %get-tuple-element.19), channel_id=1, source_target_pairs={{0,20},{4,24},{8,28},{12,0},{16,4},{20,8},{24,12},{28,16},{1,21},{... | collective-permute-start | bytes 393224 | tf_op jit(solution)/shard_map/ppermute | solution.py:373
  56.2 15.9 %collective-permute-start.3 = (bf16[2,8,2,8,256]{4,3,2,1,0:T(8,128)(2,1)S(1)}, bf16[2,8,2,8,256]{4,3,2,1,0:T(8,128)(2,1)S(1)}, u32[]{:S(2)}, u32[]{:S(2)}) collective-permute-start(bf16[2,8,2,8,256]{4,3,2,1,0:T(8,128)(2,1)S(1)} %get-tuple-element.20), channel_id=1, source_target_pairs={{0,16},{4,20},{8,24},{12,28},{16,0},{20,4},{24,8},{28,12},{1,17},{... | collective-permute-start | bytes 393224 | tf_op jit(solution)/shard_map/ppermute | solution.py:373
  56.2 29.1 %collective-permute-start.7 = (bf16[4,8,2,8,256]{4,3,2,1,0:T(8,128)(2,1)}, bf16[4,8,2,8,256]{4,3,2,1,0:T(8,128)(2,1)S(1)}, u32[]{:S(2)}, u32[]{:S(2)}) collective-permute-start(bf16[4,8,2,8,256]{4,3,2,1,0:T(8,128)(2,1)} %get-tuple-element.13), channel_id=1, source_target_pairs={{0,24},{4,28},{8,0},{12,4},{16,8},{20,12},{24,16},{28,20},{1,25},{... | collective-permute-start | bytes 786440 | tf_op jit(solution)/shard_map/ppermute | solution.py:373
  60.6 40.4 %collective-permute-start.6 = (bf16[4,8,2,8,256]{4,3,2,1,0:T(8,128)(2,1)}, bf16[4,8,2,8,256]{4,3,2,1,0:T(8,128)(2,1)S(1)}, u32[]{:S(2)}, u32[]{:S(2)}) collective-permute-start(bf16[4,8,2,8,256]{4,3,2,1,0:T(8,128)(2,1)} %get-tuple-element.14), channel_id=1, source_target_pairs={{0,20},{4,24},{8,28},{12,0},{16,4},{20,8},{24,12},{28,16},{1,21},{... | collective-permute-start | bytes 786440 | tf_op jit(solution)/shard_map/ppermute | solution.py:373
  72.1 29.0 %collective-permute-start.2 = (bf16[4,8,2,8,256]{4,3,2,1,0:T(8,128)(2,1)}, bf16[4,8,2,8,256]{4,3,2,1,0:T(8,128)(2,1)S(1)}, u32[]{:S(2)}, u32[]{:S(2)}) collective-permute-start(bf16[4,8,2,8,256]{4,3,2,1,0:T(8,128)(2,1)} %get-tuple-element.15), channel_id=1, source_target_pairs={{0,12},{4,16},{8,20},{12,24},{16,28},{20,0},{24,4},{28,8},{1,13},{... | collective-permute-start | bytes 786440 | tf_op jit(solution)/shard_map/ppermute | solution.py:373
  72.1 35.1 %copy-start.8 = (bf16[2,8,2,8,256]{4,3,2,1,0:T(8,128)(2,1)}, bf16[2,8,2,8,256]{4,3,2,1,0:T(8,128)(2,1)S(1)}, u32[]{:S(2)}) copy-start(bf16[2,8,2,8,256]{4,3,2,1,0:T(8,128)(2,1)S(1)} %collective-permute-done.3.refs_4_) | copy-start | bytes 393220
  72.1 29.0 %collective-permute-start.1 = (bf16[4,8,2,8,256]{4,3,2,1,0:T(8,128)(2,1)}, bf16[4,8,2,8,256]{4,3,2,1,0:T(8,128)(2,1)S(1)}, u32[]{:S(2)}, u32[]{:S(2)}) collective-permute-start(bf16[4,8,2,8,256]{4,3,2,1,0:T(8,128)(2,1)} %get-tuple-element.16), channel_id=1, source_target_pairs={{0,8},{4,12},{8,16},{12,20},{16,24},{20,28},{24,0},{28,4},{1,9},{5... | collective-permute-start | bytes 786440 | tf_op jit(solution)/shard_map/ppermute | solution.py:373
  79.0 28.2 %copy-start.1 = (bf16[4,8,2,8,256]{4,3,2,1,0:T(8,128)(2,1)}, bf16[4,8,2,8,256]{4,3,2,1,0:T(8,128)(2,1)S(1)}, u32[]{:S(2)}) copy-start(bf16[4,8,2,8,256]{4,3,2,1,0:T(8,128)(2,1)S(1)} %collective-permute-done.8.refs_8_) | copy-start | bytes 786436
  79.0 27.5 %collective-permute-start = (bf16[4,8,2,8,256]{4,3,2,1,0:T(8,128)(2,1)}, bf16[4,8,2,8,256]{4,3,2,1,0:T(8,128)(2,1)S(1)}, u32[]{:S(2)}, u32[]{:S(2)}) collective-permute-start(bf16[4,8,2,8,256]{4,3,2,1,0:T(8,128)(2,1)} %get-tuple-element.17), channel_id=1, source_target_pairs={{0,4},{4,8},{8,12},{12,16},{16,20},{20,24},{24,28},{28,0},{1,5},{5... | collective-permute-start | bytes 786440 | tf_op jit(solution)/shard_map/ppermute | solution.py:373
  85.2 22.0 %copy-start.2 = (bf16[4,8,2,8,256]{4,3,2,1,0:T(8,128)(2,1)}, bf16[4,8,2,8,256]{4,3,2,1,0:T(8,128)(2,1)S(1)}, u32[]{:S(2)}) copy-start(bf16[4,8,2,8,256]{4,3,2,1,0:T(8,128)(2,1)S(1)} %collective-permute-done.7.refs_7_) | copy-start | bytes 786436
  85.2 22.0 %collective-permute-start.5 = (bf16[2,8,2,8,256]{4,3,2,1,0:T(8,128)(2,1)S(1)}, bf16[2,8,2,8,256]{4,3,2,1,0:T(8,128)(2,1)}, u32[]{:S(2)}, u32[]{:S(2)}) collective-permute-start(bf16[2,8,2,8,256]{4,3,2,1,0:T(8,128)(2,1)S(1)} %collective-permute-done.4), channel_id=1, source_target_pairs={{0,28},{4,0},{8,4},{12,8},{16,12},{20,16},{24,20},{28,24},{1,29},{... | collective-permute-start | bytes 393224 | tf_op jit(solution)/shard_map/ppermute | solution.py:373
  101.1 6.2 %copy-start.3 = (bf16[4,8,2,8,256]{4,3,2,1,0:T(8,128)(2,1)}, bf16[4,8,2,8,256]{4,3,2,1,0:T(8,128)(2,1)S(1)}, u32[]{:S(2)}) copy-start(bf16[4,8,2,8,256]{4,3,2,1,0:T(8,128)(2,1)S(1)} %collective-permute-done.6.refs_6_) | copy-start | bytes 786436
  101.1 6.2 %copy-start.4 = (bf16[4,8,2,8,256]{4,3,2,1,0:T(8,128)(2,1)}, bf16[4,8,2,8,256]{4,3,2,1,0:T(8,128)(2,1)S(1)}, u32[]{:S(2)}) copy-start(bf16[4,8,2,8,256]{4,3,2,1,0:T(8,128)(2,1)S(1)} %collective-permute-done.2.refs_3_) | copy-start | bytes 786436
  101.1 6.2 %copy-start.5 = (bf16[4,8,2,8,256]{4,3,2,1,0:T(8,128)(2,1)}, bf16[4,8,2,8,256]{4,3,2,1,0:T(8,128)(2,1)S(1)}, u32[]{:S(2)}) copy-start(bf16[4,8,2,8,256]{4,3,2,1,0:T(8,128)(2,1)S(1)} %collective-permute-done.1.refs_2_) | copy-start | bytes 786436
  106.5 0.7 copy-start.6
  110.0 10.5 %collective-permute-start.9 = (bf16[2,64,8,256]{3,2,1,0:T(8,128)(2,1)}, bf16[2,64,8,256]{3,2,1,0:T(8,128)(2,1)S(1)}, u32[]{:S(2)}, u32[]{:S(2)}) collective-permute-start(bf16[2,64,8,256]{3,2,1,0:T(8,128)(2,1)} %get-tuple-element.8.hi_ref), channel_id=1, source_target_pairs={{0,4},{4,8},{8,12},{12,16},{16,20},{20,24},{24,28},{1,5},{5,9},{9,... | collective-permute-start | bytes 1572872 | tf_op jit(solution)/shard_map/ppermute | solution.py:397
  111.4 12.9 %collective-permute-start.10 = (bf16[2,64,8,256]{3,2,1,0:T(8,128)(2,1)}, bf16[2,64,8,256]{3,2,1,0:T(8,128)(2,1)S(1)}, u32[]{:S(2)}, u32[]{:S(2)}) collective-permute-start(bf16[2,64,8,256]{3,2,1,0:T(8,128)(2,1)} %get-tuple-element.9.lo_ref), channel_id=1, source_target_pairs={{4,0},{8,4},{12,8},{16,12},{20,16},{24,20},{28,24},{5,1},{9,5},{13... | collective-permute-start | bytes 1572872 | tf_op jit(solution)/shard_map/ppermute | solution.py:398
  128.8 10.7 %copy-start.11 = (f32[64]{0:T(128)S(1)}, f32[64]{0:T(128)}, u32[]{:S(2)}) copy-start(f32[64]{0:T(128)} %param.16) | copy-start | bytes 772
  128.8 10.8 %copy-start.10 = (s32[64,8]{0,1:T(8,128)S(1)}, s32[64,8]{0,1:T(8,128)}, u32[]{:S(2)}) copy-start(s32[64,8]{0,1:T(8,128)} %param.19) | copy-start | bytes 6148
  128.8 12.4 %copy-start.7 = (bf16[256,256]{1,0:T(8,128)(2,1)S(1)}, bf16[256,256]{1,0:T(8,128)(2,1)}, u32[]{:S(2)}) copy-start(bf16[256,256]{1,0:T(8,128)(2,1)} %trans_ref.1) | copy-start | bytes 393220
  128.8 13.1 %copy-start.9 = (bf16[256,256]{1,0:T(8,128)(2,1)S(1)}, bf16[256,256]{1,0:T(8,128)(2,1)}, u32[]{:S(2)}) copy-start(bf16[256,256]{1,0:T(8,128)(2,1)} %param.13) | copy-start | bytes 393220
  128.8 37.7 %all-to-all-start.2 = ((bf16[32,8,2,8,256]{4,3,2,1,0:T(8,128)(2,1)}), bf16[32,8,2,8,256]{4,3,2,1,0:T(8,128)(2,1)S(1)}, u32[]{:S(2)}, u32[]{:S(2)}) async-start(bf16[32,8,2,8,256]{4,3,2,1,0:T(8,128)(2,1)} %bitcast.36), calls=%async_computation.2 | async-start | bytes 4194304 | tf_op jit(solution)/shard_map/all_to_all | solution.py:370

commit v6 on v5

--- a/solution.py
+++ b/solution.py
@@ -274,15 +274,15 @@
     def right(xs, m):
         return [_dot(x, m) for x in xs]
 
-    two = []
-    cm = []
+    marks = []
+    b1 = []
     for r, s in pairs:
-        row = jnp.maximum(mask_i_ref[r], mask_j_ref[s])
-        two.append(row.T * row)
-        coup = coup_ref[:, k * step + r, s].astype(jnp.float32).reshape(w, w)
-        cm.append(coup * two[-1])
-    third = right(bf(left(over, bf(cm))), over)
-    res = [m * (base_ref[r, s] - t) for m, t, (r, s) in zip(two, third, pairs)]
+        mark = jnp.maximum(mask_i_ref[r], mask_j_ref[s])
+        marks.append(mark)
+        coup = coup_ref[:, k * step + r, s].reshape(w, w)
+        b1.append(_dot((over.astype(jnp.float32) * mark).astype(jnp.bfloat16), coup) * mark)
+    third = right(bf(b1), over)
+    res = [(base_ref[r, s] - t) * m * m.T for m, t, (r, s) in zip(marks, third, pairs)]
     for x, (r, s) in zip(res, pairs):
         res_ref[r, s] = x
     q = right(bf(left(tt, bf(res))), trans)
@@ -297,7 +297,7 @@
 
 def finish(occ, base, amp, coup, mask_i, mask_j, over, trans, energy):
     rows, cols, w, _ = amp.shape
-    step = 2
+    step = 4
     big = pl.BlockSpec((step, cols, w, w), lambda k, *_: (k, 0, 0, 0))
     mat = pl.BlockSpec((w, w), lambda k, *_: (0, 0))
     return pl.pallas_call(

time: 179 us -> 178 us (level)
  transfers between devices with their start and end apart: 14 -> 14, of which waited for: 8 -> 8; matrix products, arithmetic and copies ran while one was open for 3% -> 3% of each run, Pallas kernels for 14% -> 15%
where the time goes in v6:
time: 178 us; the launch traced here: 175 us
  waiting for transfers between devices  74.5 us (42%)
  starting transfers between devices  48.1 us (27%)
  Pallas kernels  43.8 us (25%)
  local copies, waits for them, and re-layouts  6.13 us (3%)
    ppermute x9, waiting for transfers between devices, shift(): return lax.ppermute(x, 'z', [(q, (q + k) % z_n) for q in range(z_n)])  38 us
    all_to_all x3, waiting for transfers between devices, spread(): return lax.all_to_all(x, plane, 0, 0, tiled=True)  31.5 us
    all_to_all x3, starting transfers between devices, spread(): return lax.all_to_all(x, plane, 0, 0, tiled=True)  25.9 us
    ppermute x9, starting transfers between devices, shift(): return lax.ppermute(x, 'z', [(q, (q + k) % z_n) for q in range(z_n)])  19.6 us
    pallas_call x2, Pallas kernels, add_term(): pl.pallas_call(pre_kernel, grid=(rows,), in_specs=[big, big, mat, mat], o...  16.2 us
    pallas_call x1, Pallas kernels, finish(): pl.pallas_call(post_kernel, grid_spec=pltpu.PrefetchScalarGridSpec(num_sc...  8.13 us
    pallas_call x1, Pallas kernels, couple_inner(): pl.pallas_call(functools.partial(inner_kernel, split=split), in_specs=[SM...  6.6 us
    pallas_call x2, Pallas kernels, pack(): pl.pallas_call(functools.partial(pack_kernel, flip=flip), grid=(rows // s...  5.59 us
  transfers between devices with their start and end apart: 14, of which 8 were waited for; matrix products, arithmetic and copies ran while one was open for 3% of the time, Pallas kernels for 15%

profile of v6, /device:TPU:3, one launch (start us, length us, event | category | flops | bytes accessed | tf_op | source)
XLA Modules:
  0.0 174.7 jit_solution(11473078131977050303)
XLA Ops:
  0.6 2.9 %pack_flip.1 = bf16[32,8,2,8,256]{4,3,2,1,0:T(8,128)(2,1)} custom-call(bf16[8,2,256,256]{3,2,1,0:T(8,128)(2,1)} %amp_ref.5), custom_call_target="tpu_custom_call" | custom-call | tf_op jit(solution)/shard_map/pack_flip/pallas_call | solution.py:34
  3.5 7.9 %all-to-all-start = ((bf16[32,8,2,8,256]{4,3,2,1,0:T(8,128)(2,1)}), bf16[32,8,2,8,256]{4,3,2,1,0:T(8,128)(2,1)S(1)}, u32[]{:S(2)}, u32[]{:S(2)}) async-start(bf16[32,8,2,8,256]{4,3,2,1,0:T(8,128)(2,1)} %pack_flip.1), calls=%async_computation | async-start | bytes 4194304 | tf_op jit(solution)/shard_map/all_to_all | solution.py:370
  11.5 2.7 %pack.1 = bf16[32,8,2,8,256]{4,3,2,1,0:T(8,128)(2,1)} custom-call(bf16[8,2,256,256]{3,2,1,0:T(8,128)(2,1)} %amp_ref.5), custom_call_target="tpu_custom_call" | custom-call | tf_op jit(solution)/shard_map/pack/pallas_call | solution.py:34
  14.2 24.4 %all-to-all-done = bf16[32,8,2,8,256]{4,3,2,1,0:T(8,128)(2,1)S(1)} async-done(((bf16[32,8,2,8,256]{4,3,2,1,0:T(8,128)(2,1)}), bf16[32,8,2,8,256]{4,3,2,1,0:T(8,128)(2,1)S(1)}, u32[]{:S(2)}, u32[]{:S(2)}) %all-to-all-start) | async-done | bytes 2097184 | tf_op jit(solution)/shard_map/all_to_all | solution.py:370
  38.6 1.3 dynamic-slice_bitcast_fusion
  39.9 0.6 copy-done
  40.5 7.3 %all-to-all-start.1 = ((bf16[32,8,2,8,256]{4,3,2,1,0:T(8,128)(2,1)}), bf16[32,8,2,8,256]{4,3,2,1,0:T(8,128)(2,1)S(1)}, u32[]{:S(2)}, u32[]{:S(2)}) async-start(bf16[32,8,2,8,256]{4,3,2,1,0:T(8,128)(2,1)} %pack.1), calls=%async_computation.1 | async-start | bytes 4194304 | tf_op jit(solution)/shard_map/all_to_all | solution.py:370
  47.8 5.7 %collective-permute-start.8 = (bf16[4,8,2,8,256]{4,3,2,1,0:T(8,128)(2,1)}, bf16[4,8,2,8,256]{4,3,2,1,0:T(8,128)(2,1)S(1)}, u32[]{:S(2)}, u32[]{:S(2)}) collective-permute-start(bf16[4,8,2,8,256]{4,3,2,1,0:T(8,128)(2,1)} %get-tuple-element.12), channel_id=1, source_target_pairs={{0,28},{4,0},{8,4},{12,8},{16,12},{20,16},{24,20},{28,24},{1,29},{... | collective-permute-start | bytes 786440 | tf_op jit(solution)/shard_map/ppermute | solution.py:373
  53.5 1.0 dynamic-slice_bitcast_fusion.7
  54.5 1.7 collective-permute-start.4
  56.2 0.0 collective-permute-start.3
  56.2 4.5 %collective-permute-start.7 = (bf16[4,8,2,8,256]{4,3,2,1,0:T(8,128)(2,1)}, bf16[4,8,2,8,256]{4,3,2,1,0:T(8,128)(2,1)S(1)}, u32[]{:S(2)}, u32[]{:S(2)}) collective-permute-start(bf16[4,8,2,8,256]{4,3,2,1,0:T(8,128)(2,1)} %get-tuple-element.13), channel_id=1, source_target_pairs={{0,24},{4,28},{8,0},{12,4},{16,8},{20,12},{24,16},{28,20},{1,25},{... | collective-permute-start | bytes 786440 | tf_op jit(solution)/shard_map/ppermute | solution.py:373
  60.6 0.9 collective-permute-start.6
  61.6 10.5 %collective-permute-done.4 = bf16[2,8,2,8,256]{4,3,2,1,0:T(8,128)(2,1)S(1)} collective-permute-done((bf16[2,8,2,8,256]{4,3,2,1,0:T(8,128)(2,1)S(1)}, bf16[2,8,2,8,256]{4,3,2,1,0:T(8,128)(2,1)S(1)}, u32[]{:S(2)}, u32[]{:S(2)}) %collective-permute-start.4) | collective-permute-done | bytes 131104 | tf_op jit(solution)/shard_map/ppermute | solution.py:373
  72.1 0.0 collective-permute-start.2
  72.1 0.0 collective-permute-done.3.refs_4_
  72.1 6.9 %collective-permute-start.1 = (bf16[4,8,2,8,256]{4,3,2,1,0:T(8,128)(2,1)}, bf16[4,8,2,8,256]{4,3,2,1,0:T(8,128)(2,1)S(1)}, u32[]{:S(2)}, u32[]{:S(2)}) collective-permute-start(bf16[4,8,2,8,256]{4,3,2,1,0:T(8,128)(2,1)} %get-tuple-element.16), channel_id=1, source_target_pairs={{0,8},{4,12},{8,16},{12,20},{16,24},{20,28},{24,0},{28,4},{1,9},{5... | collective-permute-start | bytes 786440 | tf_op jit(solution)/shard_map/ppermute | solution.py:373
  79.0 0.0 collective-permute-done.8.refs_8_
  79.0 0.0 collective-permute-start
  79.0 6.2 %collective-permute-done.7.refs_7_ = bf16[4,8,2,8,256]{4,3,2,1,0:T(8,128)(2,1)S(1)} collective-permute-done((bf16[4,8,2,8,256]{4,3,2,1,0:T(8,128)(2,1)}, bf16[4,8,2,8,256]{4,3,2,1,0:T(8,128)(2,1)S(1)}, u32[]{:S(2)}, u32[]{:S(2)}) %collective-permute-start.7) | collective-permute-done | bytes 262176 | tf_op jit(solution)/shard_map/ppermute | solution.py:373
  85.2 0.0 collective-permute-start.5
  85.2 15.8 %collective-permute-done.6.refs_6_ = bf16[4,8,2,8,256]{4,3,2,1,0:T(8,128)(2,1)S(1)} collective-permute-done((bf16[4,8,2,8,256]{4,3,2,1,0:T(8,128)(2,1)}, bf16[4,8,2,8,256]{4,3,2,1,0:T(8,128)(2,1)S(1)}, u32[]{:S(2)}, u32[]{:S(2)}) %collective-permute-start.6) | collective-permute-done | bytes 262176 | tf_op jit(solution)/shard_map/ppermute | solution.py:373
  101.1 0.0 collective-permute-done.2.refs_3_
  101.1 0.0 collective-permute-done.1.refs_2_
  101.1 0.0 copy-start.5
  101.1 5.4 %collective-permute-done.refs_1_ = bf16[4,8,2,8,256]{4,3,2,1,0:T(8,128)(2,1)S(1)} collective-permute-done((bf16[4,8,2,8,256]{4,3,2,1,0:T(8,128)(2,1)}, bf16[4,8,2,8,256]{4,3,2,1,0:T(8,128)(2,1)S(1)}, u32[]{:S(2)}, u32[]{:S(2)}) %collective-permute-start) | collective-permute-done | bytes 262176 | tf_op jit(solution)/shard_map/ppermute | solution.py:373
  106.5 0.7 copy-done.6
  107.2 0.0 collective-permute-done.5.refs_5_
  107.2 0.0 all-to-all-done.1
  107.2 0.0 copy-done.8
  107.2 0.0 copy-done.1
  107.2 0.0 copy-done.2
  107.2 0.0 copy-done.3
  107.2 0.0 copy-done.4
  107.3 0.0 copy-done.5
  107.3 2.8 %halo.1 = (bf16[2,64,8,256]{3,2,1,0:T(8,128)(2,1)}, bf16[2,64,8,256]{3,2,1,0:T(8,128)(2,1)}) custom-call(s32[1]{0:T(128)} %bitcast.8.z_ref, bf16[8,4,8,2,8,256]{5,4,3,2,1,0:T(8,128)(2,1)S(1)} %bitcast.32, bf16[4,8,2,8,256]{4,3,2,1,0:T(8,128)(2,1)} %get-tuple-element.18.refs_0_, bf16[4,8,2,8,256]{4,3,2,1,0:T(8,128)(2,1)} %copy-done.6, ...), custom_call_target="tpu_custom_call" | custom-call | tf_op jit(solution)/shard_map/halo/pallas_call | solution.py:170
  110.0 1.3 collective-permute-start.9
  111.4 1.3 collective-permute-start.10
  112.7 6.6 %inner.1 = (bf16[4,64,8,256]{3,2,1,0:T(8,128)(2,1)}, bf16[8,4,8,2,8,256]{5,4,3,2,1,0:T(8,128)(2,1)}) custom-call(s32[1]{0:T(128)} %bitcast.8.z_ref, s32[2,64]{1,0:T(2,128)} %bitcast.40, f32[2,64]{1,0:T(2,128)} %bitcast.42, s32[1]{0:T(128)} %bitcast.7.start_ref, bf16[8,4,8,2,8,256]{5,4,3,2,1,0:T(8,128)(2,1)S(1)} %bitcast.33, ...), custom_call_target="tpu_custom_call" | custom-call | tf_op jit(solution)/shard_map/inner/pallas_call | solution.py:185
  119.3 1.3 collective-permute-done.9.left_ref
  120.5 3.8 %collective-permute-done.10.right_ref = bf16[2,64,8,256]{3,2,1,0:T(8,128)(2,1)S(1)} collective-permute-done((bf16[2,64,8,256]{3,2,1,0:T(8,128)(2,1)}, bf16[2,64,8,256]{3,2,1,0:T(8,128)(2,1)S(1)}, u32[]{:S(2)}, u32[]{:S(2)}) %collective-permute-start.10) | collective-permute-done | bytes 524320 | tf_op jit(solution)/shard_map/ppermute | solution.py:398
  124.3 4.5 %edge.1 = bf16[8,4,8,2,8,256]{5,4,3,2,1,0:T(8,128)(2,1)} custom-call(s32[2,64]{1,0:T(2,128)} %bitcast.41, f32[2,64]{1,0:T(2,128)} %bitcast.43, s32[1]{0:T(128)} %bitcast.7.start_ref, bf16[2,64,8,256]{3,2,1,0:T(8,128)(2,1)S(1)} %collective-permute-done.9.left_ref, bf16[2,64,8,256]{3,2,1,0:T(8,128)(2,1)} %get-tuple-element.9.lo_ref, ...), custom_call_target="tpu_custom_call", output_to_operand_aliasing={{}: (8, {})} | custom-call | tf_op jit(solution)/shard_map/edge/pallas_call | solution.py:207
  128.8 0.0 copy-start.11
  128.8 0.0 copy-start.10
  128.8 0.0 copy-start.7
  128.8 0.0 copy-start.9
  128.8 10.6 %all-to-all-start.2 = ((bf16[32,8,2,8,256]{4,3,2,1,0:T(8,128)(2,1)}), bf16[32,8,2,8,256]{4,3,2,1,0:T(8,128)(2,1)S(1)}, u32[]{:S(2)}, u32[]{:S(2)}) async-start(bf16[32,8,2,8,256]{4,3,2,1,0:T(8,128)(2,1)} %bitcast.36), calls=%async_computation.2 | async-start | bytes 4194304 | tf_op jit(solution)/shard_map/all_to_all | solution.py:370
  139.5 0.0 copy-done.11
  139.5 0.1 dynamic_slice.38
  139.6 0.1 dynamic_slice.37
  139.6 0.0 copy-done.10
  139.7 0.1 dynamic-slice_bitcast_fusion.9
  139.8 0.7 copy.19.mask_j_ref
  140.4 0.1 dynamic-slice_bitcast_fusion.10
  140.5 0.7 copy.18.mask_i_ref
  141.2 0.0 copy-done.7
  141.2 0.8 copy.17
  142.0 0.0 copy-done.9
  142.0 0.7 add_convert_fusion.right_ref.left_ref.over_ref
  142.7 7.9 %term.2.x_ref = f32[8,2,256,256]{3,2,1,0:T(8,128)} custom-call(bf16[8,2,256,256]{3,2,1,0:T(8,128)(2,1)} %x_ref.3, bf16[8,2,256,256]{3,2,1,0:T(8,128)(2,1)} %amp_ref.5, bf16[256,256]{1,0:T(8,128)(2,1)} %right_ref.1, bf16[256,256]{1,0:T(8,128)(2,1)} %add_convert_fusion.right_ref.left_ref.over_ref), custom_call_target="tpu_custom_call" | custom-call | tf_op jit(solution)/shard_map/term/pallas_call | solution.py:238
  150.6 8.3 %term.3.base_ref = f32[8,2,256,256]{3,2,1,0:T(8,128)} custom-call(f32[8,2,256,256]{3,2,1,0:T(8,128)} %term.2.x_ref, bf16[8,2,256,256]{3,2,1,0:T(8,128)(2,1)} %amp_ref.5, bf16[256,256]{1,0:T(8,128)(2,1)} %add_convert_fusion.right_ref.left_ref.over_ref, bf16[256,256]{1,0:T(8,128)(2,1)} %right_ref.1), custom_call_target="tpu_custom_call" | custom-call | tf_op jit(solution)/shard_map/term/pallas_call | solution.py:238
  158.9 0.6 pad_maximum_fusion.occ_ref
  159.5 7.1 %all-to-all-done.2.coup_ref = bf16[32,8,2,8,256]{4,3,2,1,0:T(8,128)(2,1)S(1)} async-done(((bf16[32,8,2,8,256]{4,3,2,1,0:T(8,128)(2,1)}), bf16[32,8,2,8,256]{4,3,2,1,0:T(8,128)(2,1)S(1)}, u32[]{:S(2)}, u32[]{:S(2)}) %all-to-all-start.2) | async-done | bytes 2097184 | tf_op jit(solution)/shard_map/all_to_all | solution.py:370
  166.6 8.1 %finish.1 = (f32[8,2,256,256]{3,2,1,0:T(8,128)}, bf16[8,2,256,256]{3,2,1,0:T(8,128)(2,1)}) custom-call(f32[10]{0:T(128)} %pad_maximum_fusion.occ_ref, f32[8,2,256,256]{3,2,1,0:T(8,128)} %term.3.base_ref, bf16[8,2,256,256]{3,2,1,0:T(8,128)(2,1)} %amp_ref.5, f32[8,1,256]{2,1,0:T(1,128)} %copy.18.mask_i_ref, f32[2,1,256]{2,1,0:T(1,128)} %copy.19.mask_j_ref, ...), custom_call_target="tpu_custom_call" | custom-call | tf_op jit(solution)/shard_map/finish/pallas_call | solution.py:303
  (9 shorter events, 0.0 us)
Async XLA Ops:
  3.5 35.0 %all-to-all-start = ((bf16[32,8,2,8,256]{4,3,2,1,0:T(8,128)(2,1)}), bf16[32,8,2,8,256]{4,3,2,1,0:T(8,128)(2,1)S(1)}, u32[]{:S(2)}, u32[]{:S(2)}) async-start(bf16[32,8,2,8,256]{4,3,2,1,0:T(8,128)(2,1)} %pack_flip.1), calls=%async_computation | async-start | bytes 4194304 | tf_op jit(solution)/shard_map/all_to_all | solution.py:370
  38.6 1.9 %copy-start = (bf16[32,8,2,8,256]{4,3,2,1,0:T(8,128)(2,1)}, bf16[32,8,2,8,256]{4,3,2,1,0:T(8,128)(2,1)S(1)}, u32[]{:S(2)}) copy-start(bf16[32,8,2,8,256]{4,3,2,1,0:T(8,128)(2,1)S(1)} %all-to-all-done) | copy-start | bytes 6291460
  40.5 66.7 %all-to-all-start.1 = ((bf16[32,8,2,8,256]{4,3,2,1,0:T(8,128)(2,1)}), bf16[32,8,2,8,256]{4,3,2,1,0:T(8,128)(2,1)S(1)}, u32[]{:S(2)}, u32[]{:S(2)}) async-start(bf16[32,8,2,8,256]{4,3,2,1,0:T(8,128)(2,1)} %pack.1), calls=%async_computation.1 | async-start | bytes 4194304 | tf_op jit(solution)/shard_map/all_to_all | solution.py:370
  47.8 31.1 %collective-permute-start.8 = (bf16[4,8,2,8,256]{4,3,2,1,0:T(8,128)(2,1)}, bf16[4,8,2,8,256]{4,3,2,1,0:T(8,128)(2,1)S(1)}, u32[]{:S(2)}, u32[]{:S(2)}) collective-permute-start(bf16[4,8,2,8,256]{4,3,2,1,0:T(8,128)(2,1)} %get-tuple-element.12), channel_id=1, source_target_pairs={{0,28},{4,0},{8,4},{12,8},{16,12},{20,16},{24,20},{28,24},{1,29},{... | collective-permute-start | bytes 786440 | tf_op jit(solution)/shard_map/ppermute | solution.py:373
  54.5 17.6 %collective-permute-start.4 = (bf16[2,8,2,8,256]{4,3,2,1,0:T(8,128)(2,1)S(1)}, bf16[2,8,2,8,256]{4,3,2,1,0:T(8,128)(2,1)S(1)}, u32[]{:S(2)}, u32[]{:S(2)}) collective-permute-start(bf16[2,8,2,8,256]{4,3,2,1,0:T(8,128)(2,1)S(1)} %get-tuple-element.19), channel_id=1, source_target_pairs={{0,20},{4,24},{8,28},{12,0},{16,4},{20,8},{24,12},{28,16},{1,21},{... | collective-permute-start | bytes 393224 | tf_op jit(solution)/shard_map/ppermute | solution.py:373
  56.2 15.9 %collective-permute-start.3 = (bf16[2,8,2,8,256]{4,3,2,1,0:T(8,128)(2,1)S(1)}, bf16[2,8,2,8,256]{4,3,2,1,0:T(8,128)(2,1)S(1)}, u32[]{:S(2)}, u32[]{:S(2)}) collective-permute-start(bf16[2,8,2,8,256]{4,3,2,1,0:T(8,128)(2,1)S(1)} %get-tuple-element.20), channel_id=1, source_target_pairs={{0,16},{4,20},{8,24},{12,28},{16,0},{20,4},{24,8},{28,12},{1,17},{... | collective-permute-start | bytes 393224 | tf_op jit(solution)/shard_map/ppermute | solution.py:373
  56.2 29.1 %collective-permute-start.7 = (bf16[4,8,2,8,256]{4,3,2,1,0:T(8,128)(2,1)}, bf16[4,8,2,8,256]{4,3,2,1,0:T(8,128)(2,1)S(1)}, u32[]{:S(2)}, u32[]{:S(2)}) collective-permute-start(bf16[4,8,2,8,256]{4,3,2,1,0:T(8,128)(2,1)} %get-tuple-element.13), channel_id=1, source_target_pairs={{0,24},{4,28},{8,0},{12,4},{16,8},{20,12},{24,16},{28,20},{1,25},{... | collective-permute-start | bytes 786440 | tf_op jit(solution)/shard_map/ppermute | solution.py:373
  60.6 40.4 %collective-permute-start.6 = (bf16[4,8,2,8,256]{4,3,2,1,0:T(8,128)(2,1)}, bf16[4,8,2,8,256]{4,3,2,1,0:T(8,128)(2,1)S(1)}, u32[]{:S(2)}, u32[]{:S(2)}) collective-permute-start(bf16[4,8,2,8,256]{4,3,2,1,0:T(8,128)(2,1)} %get-tuple-element.14), channel_id=1, source_target_pairs={{0,20},{4,24},{8,28},{12,0},{16,4},{20,8},{24,12},{28,16},{1,21},{... | collective-permute-start | bytes 786440 | tf_op jit(solution)/shard_map/ppermute | solution.py:373
  72.1 29.0 %collective-permute-start.2 = (bf16[4,8,2,8,256]{4,3,2,1,0:T(8,128)(2,1)}, bf16[4,8,2,8,256]{4,3,2,1,0:T(8,128)(2,1)S(1)}, u32[]{:S(2)}, u32[]{:S(2)}) collective-permute-start(bf16[4,8,2,8,256]{4,3,2,1,0:T(8,128)(2,1)} %get-tuple-element.15), channel_id=1, source_target_pairs={{0,12},{4,16},{8,20},{12,24},{16,28},{20,0},{24,4},{28,8},{1,13},{... | collective-permute-start | bytes 786440 | tf_op jit(solution)/shard_map/ppermute | solution.py:373
  72.1 35.1 %copy-start.8 = (bf16[2,8,2,8,256]{4,3,2,1,0:T(8,128)(2,1)}, bf16[2,8,2,8,256]{4,3,2,1,0:T(8,128)(2,1)S(1)}, u32[]{:S(2)}) copy-start(bf16[2,8,2,8,256]{4,3,2,1,0:T(8,128)(2,1)S(1)} %collective-permute-done.3.refs_4_) | copy-start | bytes 393220
  72.1 29.0 %collective-permute-start.1 = (bf16[4,8,2,8,256]{4,3,2,1,0:T(8,128)(2,1)}, bf16[4,8,2,8,256]{4,3,2,1,0:T(8,128)(2,1)S(1)}, u32[]{:S(2)}, u32[]{:S(2)}) collective-permute-start(bf16[4,8,2,8,256]{4,3,2,1,0:T(8,128)(2,1)} %get-tuple-element.16), channel_id=1, source_target_pairs={{0,8},{4,12},{8,16},{12,20},{16,24},{20,28},{24,0},{28,4},{1,9},{5... | collective-permute-start | bytes 786440 | tf_op jit(solution)/shard_map/ppermute | solution.py:373
  79.0 28.2 %copy-start.1 = (bf16[4,8,2,8,256]{4,3,2,1,0:T(8,128)(2,1)}, bf16[4,8,2,8,256]{4,3,2,1,0:T(8,128)(2,1)S(1)}, u32[]{:S(2)}) copy-start(bf16[4,8,2,8,256]{4,3,2,1,0:T(8,128)(2,1)S(1)} %collective-permute-done.8.refs_8_) | copy-start | bytes 786436
  79.0 27.5 %collective-permute-start = (bf16[4,8,2,8,256]{4,3,2,1,0:T(8,128)(2,1)}, bf16[4,8,2,8,256]{4,3,2,1,0:T(8,128)(2,1)S(1)}, u32[]{:S(2)}, u32[]{:S(2)}) collective-permute-start(bf16[4,8,2,8,256]{4,3,2,1,0:T(8,128)(2,1)} %get-tuple-element.17), channel_id=1, source_target_pairs={{0,4},{4,8},{8,12},{12,16},{16,20},{20,24},{24,28},{28,0},{1,5},{5... | collective-permute-start | bytes 786440 | tf_op jit(solution)/shard_map/ppermute | solution.py:373
  85.2 22.0 %copy-start.2 = (bf16[4,8,2,8,256]{4,3,2,1,0:T(8,128)(2,1)}, bf16[4,8,2,8,256]{4,3,2,1,0:T(8,128)(2,1)S(1)}, u32[]{:S(2)}) copy-start(bf16[4,8,2,8,256]{4,3,2,1,0:T(8,128)(2,1)S(1)} %collective-permute-done.7.refs_7_) | copy-start | bytes 786436
  85.2 22.0 %collective-permute-start.5 = (bf16[2,8,2,8,256]{4,3,2,1,0:T(8,128)(2,1)S(1)}, bf16[2,8,2,8,256]{4,3,2,1,0:T(8,128)(2,1)}, u32[]{:S(2)}, u32[]{:S(2)}) collective-permute-start(bf16[2,8,2,8,256]{4,3,2,1,0:T(8,128)(2,1)S(1)} %collective-permute-done.4), channel_id=1, source_target_pairs={{0,28},{4,0},{8,4},{12,8},{16,12},{20,16},{24,20},{28,24},{1,29},{... | collective-permute-start | bytes 393224 | tf_op jit(solution)/shard_map/ppermute | solution.py:373
  101.1 6.2 %copy-start.3 = (bf16[4,8,2,8,256]{4,3,2,1,0:T(8,128)(2,1)}, bf16[4,8,2,8,256]{4,3,2,1,0:T(8,128)(2,1)S(1)}, u32[]{:S(2)}) copy-start(bf16[4,8,2,8,256]{4,3,2,1,0:T(8,128)(2,1)S(1)} %collective-permute-done.6.refs_6_) | copy-start | bytes 786436
  101.1 6.2 %copy-start.4 = (bf16[4,8,2,8,256]{4,3,2,1,0:T(8,128)(2,1)}, bf16[4,8,2,8,256]{4,3,2,1,0:T(8,128)(2,1)S(1)}, u32[]{:S(2)}) copy-start(bf16[4,8,2,8,256]{4,3,2,1,0:T(8,128)(2,1)S(1)} %collective-permute-done.2.refs_3_) | copy-start | bytes 786436
  101.1 6.2 %copy-start.5 = (bf16[4,8,2,8,256]{4,3,2,1,0:T(8,128)(2,1)}, bf16[4,8,2,8,256]{4,3,2,1,0:T(8,128)(2,1)S(1)}, u32[]{:S(2)}) copy-start(bf16[4,8,2,8,256]{4,3,2,1,0:T(8,128)(2,1)S(1)} %collective-permute-done.1.refs_2_) | copy-start | bytes 786436
  106.5 0.7 copy-start.6
  110.0 10.5 %collective-permute-start.9 = (bf16[2,64,8,256]{3,2,1,0:T(8,128)(2,1)}, bf16[2,64,8,256]{3,2,1,0:T(8,128)(2,1)S(1)}, u32[]{:S(2)}, u32[]{:S(2)}) collective-permute-start(bf16[2,64,8,256]{3,2,1,0:T(8,128)(2,1)} %get-tuple-element.8.hi_ref), channel_id=1, source_target_pairs={{0,4},{4,8},{8,12},{12,16},{16,20},{20,24},{24,28},{1,5},{5,9},{9,... | collective-permute-start | bytes 1572872 | tf_op jit(solution)/shard_map/ppermute | solution.py:397
  111.4 12.9 %collective-permute-start.10 = (bf16[2,64,8,256]{3,2,1,0:T(8,128)(2,1)}, bf16[2,64,8,256]{3,2,1,0:T(8,128)(2,1)S(1)}, u32[]{:S(2)}, u32[]{:S(2)}) collective-permute-start(bf16[2,64,8,256]{3,2,1,0:T(8,128)(2,1)} %get-tuple-element.9.lo_ref), channel_id=1, source_target_pairs={{4,0},{8,4},{12,8},{16,12},{20,16},{24,20},{28,24},{5,1},{9,5},{13... | collective-permute-start | bytes 1572872 | tf_op jit(solution)/shard_map/ppermute | solution.py:398
  128.8 10.7 %copy-start.11 = (f32[64]{0:T(128)S(1)}, f32[64]{0:T(128)}, u32[]{:S(2)}) copy-start(f32[64]{0:T(128)} %param.16) | copy-start | bytes 772
  128.8 10.8 %copy-start.10 = (s32[64,8]{0,1:T(8,128)S(1)}, s32[64,8]{0,1:T(8,128)}, u32[]{:S(2)}) copy-start(s32[64,8]{0,1:T(8,128)} %param.19) | copy-start | bytes 6148
  128.8 12.4 %copy-start.7 = (bf16[256,256]{1,0:T(8,128)(2,1)S(1)}, bf16[256,256]{1,0:T(8,128)(2,1)}, u32[]{:S(2)}) copy-start(bf16[256,256]{1,0:T(8,128)(2,1)} %trans_ref.1) | copy-start | bytes 393220
  128.8 13.2 %copy-start.9 = (bf16[256,256]{1,0:T(8,128)(2,1)S(1)}, bf16[256,256]{1,0:T(8,128)(2,1)}, u32[]{:S(2)}) copy-start(bf16[256,256]{1,0:T(8,128)(2,1)} %param.13) | copy-start | bytes 393220
  128.8 37.7 %all-to-all-start.2 = ((bf16[32,8,2,8,256]{4,3,2,1,0:T(8,128)(2,1)}), bf16[32,8,2,8,256]{4,3,2,1,0:T(8,128)(2,1)S(1)}, u32[]{:S(2)}, u32[]{:S(2)}) async-start(bf16[32,8,2,8,256]{4,3,2,1,0:T(8,128)(2,1)} %bitcast.36), calls=%async_computation.2 | async-start | bytes 4194304 | tf_op jit(solution)/shard_map/all_to_all | solution.py:370

commit v7 on v6

--- a/solution.py
+++ b/solution.py
@@ -11,6 +11,7 @@
 REACH = 2
 VMEM = pl.BlockSpec(memory_space=pltpu.VMEM)
 SMEM = pl.BlockSpec(memory_space=pltpu.SMEM)
+GRANT = pltpu.CompilerParams(vmem_limit_bytes=52 * 1024 * 1024)
 
 
 def near(x):
@@ -74,90 +75,67 @@
 def inner_kernel(
     z_ref, lists_ref, weights_ref, start_ref, a_ref, lo_ref, hi_ref, *refs, split
 ):
-    got, (mid_ref, o_ref, all_ref) = refs[:-3], refs[-3:]
+    got, (ext_ref, row_ref, o_ref) = refs[:-3], refs[-3:]
     t_n, g_n, r_n, s_n, _, _ = a_ref.shape
     j_n = g_n * s_n
-    start = start_ref[0]
-    all_ref[0:REACH] = lo_ref[...]
-    all_ref[j_n - REACH :] = hi_ref[...]
+    per = REACH // s_n
+    base = start_ref[0] - REACH
+    ext_ref[REACH : 2 * REACH] = lo_ref[...]
+    ext_ref[j_n : j_n + REACH] = hi_ref[...]
     for k in range(t_n):
         t = lax.rem(z_ref[0] + (t_n - k), t_n)
         for j in range(REACH, j_n - REACH):
             for i in range(r_n):
                 mir = _mirrored(got, split, k, j, i, g_n, s_n)
-                val = _sym(a_ref[t, j // s_n, i, j % s_n], mir)
-                all_ref[j, t * r_n + i] = val
-                mid_ref[j - REACH, t * r_n + i] = val
+                ext_ref[j + REACH, t * r_n + i] = _sym(a_ref[t, j // s_n, i, j % s_n], mir)
 
     def tile(t, carry):
         for j in range(j_n):
-            gj = start + j
+            gj = start_ref[0] + j
+            g, s = j // s_n, j % s_n
             for r in range(r_n):
                 i = t * r_n + r
-                out = _mix(weights_ref, i, all_ref[j, lists_ref[0, i]], all_ref[j, lists_ref[1, i]])
+                x0 = ext_ref[j + REACH, lists_ref[0, i]]
+                x1 = ext_ref[j + REACH, lists_ref[1, i]]
+                out = _mix(weights_ref, i, x0, x1)
                 if REACH <= j < j_n - REACH:
-                    x0 = all_ref[lists_ref[0, gj] - start, i]
-                    x1 = all_ref[lists_ref[1, gj] - start, i]
+                    x0 = ext_ref[lists_ref[0, gj] - base, i]
+                    x1 = ext_ref[lists_ref[1, gj] - base, i]
                     col = _mix(weights_ref, gj, x0, x1)
                     out = (out.astype(jnp.float32) + col.astype(jnp.float32)).astype(jnp.bfloat16)
-                o_ref[t, j // s_n, r, j % s_n] = out
+                    o_ref[t, g, r, s] = out
+                else:
+                    row_ref[t, g if g < per else g - (g_n - 2 * per), r, s] = out
         return carry
 
     lax.fori_loop(0, t_n, tile, 0)
 
 
 def edge_kernel(
-    lists_ref, weights_ref, start_ref, left_ref, lo_ref, mid_ref, hi_ref, right_ref, x_ref, o_ref, ext_ref, sems
+    lists_ref, weights_ref, start_ref, left_ref, right_ref, row_ref, _, __, ext_ref, o_ref
 ):
     t_n, _, r_n, s_n, _, _ = o_ref.shape
+    j_n = ext_ref.shape[0] - 2 * REACH
+    per = REACH // s_n
     k = pl.program_id(0)
-    per = REACH // s_n
-    start = start_ref[0]
-    copies = []
-    at = 0
-    for ref, q0, n in (
-        (left_ref, 0, REACH),
-        (lo_ref, 0, REACH),
-        (mid_ref, 0, REACH),
-        (mid_ref, REACH, REACH),
-        (hi_ref, 0, REACH),
-        (right_ref, 0, REACH),
-    ):
-        src = ref.at[pl.ds(q0, n)]
-        copies.append(pltpu.make_async_copy(src, ext_ref.at[pl.ds(at, n)], sems.at[len(copies)]))
-        at += n
+    base = start_ref[0] - REACH
+    gj0 = start_ref[0] + k * s_n + jnp.where(k >= per, j_n - 2 * REACH, 0)
 
     @pl.when(k == 0)
     def _():
-        for c in copies:
-            c.start()
-        for c in copies[:3]:
-            c.wait()
-
-    @pl.when(k == per)
-    def _():
-        for c in copies[3:]:
-            c.wait()
-
-    high = k >= per
-    j0 = k * s_n
-    gap = mid_ref.shape[0] - 2 * REACH
-    gj0 = start + j0 + jnp.where(high, mid_ref.shape[0], 0)
-    base = start - REACH + jnp.where(high, gap, 0)
+        ext_ref[0:REACH] = left_ref[...]
+        ext_ref[j_n + REACH :] = right_ref[...]
 
     def tile(t, carry):
         for s in range(s_n):
             gj = gj0 + s
             for r in range(r_n):
                 i = t * r_n + r
-                col = _mix(
-                    weights_ref,
-                    gj,
-                    ext_ref[lists_ref[0, gj] - base, i],
-                    ext_ref[lists_ref[1, gj] - base, i],
-                )
-                row = x_ref[t, 0, r, s].astype(jnp.float32)
-                o_ref[t, 0, r, s] = (row + col.astype(jnp.float32)).astype(jnp.bfloat16)
+                x0 = ext_ref[lists_ref[0, gj] - base, i]
+                x1 = ext_ref[lists_ref[1, gj] - base, i]
+                col = _mix(weights_ref, gj, x0, x1).astype(jnp.float32)
+                row = row_ref[t, k, r, s].astype(jnp.float32)
+                o_ref[t, 0, r, s] = (row + col).astype(jnp.bfloat16)
         return carry
 
     lax.fori_loop(0, t_n, tile, 0)
@@ -178,28 +156,25 @@
 
 def couple_inner(z, lists, weights, start, own, got, low, high):
     t_n, g_n, r_n, s_n, sr, sl = own.shape
-    j_n = g_n * s_n
     split = [len(tile) for tile in got]
     flat = [part for tile in got for part in tile]
-    columns = lambda n: (n, t_n * r_n, sr, sl)
     return pl.pallas_call(
         functools.partial(inner_kernel, split=split),
         in_specs=[SMEM] * 4 + [VMEM] * (3 + len(flat)),
-        out_specs=[VMEM] * 2,
+        out_specs=[VMEM] * 3,
         out_shape=[
-            jax.ShapeDtypeStruct(columns(j_n - 2 * REACH), jnp.bfloat16),
+            pltpu.VMEM((g_n * s_n + 2 * REACH, t_n * r_n, sr, sl), jnp.bfloat16),
+            pltpu.VMEM((t_n, 2 * REACH // s_n, r_n, s_n, sr, sl), jnp.bfloat16),
             jax.ShapeDtypeStruct(own.shape, jnp.bfloat16),
         ],
-        scratch_shapes=[pltpu.VMEM(columns(j_n), jnp.bfloat16)],
+        compiler_params=GRANT,
         name="inner",
     )(z[None], lists, weights, start, own, low, high, *flat)
 
 
-def couple_edge(lists, weights, start, left, low, middle, high, right, part):
+def couple_edge(lists, weights, start, left, right, ext, row, part):
     t_n, g_n, r_n, s_n, sr, sl = part.shape
     per = REACH // s_n
-    i_n = t_n * r_n
-    hbm = pl.BlockSpec(memory_space=pl.ANY)
     block = pl.BlockSpec(
         (t_n, 1, r_n, s_n, sr, sl),
         lambda k: (0, k + jnp.where(k >= per, g_n - 2 * per, 0), 0, 0, 0, 0),
@@ -207,16 +182,16 @@
     return pl.pallas_call(
         edge_kernel,
         grid=(2 * per,),
-        in_specs=[SMEM, SMEM, SMEM, VMEM, hbm, hbm, hbm, VMEM, block],
-        out_specs=block,
-        out_shape=jax.ShapeDtypeStruct(part.shape, jnp.bfloat16),
-        scratch_shapes=[
-            pltpu.VMEM((6 * REACH, i_n, sr, sl), jnp.bfloat16),
-            pltpu.SemaphoreType.DMA((6,)),
+        in_specs=[SMEM] * 3 + [VMEM] * 4 + [pl.BlockSpec(memory_space=pl.ANY)],
+        out_specs=[VMEM, block],
+        out_shape=[
+            pltpu.VMEM(ext.shape, ext.dtype),
+            jax.ShapeDtypeStruct(part.shape, part.dtype),
         ],
-        input_output_aliases={8: 0},
+        input_output_aliases={6: 0, 7: 1},
+        compiler_params=GRANT,
         name="edge",
-    )(lists, weights, start, left, low, middle, high, right, part)
+    )(lists, weights, start, left, right, row, ext, part)[1]
 
 
 def _dot(x, y):
@@ -398,8 +373,8 @@
     right = lax.ppermute(low, "z", [(k + 1, k) for k in range(z_n - 1)])
     lists = partners.T
     weights = coupling.T
-    middle, part = couple_inner(z, lists, weights, start_z[None], own, got, low, high)
-    part = couple_edge(lists, weights, start_z[None], near(left), low, middle, high, near(right), part)
+    ext, row, part = couple_inner(z, lists, weights, start_z[None], own, got, low, high)
+    part = couple_edge(lists, weights, start_z[None], near(left), near(right), ext, near(row), part)
     coup = near(spread(part.reshape(n, rows, cols, width // n, width)))
 
     masks = jnp.repeat(domain.astype(jnp.float32), width // blocks, axis=1)

time: 178 us -> 178 us (level)
  starting transfers between devices: 48.1 us -> 60.8 us
  waiting for transfers between devices: 74.5 us -> 63.7 us
  Pallas kernels: 43.8 us -> 41.9 us
    ppermute x9, starting transfers between devices: 19.6 us -> 29.4 us  [shift(): return lax.ppermute(x, 'z', [(q, (q + k) % z_n) for q in range(z_n)])]
    ppermute x9, waiting for transfers between devices: 38 us -> 28.3 us  [shift(): return lax.ppermute(x, 'z', [(q, (q + k) % z_n) for q in range(z_n)])]
    ppermute x1, starting transfers between devices: 1.31 us -> 5.71 us  [per_device(): left = lax.ppermute(high, 'z', [(k, k + 1) for k in range(z_n - 1)])]
  transfers between devices with their start and end apart: 14 -> 14, of which waited for: 8 -> 9; matrix products, arithmetic and copies ran while one was open for 3% -> 3% of each run, Pallas kernels for 15% -> 14%
where the time goes in v7:
time: 178 us; the launch traced here: 175 us
  waiting for transfers between devices  63.7 us (36%)
  starting transfers between devices  60.8 us (34%)
  Pallas kernels  41.9 us (24%)
  local copies, waits for them, and re-layouts  6.11 us (3%)
    all_to_all x3, waiting for transfers between devices, spread(): return lax.all_to_all(x, plane, 0, 0, tiled=True)  31.4 us
    ppermute x9, starting transfers between devices, shift(): return lax.ppermute(x, 'z', [(q, (q + k) % z_n) for q in range(z_n)])  29.4 us
    ppermute x9, waiting for transfers between devices, shift(): return lax.ppermute(x, 'z', [(q, (q + k) % z_n) for q in range(z_n)])  28.3 us
    all_to_all x3, starting transfers between devices, spread(): return lax.all_to_all(x, plane, 0, 0, tiled=True)  24.4 us
    pallas_call x2, Pallas kernels, add_term(): pl.pallas_call(pre_kernel, grid=(rows,), in_specs=[big, big, mat, mat], o...  16.2 us
    pallas_call x1, Pallas kernels, finish(): pl.pallas_call(post_kernel, grid_spec=pltpu.PrefetchScalarGridSpec(num_sc...  8.12 us
    pallas_call x1, Pallas kernels, couple_inner(): pl.pallas_call(functools.partial(inner_kernel, split=split), in_specs=[SM...  6.33 us
    ppermute x1, starting transfers between devices, per_device(): left = lax.ppermute(high, 'z', [(k, k + 1) for k in range(z_n - 1)])  5.71 us
  transfers between devices with their start and end apart: 14, of which 9 were waited for; matrix products, arithmetic and copies ran while one was open for 3% of the time, Pallas kernels for 14%

profile of v7, /device:TPU:3, one launch (start us, length us, event | category | flops | bytes accessed | tf_op | source)
XLA Modules:
  0.0 174.7 jit_solution(7945961841324227269)
XLA Ops:
  0.6 2.9 %pack_flip.1 = bf16[32,8,2,8,256]{4,3,2,1,0:T(8,128)(2,1)} custom-call(bf16[8,2,256,256]{3,2,1,0:T(8,128)(2,1)} %amp_ref.5), custom_call_target="tpu_custom_call" | custom-call | tf_op jit(solution)/shard_map/pack_flip/pallas_call | solution.py:35
  3.5 7.9 %all-to-all-start = ((bf16[32,8,2,8,256]{4,3,2,1,0:T(8,128)(2,1)}), bf16[32,8,2,8,256]{4,3,2,1,0:T(8,128)(2,1)S(1)}, u32[]{:S(2)}, u32[]{:S(2)}) async-start(bf16[32,8,2,8,256]{4,3,2,1,0:T(8,128)(2,1)} %pack_flip.1), calls=%async_computation | async-start | bytes 4194304 | tf_op jit(solution)/shard_map/all_to_all | solution.py:345
  11.5 2.7 %pack.1 = bf16[32,8,2,8,256]{4,3,2,1,0:T(8,128)(2,1)} custom-call(bf16[8,2,256,256]{3,2,1,0:T(8,128)(2,1)} %amp_ref.5), custom_call_target="tpu_custom_call" | custom-call | tf_op jit(solution)/shard_map/pack/pallas_call | solution.py:35
  14.2 24.4 %all-to-all-done = bf16[32,8,2,8,256]{4,3,2,1,0:T(8,128)(2,1)S(1)} async-done(((bf16[32,8,2,8,256]{4,3,2,1,0:T(8,128)(2,1)}), bf16[32,8,2,8,256]{4,3,2,1,0:T(8,128)(2,1)S(1)}, u32[]{:S(2)}, u32[]{:S(2)}) %all-to-all-start) | async-done | bytes 2097184 | tf_op jit(solution)/shard_map/all_to_all | solution.py:345
  38.6 0.0 copy-start
  38.6 1.3 dynamic-slice_bitcast_fusion
  39.8 0.6 copy-done
  40.5 7.3 %all-to-all-start.1 = ((bf16[32,8,2,8,256]{4,3,2,1,0:T(8,128)(2,1)}), bf16[32,8,2,8,256]{4,3,2,1,0:T(8,128)(2,1)S(1)}, u32[]{:S(2)}, u32[]{:S(2)}) async-start(bf16[32,8,2,8,256]{4,3,2,1,0:T(8,128)(2,1)} %pack.1), calls=%async_computation.1 | async-start | bytes 4194304 | tf_op jit(solution)/shard_map/all_to_all | solution.py:345
  47.8 1.7 collective-permute-start
  49.5 1.0 dynamic-slice_bitcast_fusion.7
  50.5 5.6 %collective-permute-start.4 = (bf16[2,8,2,8,256]{4,3,2,1,0:T(8,128)(2,1)S(1)}, bf16[2,8,2,8,256]{4,3,2,1,0:T(8,128)(2,1)S(1)}, u32[]{:S(2)}, u32[]{:S(2)}) collective-permute-start(bf16[2,8,2,8,256]{4,3,2,1,0:T(8,128)(2,1)S(1)} %get-tuple-element.23), channel_id=1, source_target_pairs={{0,20},{4,24},{8,28},{12,0},{16,4},{20,8},{24,12},{28,16},{1,21},{... | collective-permute-start | bytes 393224 | tf_op jit(solution)/shard_map/ppermute | solution.py:348
  56.2 0.5 collective-permute-start.3
  56.7 3.9 %collective-permute-start.1 = (bf16[4,8,2,8,256]{4,3,2,1,0:T(8,128)(2,1)}, bf16[4,8,2,8,256]{4,3,2,1,0:T(8,128)(2,1)S(1)}, u32[]{:S(2)}, u32[]{:S(2)}) collective-permute-start(bf16[4,8,2,8,256]{4,3,2,1,0:T(8,128)(2,1)} %get-tuple-element.20), channel_id=1, source_target_pairs={{0,8},{4,12},{8,16},{12,20},{16,24},{20,28},{24,0},{28,4},{1,9},{5... | collective-permute-start | bytes 786440 | tf_op jit(solution)/shard_map/ppermute | solution.py:348
  60.6 1.6 collective-permute-start.2
  62.3 2.7 %collective-permute-done.4 = bf16[2,8,2,8,256]{4,3,2,1,0:T(8,128)(2,1)S(1)} collective-permute-done((bf16[2,8,2,8,256]{4,3,2,1,0:T(8,128)(2,1)S(1)}, bf16[2,8,2,8,256]{4,3,2,1,0:T(8,128)(2,1)S(1)}, u32[]{:S(2)}, u32[]{:S(2)}) %collective-permute-start.4) | collective-permute-done | bytes 131104 | tf_op jit(solution)/shard_map/ppermute | solution.py:348
  65.0 4.4 %collective-permute-start.6 = (bf16[4,8,2,8,256]{4,3,2,1,0:T(8,128)(2,1)}, bf16[4,8,2,8,256]{4,3,2,1,0:T(8,128)(2,1)S(1)}, u32[]{:S(2)}, u32[]{:S(2)}) collective-permute-start(bf16[4,8,2,8,256]{4,3,2,1,0:T(8,128)(2,1)} %get-tuple-element.18), channel_id=1, source_target_pairs={{0,20},{4,24},{8,28},{12,0},{16,4},{20,8},{24,12},{28,16},{1,21},{... | collective-permute-start | bytes 786440 | tf_op jit(solution)/shard_map/ppermute | solution.py:348
  69.4 0.0 collective-permute-done.3.refs_4_
  69.4 5.9 %collective-permute-start.7 = (bf16[4,8,2,8,256]{4,3,2,1,0:T(8,128)(2,1)}, bf16[4,8,2,8,256]{4,3,2,1,0:T(8,128)(2,1)S(1)}, u32[]{:S(2)}, u32[]{:S(2)}) collective-permute-start(bf16[4,8,2,8,256]{4,3,2,1,0:T(8,128)(2,1)} %get-tuple-element.17), channel_id=1, source_target_pairs={{0,24},{4,28},{8,0},{12,4},{16,8},{20,12},{24,16},{28,20},{1,25},{... | collective-permute-start | bytes 786440 | tf_op jit(solution)/shard_map/ppermute | solution.py:348
  75.3 0.0 collective-permute-done.refs_1_
  75.3 0.0 copy-start.1
  75.3 0.0 collective-permute-start.8
  75.3 0.0 collective-permute-done.1.refs_2_
  75.3 0.0 copy-start.2
  75.3 5.6 %collective-permute-start.5 = (bf16[2,8,2,8,256]{4,3,2,1,0:T(8,128)(2,1)S(1)}, bf16[2,8,2,8,256]{4,3,2,1,0:T(8,128)(2,1)}, u32[]{:S(2)}, u32[]{:S(2)}) collective-permute-start(bf16[2,8,2,8,256]{4,3,2,1,0:T(8,128)(2,1)S(1)} %collective-permute-done.4), channel_id=1, source_target_pairs={{0,28},{4,0},{8,4},{12,8},{16,12},{20,16},{24,20},{28,24},{1,29},{... | collective-permute-start | bytes 393224 | tf_op jit(solution)/shard_map/ppermute | solution.py:348
  80.9 13.9 %collective-permute-done.2.refs_3_ = bf16[4,8,2,8,256]{4,3,2,1,0:T(8,128)(2,1)S(1)} collective-permute-done((bf16[4,8,2,8,256]{4,3,2,1,0:T(8,128)(2,1)}, bf16[4,8,2,8,256]{4,3,2,1,0:T(8,128)(2,1)S(1)}, u32[]{:S(2)}, u32[]{:S(2)}) %collective-permute-start.2) | collective-permute-done | bytes 262176 | tf_op jit(solution)/shard_map/ppermute | solution.py:348
  94.8 0.0 copy-start.3
  94.8 0.0 collective-permute-done.6.refs_6_
  94.9 0.0 copy-start.4
  94.9 6.7 %collective-permute-done.7.refs_7_ = bf16[4,8,2,8,256]{4,3,2,1,0:T(8,128)(2,1)S(1)} collective-permute-done((bf16[4,8,2,8,256]{4,3,2,1,0:T(8,128)(2,1)}, bf16[4,8,2,8,256]{4,3,2,1,0:T(8,128)(2,1)S(1)}, u32[]{:S(2)}, u32[]{:S(2)}) %collective-permute-start.7) | collective-permute-done | bytes 262176 | tf_op jit(solution)/shard_map/ppermute | solution.py:348
  101.6 3.0 %collective-permute-done.8.refs_8_ = bf16[4,8,2,8,256]{4,3,2,1,0:T(8,128)(2,1)S(1)} collective-permute-done((bf16[4,8,2,8,256]{4,3,2,1,0:T(8,128)(2,1)}, bf16[4,8,2,8,256]{4,3,2,1,0:T(8,128)(2,1)S(1)}, u32[]{:S(2)}, u32[]{:S(2)}) %collective-permute-start.8) | collective-permute-done | bytes 262176 | tf_op jit(solution)/shard_map/ppermute | solution.py:348
  104.5 0.7 copy-done.6
  105.2 2.0 %collective-permute-done.5.refs_5_ = bf16[2,8,2,8,256]{4,3,2,1,0:T(8,128)(2,1)} collective-permute-done((bf16[2,8,2,8,256]{4,3,2,1,0:T(8,128)(2,1)S(1)}, bf16[2,8,2,8,256]{4,3,2,1,0:T(8,128)(2,1)}, u32[]{:S(2)}, u32[]{:S(2)}) %collective-permute-start.5) | collective-permute-done | bytes 131104 | tf_op jit(solution)/shard_map/ppermute | solution.py:348
  107.2 0.0 all-to-all-done.1
  107.2 0.0 copy-done.8
  107.2 0.0 copy-done.1
  107.2 0.0 copy-done.2
  107.2 0.0 copy-done.3
  107.3 0.0 copy-done.4
  107.3 0.0 copy-done.5
  107.3 2.8 %halo.1 = (bf16[2,64,8,256]{3,2,1,0:T(8,128)(2,1)}, bf16[2,64,8,256]{3,2,1,0:T(8,128)(2,1)}) custom-call(s32[1]{0:T(128)} %bitcast.8.z_ref, bf16[8,4,8,2,8,256]{5,4,3,2,1,0:T(8,128)(2,1)S(1)} %bitcast.32, bf16[4,8,2,8,256]{4,3,2,1,0:T(8,128)(2,1)} %get-tuple-element.22.refs_0_, bf16[4,8,2,8,256]{4,3,2,1,0:T(8,128)(2,1)} %copy-done.1, ...), custom_call_target="tpu_custom_call" | custom-call | tf_op jit(solution)/shard_map/halo/pallas_call | solution.py:148
  110.0 1.3 collective-permute-start.10
  111.3 5.7 %collective-permute-start.9 = (bf16[2,64,8,256]{3,2,1,0:T(8,128)(2,1)}, bf16[2,64,8,256]{3,2,1,0:T(8,128)(2,1)S(1)}, u32[]{:S(2)}, u32[]{:S(2)}) collective-permute-start(bf16[2,64,8,256]{3,2,1,0:T(8,128)(2,1)} %get-tuple-element.10.hi_ref), channel_id=1, source_target_pairs={{0,4},{4,8},{8,12},{12,16},{16,20},{20,24},{24,28},{1,5},{5,9},{9,... | collective-permute-start | bytes 1572872 | tf_op jit(solution)/shard_map/ppermute | solution.py:372
  117.0 6.3 %inner.1 = (bf16[12,64,8,256]{3,2,1,0:T(8,128)(2,1)S(1)}, bf16[8,2,8,2,8,256]{5,4,3,2,1,0:T(8,128)(2,1)S(1)}, bf16[8,4,8,2,8,256]{5,4,3,2,1,0:T(8,128)(2,1)}) custom-call(s32[1]{0:T(128)} %bitcast.8.z_ref, s32[2,64]{1,0:T(2,128)} %bitcast.40, f32[2,64]{1,0:T(2,128)} %bitcast.42, s32[1]{0:T(128)} %bitcast.7.start_ref, ...), custom_call_target="tpu_custom_call" | custom-call | tf_op jit(solution)/shard_map/inner/pallas_call | solution.py:161
  123.4 3.0 %collective-permute-done.10.right_ref = bf16[2,64,8,256]{3,2,1,0:T(8,128)(2,1)S(1)} collective-permute-done((bf16[2,64,8,256]{3,2,1,0:T(8,128)(2,1)}, bf16[2,64,8,256]{3,2,1,0:T(8,128)(2,1)S(1)}, u32[]{:S(2)}, u32[]{:S(2)}) %collective-permute-start.10) | collective-permute-done | bytes 524320 | tf_op jit(solution)/shard_map/ppermute | solution.py:373
  126.4 1.0 collective-permute-done.9.left_ref
  127.4 2.9 %edge.1 = (bf16[12,64,8,256]{3,2,1,0:T(8,128)(2,1)S(1)}, bf16[8,4,8,2,8,256]{5,4,3,2,1,0:T(8,128)(2,1)}) custom-call(s32[2,64]{1,0:T(2,128)} %bitcast.41, f32[2,64]{1,0:T(2,128)} %bitcast.43, s32[1]{0:T(128)} %bitcast.7.start_ref, bf16[2,64,8,256]{3,2,1,0:T(8,128)(2,1)S(1)} %collective-permute-done.9.left_ref, ...), custom_call_target="tpu_custom_call", output_to_operand_aliasing={{0}: (6, {}), {1}: (7, {})} | custom-call | tf_op jit(solution)/shard_map/edge/pallas_call | solution.py:182
  130.3 9.2 %all-to-all-start.2 = ((bf16[32,8,2,8,256]{4,3,2,1,0:T(8,128)(2,1)}), bf16[32,8,2,8,256]{4,3,2,1,0:T(8,128)(2,1)S(1)}, u32[]{:S(2)}, u32[]{:S(2)}) async-start(bf16[32,8,2,8,256]{4,3,2,1,0:T(8,128)(2,1)} %bitcast.36), calls=%async_computation.2 | async-start | bytes 4194304 | tf_op jit(solution)/shard_map/all_to_all | solution.py:345
  139.5 0.0 copy-done.11
  139.5 0.1 dynamic_slice.38
  139.6 0.1 dynamic_slice.37
  139.6 0.0 copy-done.10
  139.7 0.1 dynamic-slice_bitcast_fusion.9
  139.8 0.7 copy.20.mask_j_ref
  140.4 0.1 dynamic-slice_bitcast_fusion.10
  140.5 0.7 copy.19.mask_i_ref
  141.2 0.0 copy-done.9
  141.2 0.7 add_convert_fusion.right_ref.left_ref.over_ref
  141.9 7.9 %term.2.x_ref = f32[8,2,256,256]{3,2,1,0:T(8,128)} custom-call(bf16[8,2,256,256]{3,2,1,0:T(8,128)(2,1)} %x_ref.3, bf16[8,2,256,256]{3,2,1,0:T(8,128)(2,1)} %amp_ref.5, bf16[256,256]{1,0:T(8,128)(2,1)} %right_ref.1, bf16[256,256]{1,0:T(8,128)(2,1)} %add_convert_fusion.right_ref.left_ref.over_ref), custom_call_target="tpu_custom_call" | custom-call | tf_op jit(solution)/shard_map/term/pallas_call | solution.py:213
  149.8 8.3 %term.3.base_ref = f32[8,2,256,256]{3,2,1,0:T(8,128)} custom-call(f32[8,2,256,256]{3,2,1,0:T(8,128)} %term.2.x_ref, bf16[8,2,256,256]{3,2,1,0:T(8,128)(2,1)} %amp_ref.5, bf16[256,256]{1,0:T(8,128)(2,1)} %add_convert_fusion.right_ref.left_ref.over_ref, bf16[256,256]{1,0:T(8,128)(2,1)} %right_ref.1), custom_call_target="tpu_custom_call" | custom-call | tf_op jit(solution)/shard_map/term/pallas_call | solution.py:213
  158.1 0.0 copy-done.7
  158.1 0.8 copy.18
  158.9 0.7 pad_maximum_fusion.occ_ref
  159.6 7.0 %all-to-all-done.2.coup_ref = bf16[32,8,2,8,256]{4,3,2,1,0:T(8,128)(2,1)S(1)} async-done(((bf16[32,8,2,8,256]{4,3,2,1,0:T(8,128)(2,1)}), bf16[32,8,2,8,256]{4,3,2,1,0:T(8,128)(2,1)S(1)}, u32[]{:S(2)}, u32[]{:S(2)}) %all-to-all-start.2) | async-done | bytes 2097184 | tf_op jit(solution)/shard_map/all_to_all | solution.py:345
  166.6 8.1 %finish.1 = (f32[8,2,256,256]{3,2,1,0:T(8,128)}, bf16[8,2,256,256]{3,2,1,0:T(8,128)(2,1)}) custom-call(f32[10]{0:T(128)} %pad_maximum_fusion.occ_ref, f32[8,2,256,256]{3,2,1,0:T(8,128)} %term.3.base_ref, bf16[8,2,256,256]{3,2,1,0:T(8,128)(2,1)} %amp_ref.5, f32[8,1,256]{2,1,0:T(1,128)} %copy.19.mask_i_ref, f32[2,1,256]{2,1,0:T(1,128)} %copy.20.mask_j_ref, ...), custom_call_target="tpu_custom_call" | custom-call | tf_op jit(solution)/shard_map/finish/pallas_call | solution.py:278
  (9 shorter events, 0.0 us)
Async XLA Ops:
  3.5 35.0 %all-to-all-start = ((bf16[32,8,2,8,256]{4,3,2,1,0:T(8,128)(2,1)}), bf16[32,8,2,8,256]{4,3,2,1,0:T(8,128)(2,1)S(1)}, u32[]{:S(2)}, u32[]{:S(2)}) async-start(bf16[32,8,2,8,256]{4,3,2,1,0:T(8,128)(2,1)} %pack_flip.1), calls=%async_computation | async-start | bytes 4194304 | tf_op jit(solution)/shard_map/all_to_all | solution.py:345
  38.6 1.9 %copy-start = (bf16[32,8,2,8,256]{4,3,2,1,0:T(8,128)(2,1)}, bf16[32,8,2,8,256]{4,3,2,1,0:T(8,128)(2,1)S(1)}, u32[]{:S(2)}) copy-start(bf16[32,8,2,8,256]{4,3,2,1,0:T(8,128)(2,1)S(1)} %all-to-all-done) | copy-start | bytes 6291460
  40.5 66.8 %all-to-all-start.1 = ((bf16[32,8,2,8,256]{4,3,2,1,0:T(8,128)(2,1)}), bf16[32,8,2,8,256]{4,3,2,1,0:T(8,128)(2,1)S(1)}, u32[]{:S(2)}, u32[]{:S(2)}) async-start(bf16[32,8,2,8,256]{4,3,2,1,0:T(8,128)(2,1)} %pack.1), calls=%async_computation.1 | async-start | bytes 4194304 | tf_op jit(solution)/shard_map/all_to_all | solution.py:345
  47.8 27.5 %collective-permute-start = (bf16[4,8,2,8,256]{4,3,2,1,0:T(8,128)(2,1)}, bf16[4,8,2,8,256]{4,3,2,1,0:T(8,128)(2,1)S(1)}, u32[]{:S(2)}, u32[]{:S(2)}) collective-permute-start(bf16[4,8,2,8,256]{4,3,2,1,0:T(8,128)(2,1)} %get-tuple-element.21), channel_id=1, source_target_pairs={{0,4},{4,8},{8,12},{12,16},{16,20},{20,24},{24,28},{28,0},{1,5},{5... | collective-permute-start | bytes 786440 | tf_op jit(solution)/shard_map/ppermute | solution.py:348
  50.5 14.4 %collective-permute-start.4 = (bf16[2,8,2,8,256]{4,3,2,1,0:T(8,128)(2,1)S(1)}, bf16[2,8,2,8,256]{4,3,2,1,0:T(8,128)(2,1)S(1)}, u32[]{:S(2)}, u32[]{:S(2)}) collective-permute-start(bf16[2,8,2,8,256]{4,3,2,1,0:T(8,128)(2,1)S(1)} %get-tuple-element.23), channel_id=1, source_target_pairs={{0,20},{4,24},{8,28},{12,0},{16,4},{20,8},{24,12},{28,16},{1,21},{... | collective-permute-start | bytes 393224 | tf_op jit(solution)/shard_map/ppermute | solution.py:348
  56.2 13.2 %collective-permute-start.3 = (bf16[2,8,2,8,256]{4,3,2,1,0:T(8,128)(2,1)S(1)}, bf16[2,8,2,8,256]{4,3,2,1,0:T(8,128)(2,1)S(1)}, u32[]{:S(2)}, u32[]{:S(2)}) collective-permute-start(bf16[2,8,2,8,256]{4,3,2,1,0:T(8,128)(2,1)S(1)} %get-tuple-element.24), channel_id=1, source_target_pairs={{0,16},{4,20},{8,24},{12,28},{16,0},{20,4},{24,8},{28,12},{1,17},{... | collective-permute-start | bytes 393224 | tf_op jit(solution)/shard_map/ppermute | solution.py:348
  56.7 18.6 %collective-permute-start.1 = (bf16[4,8,2,8,256]{4,3,2,1,0:T(8,128)(2,1)}, bf16[4,8,2,8,256]{4,3,2,1,0:T(8,128)(2,1)S(1)}, u32[]{:S(2)}, u32[]{:S(2)}) collective-permute-start(bf16[4,8,2,8,256]{4,3,2,1,0:T(8,128)(2,1)} %get-tuple-element.20), channel_id=1, source_target_pairs={{0,8},{4,12},{8,16},{12,20},{16,24},{20,28},{24,0},{28,4},{1,9},{5... | collective-permute-start | bytes 786440 | tf_op jit(solution)/shard_map/ppermute | solution.py:348
  60.6 34.2 %collective-permute-start.2 = (bf16[4,8,2,8,256]{4,3,2,1,0:T(8,128)(2,1)}, bf16[4,8,2,8,256]{4,3,2,1,0:T(8,128)(2,1)S(1)}, u32[]{:S(2)}, u32[]{:S(2)}) collective-permute-start(bf16[4,8,2,8,256]{4,3,2,1,0:T(8,128)(2,1)} %get-tuple-element.19), channel_id=1, source_target_pairs={{0,12},{4,16},{8,20},{12,24},{16,28},{20,0},{24,4},{28,8},{1,13},{... | collective-permute-start | bytes 786440 | tf_op jit(solution)/shard_map/ppermute | solution.py:348
  65.0 29.9 %collective-permute-start.6 = (bf16[4,8,2,8,256]{4,3,2,1,0:T(8,128)(2,1)}, bf16[4,8,2,8,256]{4,3,2,1,0:T(8,128)(2,1)S(1)}, u32[]{:S(2)}, u32[]{:S(2)}) collective-permute-start(bf16[4,8,2,8,256]{4,3,2,1,0:T(8,128)(2,1)} %get-tuple-element.18), channel_id=1, source_target_pairs={{0,20},{4,24},{8,28},{12,0},{16,4},{20,8},{24,12},{28,16},{1,21},{... | collective-permute-start | bytes 786440 | tf_op jit(solution)/shard_map/ppermute | solution.py:348
  69.4 37.8 %copy-start.8 = (bf16[2,8,2,8,256]{4,3,2,1,0:T(8,128)(2,1)}, bf16[2,8,2,8,256]{4,3,2,1,0:T(8,128)(2,1)S(1)}, u32[]{:S(2)}) copy-start(bf16[2,8,2,8,256]{4,3,2,1,0:T(8,128)(2,1)S(1)} %collective-permute-done.3.refs_4_) | copy-start | bytes 393220
  69.4 32.1 %collective-permute-start.7 = (bf16[4,8,2,8,256]{4,3,2,1,0:T(8,128)(2,1)}, bf16[4,8,2,8,256]{4,3,2,1,0:T(8,128)(2,1)S(1)}, u32[]{:S(2)}, u32[]{:S(2)}) collective-permute-start(bf16[4,8,2,8,256]{4,3,2,1,0:T(8,128)(2,1)} %get-tuple-element.17), channel_id=1, source_target_pairs={{0,24},{4,28},{8,0},{12,4},{16,8},{20,12},{24,16},{28,20},{1,25},{... | collective-permute-start | bytes 786440 | tf_op jit(solution)/shard_map/ppermute | solution.py:348
  75.3 32.0 %copy-start.1 = (bf16[4,8,2,8,256]{4,3,2,1,0:T(8,128)(2,1)}, bf16[4,8,2,8,256]{4,3,2,1,0:T(8,128)(2,1)S(1)}, u32[]{:S(2)}) copy-start(bf16[4,8,2,8,256]{4,3,2,1,0:T(8,128)(2,1)S(1)} %collective-permute-done.refs_1_) | copy-start | bytes 786436
  75.3 29.2 %collective-permute-start.8 = (bf16[4,8,2,8,256]{4,3,2,1,0:T(8,128)(2,1)}, bf16[4,8,2,8,256]{4,3,2,1,0:T(8,128)(2,1)S(1)}, u32[]{:S(2)}, u32[]{:S(2)}) collective-permute-start(bf16[4,8,2,8,256]{4,3,2,1,0:T(8,128)(2,1)} %get-tuple-element.16), channel_id=1, source_target_pairs={{0,28},{4,0},{8,4},{12,8},{16,12},{20,16},{24,20},{28,24},{1,29},{... | collective-permute-start | bytes 786440 | tf_op jit(solution)/shard_map/ppermute | solution.py:348
  75.3 31.9 %copy-start.2 = (bf16[4,8,2,8,256]{4,3,2,1,0:T(8,128)(2,1)}, bf16[4,8,2,8,256]{4,3,2,1,0:T(8,128)(2,1)S(1)}, u32[]{:S(2)}) copy-start(bf16[4,8,2,8,256]{4,3,2,1,0:T(8,128)(2,1)S(1)} %collective-permute-done.1.refs_2_) | copy-start | bytes 786436
  75.3 31.9 %collective-permute-start.5 = (bf16[2,8,2,8,256]{4,3,2,1,0:T(8,128)(2,1)S(1)}, bf16[2,8,2,8,256]{4,3,2,1,0:T(8,128)(2,1)}, u32[]{:S(2)}, u32[]{:S(2)}) collective-permute-start(bf16[2,8,2,8,256]{4,3,2,1,0:T(8,128)(2,1)S(1)} %collective-permute-done.4), channel_id=1, source_target_pairs={{0,28},{4,0},{8,4},{12,8},{16,12},{20,16},{24,20},{28,24},{1,29},{... | collective-permute-start | bytes 393224 | tf_op jit(solution)/shard_map/ppermute | solution.py:348
  94.8 12.4 %copy-start.3 = (bf16[4,8,2,8,256]{4,3,2,1,0:T(8,128)(2,1)}, bf16[4,8,2,8,256]{4,3,2,1,0:T(8,128)(2,1)S(1)}, u32[]{:S(2)}) copy-start(bf16[4,8,2,8,256]{4,3,2,1,0:T(8,128)(2,1)S(1)} %collective-permute-done.2.refs_3_) | copy-start | bytes 786436
  94.9 12.4 %copy-start.4 = (bf16[4,8,2,8,256]{4,3,2,1,0:T(8,128)(2,1)}, bf16[4,8,2,8,256]{4,3,2,1,0:T(8,128)(2,1)S(1)}, u32[]{:S(2)}) copy-start(bf16[4,8,2,8,256]{4,3,2,1,0:T(8,128)(2,1)S(1)} %collective-permute-done.6.refs_6_) | copy-start | bytes 786436
  101.5 5.7 %copy-start.5 = (bf16[4,8,2,8,256]{4,3,2,1,0:T(8,128)(2,1)}, bf16[4,8,2,8,256]{4,3,2,1,0:T(8,128)(2,1)S(1)}, u32[]{:S(2)}) copy-start(bf16[4,8,2,8,256]{4,3,2,1,0:T(8,128)(2,1)S(1)} %collective-permute-done.7.refs_7_) | copy-start | bytes 786436
  104.5 0.7 copy-start.6
  110.0 16.3 %collective-permute-start.10 = (bf16[2,64,8,256]{3,2,1,0:T(8,128)(2,1)}, bf16[2,64,8,256]{3,2,1,0:T(8,128)(2,1)S(1)}, u32[]{:S(2)}, u32[]{:S(2)}) collective-permute-start(bf16[2,64,8,256]{3,2,1,0:T(8,128)(2,1)} %get-tuple-element.11.lo_ref), channel_id=1, source_target_pairs={{4,0},{8,4},{12,8},{16,12},{20,16},{24,20},{28,24},{5,1},{9,5},{13... | collective-permute-start | bytes 1572872 | tf_op jit(solution)/shard_map/ppermute | solution.py:373
  111.3 16.1 %collective-permute-start.9 = (bf16[2,64,8,256]{3,2,1,0:T(8,128)(2,1)}, bf16[2,64,8,256]{3,2,1,0:T(8,128)(2,1)S(1)}, u32[]{:S(2)}, u32[]{:S(2)}) collective-permute-start(bf16[2,64,8,256]{3,2,1,0:T(8,128)(2,1)} %get-tuple-element.10.hi_ref), channel_id=1, source_target_pairs={{0,4},{4,8},{8,12},{12,16},{16,20},{20,24},{24,28},{1,5},{5,9},{9,... | collective-permute-start | bytes 1572872 | tf_op jit(solution)/shard_map/ppermute | solution.py:372
  130.3 9.2 %copy-start.11 = (f32[64]{0:T(128)S(1)}, f32[64]{0:T(128)}, u32[]{:S(2)}) copy-start(f32[64]{0:T(128)} %param.16) | copy-start | bytes 772
  130.3 9.4 %copy-start.10 = (s32[64,8]{0,1:T(8,128)S(1)}, s32[64,8]{0,1:T(8,128)}, u32[]{:S(2)}) copy-start(s32[64,8]{0,1:T(8,128)} %param.19) | copy-start | bytes 6148
  130.3 10.9 %copy-start.9 = (bf16[256,256]{1,0:T(8,128)(2,1)S(1)}, bf16[256,256]{1,0:T(8,128)(2,1)}, u32[]{:S(2)}) copy-start(bf16[256,256]{1,0:T(8,128)(2,1)} %param.13) | copy-start | bytes 393220
  130.3 36.3 %all-to-all-start.2 = ((bf16[32,8,2,8,256]{4,3,2,1,0:T(8,128)(2,1)}), bf16[32,8,2,8,256]{4,3,2,1,0:T(8,128)(2,1)S(1)}, u32[]{:S(2)}, u32[]{:S(2)}) async-start(bf16[32,8,2,8,256]{4,3,2,1,0:T(8,128)(2,1)} %bitcast.36), calls=%async_computation.2 | async-start | bytes 4194304 | tf_op jit(solution)/shard_map/all_to_all | solution.py:345
  149.8 8.3 %copy-start.7 = (bf16[256,256]{1,0:T(8,128)(2,1)S(1)}, bf16[256,256]{1,0:T(8,128)(2,1)}, u32[]{:S(2)}) copy-start(bf16[256,256]{1,0:T(8,128)(2,1)} %trans_ref.1) | copy-start | bytes 393220
